TPU v7x, 32 devices: a whole 2x2x4 slice. The times are simulated.
32 devices in a mesh: gx: 8 (over z, x), gy: 4 (over y, core).
Axes of the slice: x: 2, y: 2, z: 4, core: 2. Of those that a mesh axis runs over, the one named last changes fastest.
Arguments:
- impedance: bfloat16 [8, 4, 1024, 1024], P('gx', 'gy'), may hold values from -0.1875 to 0.1875
- rebuild_map: bfloat16 [8, 4, 256, 1024], P('gx', 'gy'), may hold values from -0.1875 to 0.1875
- left_trace: bfloat16 [8, 4, 512, 512], P('gx', 'gy'), may hold values from -6 to 6
- lower_trace: bfloat16 [8, 4, 512, 512], P('gx', 'gy'), may hold values from -6 to 6
- cell_kind: int32 [128, 64], P('gx', 'gy'), may hold values from 0 to 15
- kind_wavenum: float32 [16], replicated, may hold values from 0.5 to 3
Outputs:
- right_trace: bfloat16 [8, 4, 512, 512], P('gx', 'gy')
- upper_trace: bfloat16 [8, 4, 512, 512], P('gx', 'gy')
- residual: float32 [128, 64, 512], P('gx', 'gy')
All inputs are finite; a program needn't handle non-finite values.
Results may differ from a plain program's by a relative error of at most 0.0064.
Values may be sent and summed in bfloat16 or wider, within the bound.
No kernel may reach another device: no remote copies, remote signals or barrier semaphores. Data moves between devices by JAX's collectives and lax.ppermute only.
A program may use at most 64 MiB of HBM per device.

v0:
```python
import jax
import jax.numpy as jnp
from jax import lax
from jax.sharding import PartitionSpec as P

STEPS = 4


def from_behind(block, axis, distance):
    devices = range(lax.axis_size(axis))
    route = [(i - distance, i) for i in devices if i - distance in devices]
    return lax.ppermute(block, axis, route)


def extended(cells, sides, width):
    for axis, dim in sides:
        count = lax.axis_size(axis)
        ends = count - 1
        head = lax.slice_in_dim(cells, 0, width, axis=dim)
        tail = lax.slice_in_dim(cells, cells.shape[dim] - width, cells.shape[dim], axis=dim)
        cells = jnp.concatenate(
            [
                lax.ppermute(tail, axis, [(i, (i + 1) % count) for i in range(ends)]),
                cells,
                lax.ppermute(head, axis, [((i + 1) % count, i) for i in range(ends)]),
            ],
            axis=dim,
        )
    return cells


def advance(mapping, left_in, lower_in):
    stacked = jnp.concatenate([left_in, lower_in], axis=0)
    outgoing = jnp.dot(mapping, stacked, preferred_element_type=jnp.float32).astype(jnp.bfloat16)
    rows = left_in.shape[0]
    return (outgoing[:rows], outgoing[rows:])


def per_device(impedance, rebuild_map, left_trace, lower_trace, cell_kind, kind_wavenum):
    mapping = impedance[0, 0]
    left_in = left_trace[0, 0]
    lower_in = lower_trace[0, 0]
    right_out, upper_out = (left_in, lower_in)
    for sweep_step in range(STEPS):
        last_turn = sweep_step + 1 == STEPS
        half_cols = left_in.shape[1] // 2
        right_parts = []
        upper_parts = []
        for which_half in range(2):
            start_col = which_half * half_cols
            right_piece, upper_piece = advance(
                mapping,
                left_in[:, start_col : start_col + half_cols],
                lower_in[:, start_col : start_col + half_cols],
            )
            if not last_turn:
                right_piece = from_behind(right_piece, "gx", 1)
                upper_piece = from_behind(upper_piece, "gy", 1)
            right_parts.append(right_piece)
            upper_parts.append(upper_piece)
        if last_turn:
            right_out = jnp.concatenate(right_parts, axis=1)
            upper_out = jnp.concatenate(upper_parts, axis=1)
        else:
            left_in = jnp.concatenate(right_parts, axis=1)
            lower_in = jnp.concatenate(upper_parts, axis=1)
    cells_x = cell_kind.shape[0]
    cells_y = cell_kind.shape[1]
    sources = left_in.shape[1]
    stacked = jnp.concatenate([left_in, lower_in], axis=0)
    volume = jnp.dot(rebuild_map[0, 0], stacked, preferred_element_type=jnp.float32).reshape(
        cells_x, cells_y, sources
    )
    padded = extended(volume.astype(jnp.bfloat16), (("gx", 0), ("gy", 1)), 1).astype(volume.dtype)
    beside = padded[2:, 1:-1] + padded[:-2, 1:-1] + padded[1:-1, 2:] + padded[1:-1, :-2]
    kind_ids = jnp.arange(kind_wavenum.shape[0], dtype=jnp.int32)
    wavenum = jnp.sum(
        jnp.where(
            cell_kind[:, :, None] == kind_ids[None, None, :],
            kind_wavenum[None, None, :],
            jnp.float32(0.0),
        ),
        axis=-1,
    )
    residual = beside - 4.0 * volume + wavenum[:, :, None] * volume
    return (right_out[None, None], upper_out[None, None], residual)


def solution(mesh):
    return jax.shard_map(
        per_device,
        mesh=mesh,
        in_specs=(
            P("gx", "gy", None, None),
            P("gx", "gy", None, None),
            P("gx", "gy", None, None),
            P("gx", "gy", None, None),
            P("gx", "gy"),
            P(),
        ),
        out_specs=(P("gx", "gy", None, None), P("gx", "gy", None, None), P("gx", "gy", None)),
        check_vma=False,
    )
```

profile of v0, /device:TPU:1, one launch (start us, length us, event | category | flops | bytes accessed | tf_op | source)
XLA Modules:
  0.0 69.1 jit_solution(11336573422832188333)
XLA Ops:
  0.6 0.0 copy-start
  0.6 1.4 %fusion.113 = (bf16[512,256]{1,0:T(8,128)(2,1)S(1)}, bf16[512,256]{1,0:T(8,128)(2,1)S(1)}, bf16[512,256]{1,0:T(8,128)(2,1)S(1)}, bf16[512,256]{1,0:T(8,128)(2,1)S(1)}) fusion(bf16[512,512]{1,0:T(8,128)(2,1)} %bitcast.79, bf16[512,512]{1,0:T(8,128)(2,1)} %bitcast.80), kind=kLoop, calls=%fused_computation.92 | loop fusion | bytes 2097152 | tf_op jit(solution)/shard_map/slice | solution.py:53
  2.1 0.5 copy-done
  2.5 0.8 %fusion.61 = bf16[1024,256]{0,1:T(8,128)(2,1)S(1)} fusion(bf16[1,1,1024,1024]{3,2,1,0:T(8,128)(2,1)S(1)} %copy-done, bf16[512,256]{1,0:T(8,128)(2,1)S(1)} %get-tuple-element.34, bf16[512,256]{1,0:T(8,128)(2,1)S(1)} %get-tuple-element.19), kind=kOutput, calls=%fused_computation.31 | convolution fusion | flops 538181632 | bytes 3145728 | tf_op jit(solution)/shard_map/dot_general | solution.py:34
  3.4 4.0 %collective-permute-start = (bf16[512,256]{0,1:T(8,128)(2,1)S(1)}, bf16[512,256]{0,1:T(8,128)(2,1)S(1)}, u32[]{:S(2)}, u32[]{:S(2)}) collective-permute-start(bf16[512,256]{0,1:T(8,128)(2,1)S(1)} %get-tuple-element.17), channel_id=1, source_target_pairs={{0,4},{4,8},{8,12},{12,16},{16,20},{20,24},{24,28},{1,5},{5,9},{9,... | collective-permute-start | bytes 786440 | tf_op jit(solution)/shard_map/ppermute | solution.py:12
  7.3 4.0 %collective-permute-start.1 = (bf16[512,256]{0,1:T(8,128)(2,1)S(1)}, bf16[512,256]{0,1:T(8,128)(2,1)S(1)}, u32[]{:S(2)}, u32[]{:S(2)}) collective-permute-start(bf16[512,256]{0,1:T(8,128)(2,1)S(1)} %get-tuple-element.18), channel_id=1, source_target_pairs={{0,1},{1,2},{2,3},{4,5},{5,6},{6,7},{8,9},{9,10},{10,11},{12,13},{... | collective-permute-start | bytes 786440 | tf_op jit(solution)/shard_map/ppermute | solution.py:12
  11.3 0.0 copy-start.3
  11.3 0.0 copy-start.4
  11.3 0.8 %fusion.49 = bf16[1024,256]{0,1:T(8,128)(2,1)S(1)} fusion(bf16[1,1,1024,1024]{3,2,1,0:T(8,128)(2,1)S(1)} %copy-done, bf16[512,256]{1,0:T(8,128)(2,1)S(1)} %get-tuple-element.33, bf16[512,256]{1,0:T(8,128)(2,1)S(1)} %get-tuple-element.20), kind=kOutput, calls=%fused_computation.27 | convolution fusion | flops 538181632 | bytes 3145728 | tf_op jit(solution)/shard_map/dot_general | solution.py:34
  12.2 3.2 %collective-permute-start.6 = (bf16[512,256]{0,1:T(8,128)(2,1)S(1)}, bf16[512,256]{0,1:T(8,128)(2,1)S(1)}, u32[]{:S(2)}, u32[]{:S(2)}) collective-permute-start(bf16[512,256]{0,1:T(8,128)(2,1)S(1)} %get-tuple-element.27), channel_id=1, source_target_pairs={{0,4},{4,8},{8,12},{12,16},{16,20},{20,24},{24,28},{1,5},{5,9},{9,... | collective-permute-start | bytes 786440 | tf_op jit(solution)/shard_map/ppermute | solution.py:12
  15.4 2.2 %collective-permute-start.7 = (bf16[512,256]{0,1:T(8,128)(2,1)S(1)}, bf16[512,256]{0,1:T(8,128)(2,1)S(1)}, u32[]{:S(2)}, u32[]{:S(2)}) collective-permute-start(bf16[512,256]{0,1:T(8,128)(2,1)S(1)} %get-tuple-element.28), channel_id=1, source_target_pairs={{0,1},{1,2},{2,3},{4,5},{5,6},{6,7},{8,9},{9,10},{10,11},{12,13},{... | collective-permute-start | bytes 786440 | tf_op jit(solution)/shard_map/ppermute | solution.py:12
  17.6 0.0 copy-done.3
  17.6 0.0 copy-done.4
  17.6 0.8 %select_reduce_fusion = f32[16,16]{1,0:T(8,128)} fusion(f32[16]{0:T(128)S(1)} %copy-done.4, s32[16,16]{1,0:T(8,128)S(1)} %copy-done.3), kind=kLoop, calls=%fused_computation.73 | loop fusion | flops 12032 | bytes 2112 | tf_op jit(solution)/shard_map/reduce_sum | solution.py:77
  18.4 0.0 collective-permute-done
  18.4 0.0 collective-permute-done.1
  18.4 0.7 %fusion.58 = bf16[1024,256]{0,1:T(8,128)(2,1)S(1)} fusion(bf16[1,1,1024,1024]{3,2,1,0:T(8,128)(2,1)S(1)} %copy-done, bf16[512,256]{0,1:T(8,128)(2,1)S(1)} %collective-permute-done.1, bf16[512,256]{0,1:T(8,128)(2,1)S(1)} %collective-permute-done), kind=kOutput, calls=%fused_computation.30 | convolution fusion | flops 538181632 | bytes 3145728 | tf_op jit(solution)/shard_map/dot_general | solution.py:34
  19.2 3.1 %collective-permute-start.2 = (bf16[512,256]{0,1:T(8,128)(2,1)S(1)}, bf16[512,256]{0,1:T(8,128)(2,1)S(1)}, u32[]{:S(2)}, u32[]{:S(2)}) collective-permute-start(bf16[512,256]{0,1:T(8,128)(2,1)S(1)} %get-tuple-element.15), channel_id=1, source_target_pairs={{0,4},{4,8},{8,12},{12,16},{16,20},{20,24},{24,28},{1,5},{5,9},{9,... | collective-permute-start | bytes 786440 | tf_op jit(solution)/shard_map/ppermute | solution.py:12
  22.3 2.2 %collective-permute-start.3 = (bf16[512,256]{0,1:T(8,128)(2,1)S(1)}, bf16[512,256]{0,1:T(8,128)(2,1)S(1)}, u32[]{:S(2)}, u32[]{:S(2)}) collective-permute-start(bf16[512,256]{0,1:T(8,128)(2,1)S(1)} %get-tuple-element.16), channel_id=1, source_target_pairs={{0,1},{1,2},{2,3},{4,5},{5,6},{6,7},{8,9},{9,10},{10,11},{12,13},{... | collective-permute-start | bytes 786440 | tf_op jit(solution)/shard_map/ppermute | solution.py:12
  24.5 0.0 collective-permute-done.6
  24.5 0.0 collective-permute-done.7
  24.5 0.7 %fusion.46 = bf16[1024,256]{0,1:T(8,128)(2,1)S(1)} fusion(bf16[1,1,1024,1024]{3,2,1,0:T(8,128)(2,1)S(1)} %copy-done, bf16[512,256]{0,1:T(8,128)(2,1)S(1)} %collective-permute-done.7, bf16[512,256]{0,1:T(8,128)(2,1)S(1)} %collective-permute-done.6), kind=kOutput, calls=%fused_computation.26 | convolution fusion | flops 538181632 | bytes 3145728 | tf_op jit(solution)/shard_map/dot_general | solution.py:34
  25.3 3.2 %collective-permute-start.8 = (bf16[512,256]{0,1:T(8,128)(2,1)S(1)}, bf16[512,256]{0,1:T(8,128)(2,1)S(1)}, u32[]{:S(2)}, u32[]{:S(2)}) collective-permute-start(bf16[512,256]{0,1:T(8,128)(2,1)S(1)} %get-tuple-element.25), channel_id=1, source_target_pairs={{0,4},{4,8},{8,12},{12,16},{16,20},{20,24},{24,28},{1,5},{5,9},{9,... | collective-permute-start | bytes 786440 | tf_op jit(solution)/shard_map/ppermute | solution.py:12
  28.5 2.2 %collective-permute-start.9 = (bf16[512,256]{0,1:T(8,128)(2,1)S(1)}, bf16[512,256]{0,1:T(8,128)(2,1)S(1)}, u32[]{:S(2)}, u32[]{:S(2)}) collective-permute-start(bf16[512,256]{0,1:T(8,128)(2,1)S(1)} %get-tuple-element.26), channel_id=1, source_target_pairs={{0,1},{1,2},{2,3},{4,5},{5,6},{6,7},{8,9},{9,10},{10,11},{12,13},{... | collective-permute-start | bytes 786440 | tf_op jit(solution)/shard_map/ppermute | solution.py:12
  30.7 0.0 collective-permute-done.2
  30.7 0.0 collective-permute-done.3
  30.7 0.8 %fusion.55 = bf16[1024,256]{0,1:T(8,128)(2,1)S(1)} fusion(bf16[1,1,1024,1024]{3,2,1,0:T(8,128)(2,1)S(1)} %copy-done, bf16[512,256]{0,1:T(8,128)(2,1)S(1)} %collective-permute-done.3, bf16[512,256]{0,1:T(8,128)(2,1)S(1)} %collective-permute-done.2), kind=kOutput, calls=%fused_computation.29 | convolution fusion | flops 538181632 | bytes 3145728 | tf_op jit(solution)/shard_map/dot_general | solution.py:34
  31.5 3.1 %collective-permute-start.4 = (bf16[512,256]{0,1:T(8,128)(2,1)S(1)}, bf16[512,256]{0,1:T(8,128)(2,1)S(1)}, u32[]{:S(2)}, u32[]{:S(2)}) collective-permute-start(bf16[512,256]{0,1:T(8,128)(2,1)S(1)} %get-tuple-element.13), channel_id=1, source_target_pairs={{0,4},{4,8},{8,12},{12,16},{16,20},{20,24},{24,28},{1,5},{5,9},{9,... | collective-permute-start | bytes 786440 | tf_op jit(solution)/shard_map/ppermute | solution.py:12
  34.7 2.2 %collective-permute-start.5 = (bf16[512,256]{0,1:T(8,128)(2,1)S(1)}, bf16[512,256]{0,1:T(8,128)(2,1)S(1)}, u32[]{:S(2)}, u32[]{:S(2)}) collective-permute-start(bf16[512,256]{0,1:T(8,128)(2,1)S(1)} %get-tuple-element.14), channel_id=1, source_target_pairs={{0,1},{1,2},{2,3},{4,5},{5,6},{6,7},{8,9},{9,10},{10,11},{12,13},{... | collective-permute-start | bytes 786440 | tf_op jit(solution)/shard_map/ppermute | solution.py:12
  36.9 0.0 collective-permute-done.8
  36.9 0.0 collective-permute-done.9
  36.9 0.8 %fusion.43 = bf16[1024,256]{0,1:T(8,128)(2,1)S(1)} fusion(bf16[1,1,1024,1024]{3,2,1,0:T(8,128)(2,1)S(1)} %copy-done, bf16[512,256]{0,1:T(8,128)(2,1)S(1)} %collective-permute-done.9, bf16[512,256]{0,1:T(8,128)(2,1)S(1)} %collective-permute-done.8), kind=kOutput, calls=%fused_computation.25 | convolution fusion | flops 538181632 | bytes 3145728 | tf_op jit(solution)/shard_map/dot_general | solution.py:34
  37.8 3.2 %collective-permute-start.10 = (bf16[512,256]{0,1:T(8,128)(2,1)S(1)}, bf16[512,256]{0,1:T(8,128)(2,1)S(1)}, u32[]{:S(2)}, u32[]{:S(2)}) collective-permute-start(bf16[512,256]{0,1:T(8,128)(2,1)S(1)} %get-tuple-element.23), channel_id=1, source_target_pairs={{0,4},{4,8},{8,12},{12,16},{16,20},{20,24},{24,28},{1,5},{5,9},{9,... | collective-permute-start | bytes 786440 | tf_op jit(solution)/shard_map/ppermute | solution.py:12
  40.9 2.2 %collective-permute-start.11 = (bf16[512,256]{0,1:T(8,128)(2,1)S(1)}, bf16[512,256]{0,1:T(8,128)(2,1)S(1)}, u32[]{:S(2)}, u32[]{:S(2)}) collective-permute-start(bf16[512,256]{0,1:T(8,128)(2,1)S(1)} %get-tuple-element.24), channel_id=1, source_target_pairs={{0,1},{1,2},{2,3},{4,5},{5,6},{6,7},{8,9},{9,10},{10,11},{12,13},{... | collective-permute-start | bytes 786440 | tf_op jit(solution)/shard_map/ppermute | solution.py:12
  43.1 0.0 collective-permute-done.4
  43.1 0.0 collective-permute-done.5
  43.1 0.8 %fusion.52 = bf16[1024,256]{0,1:T(8,128)(2,1)S(1)} fusion(bf16[1,1,1024,1024]{3,2,1,0:T(8,128)(2,1)S(1)} %copy-done, bf16[512,256]{0,1:T(8,128)(2,1)S(1)} %collective-permute-done.5, bf16[512,256]{0,1:T(8,128)(2,1)S(1)} %collective-permute-done.4), kind=kOutput, calls=%fused_computation.28 | convolution fusion | flops 538181632 | bytes 3145728 | tf_op jit(solution)/shard_map/dot_general | solution.py:34
  44.0 0.0 copy-start.5
  44.0 2.3 %collective-permute-done.10 = bf16[512,256]{0,1:T(8,128)(2,1)S(1)} collective-permute-done((bf16[512,256]{0,1:T(8,128)(2,1)S(1)}, bf16[512,256]{0,1:T(8,128)(2,1)S(1)}, u32[]{:S(2)}, u32[]{:S(2)}) %collective-permute-start.10) | collective-permute-done | bytes 262176 | tf_op jit(solution)/shard_map/ppermute | solution.py:12
  46.3 0.1 collective-permute-done.11
  46.4 0.8 %fusion.40 = bf16[1024,256]{0,1:T(8,128)(2,1)S(1)} fusion(bf16[1,1,1024,1024]{3,2,1,0:T(8,128)(2,1)S(1)} %copy-done, bf16[512,256]{0,1:T(8,128)(2,1)S(1)} %collective-permute-done.11, bf16[512,256]{0,1:T(8,128)(2,1)S(1)} %collective-permute-done.10), kind=kOutput, calls=%fused_computation.24 | convolution fusion | flops 538181632 | bytes 3145728 | tf_op jit(solution)/shard_map/dot_general | solution.py:34
  47.3 0.0 copy-done.5
  47.3 0.5 fusion.64
  47.7 0.0 copy-start.1
  47.8 4.0 %collective-permute-start.12 = (bf16[1,16,512]{2,1,0:T(8,128)(2,1)S(1)}, bf16[1,16,512]{2,1,0:T(8,128)(2,1)S(1)}, u32[]{:S(2)}, u32[]{:S(2)}) collective-permute-start(bf16[1,16,512]{2,1,0:T(8,128)(2,1)S(1)} %get-tuple-element.31), channel_id=1, source_target_pairs={{0,4},{4,8},{8,12},{12,16},{16,20},{20,24},{24,28},{1,5},{5,9},{9,... | collective-permute-start | bytes 49160 | tf_op jit(solution)/shard_map/ppermute | solution.py:23
  51.8 1.3 %collective-permute-start.13 = (bf16[1,16,512]{2,1,0:T(8,128)(2,1)S(1)}, bf16[1,16,512]{2,1,0:T(8,128)(2,1)S(1)}, u32[]{:S(2)}, u32[]{:S(2)}) collective-permute-start(bf16[1,16,512]{2,1,0:T(8,128)(2,1)S(1)} %get-tuple-element.32), channel_id=1, source_target_pairs={{4,0},{8,4},{12,8},{16,12},{20,16},{24,20},{28,24},{5,1},{9,5},{13... | collective-permute-start | bytes 49160 | tf_op jit(solution)/shard_map/ppermute | solution.py:25
  53.2 0.0 collective-permute-done.12
  53.2 3.8 %collective-permute-done.13 = bf16[1,16,512]{2,1,0:T(8,128)(2,1)S(1)} collective-permute-done((bf16[1,16,512]{2,1,0:T(8,128)(2,1)S(1)}, bf16[1,16,512]{2,1,0:T(8,128)(2,1)S(1)}, u32[]{:S(2)}, u32[]{:S(2)}) %collective-permute-start.13) | collective-permute-done | bytes 16416 | tf_op jit(solution)/shard_map/ppermute | solution.py:25
  57.0 0.7 pad_maximum_fusion.2
  57.6 4.2 %collective-permute-start.14 = (bf16[18,1,512]{2,1,0:T(2,128)(2,1)}, bf16[18,1,512]{2,1,0:T(2,128)(2,1)S(1)}, u32[]{:S(2)}, u32[]{:S(2)}) collective-permute-start(bf16[18,1,512]{2,1,0:T(2,128)(2,1)} %get-tuple-element.29), channel_id=1, source_target_pairs={{0,1},{1,2},{2,3},{4,5},{5,6},{6,7},{8,9},{9,10},{10,11},{12,13},{... | collective-permute-start | bytes 55304 | tf_op jit(solution)/shard_map/ppermute | solution.py:23
  61.9 1.9 %collective-permute-start.15 = (bf16[18,1,512]{2,1,0:T(2,128)(2,1)S(1)}, bf16[18,1,512]{2,1,0:T(2,128)(2,1)S(1)}, u32[]{:S(2)}, u32[]{:S(2)}) collective-permute-start(bf16[18,1,512]{2,1,0:T(2,128)(2,1)S(1)} %get-tuple-element.30), channel_id=1, source_target_pairs={{1,0},{2,1},{3,2},{5,4},{6,5},{7,6},{9,8},{10,9},{11,10},{13,12},{... | collective-permute-start | bytes 55304 | tf_op jit(solution)/shard_map/ppermute | solution.py:25
  63.8 0.0 copy-done.1
  63.9 1.0 %copy.12 = bf16[1,1,512,512]{3,2,1,0:T(8,128)(2,1)} copy(bf16[1,1,512,512]{2,3,1,0:T(8,128)(2,1)S(1)} %maximum_bitcast_fusion.1) | data formatting | bytes 1048576
  64.9 0.0 copy-start.2
  64.9 1.0 %copy.11 = bf16[1,1,512,512]{3,2,1,0:T(8,128)(2,1)} copy(bf16[1,1,512,512]{2,3,1,0:T(8,128)(2,1)S(1)} %maximum_bitcast_fusion) | data formatting | bytes 1048576
  65.9 0.0 collective-permute-done.14
  65.9 1.3 %collective-permute-done.15 = bf16[18,1,512]{2,1,0:T(2,128)(2,1)S(1)} collective-permute-done((bf16[18,1,512]{2,1,0:T(2,128)(2,1)S(1)}, bf16[18,1,512]{2,1,0:T(2,128)(2,1)S(1)}, u32[]{:S(2)}, u32[]{:S(2)}) %collective-permute-start.15) | collective-permute-done | bytes 18464 | tf_op jit(solution)/shard_map/ppermute | solution.py:25
  67.2 0.2 maximum_convert_fusion
  67.3 0.0 copy-done.2
  67.4 1.7 %fusion.73 = f32[16,16,512]{2,1,0:T(8,128)} fusion(f32[18,18,512]{2,1,0:T(8,128)S(1)} %maximum_convert_fusion, f32[16,16,512]{2,1,0:T(8,128)S(1)} %bitcast.78, f32[16,16]{1,0:T(8,128)} %select_reduce_fusion), kind=kLoop, calls=%fused_computation.42 | loop fusion | flops 917504 | bytes 3146752 | tf_op jit(solution)/shard_map/add | solution.py:85
  (12 shorter events, 0.4 us)
Async XLA Ops:
  0.6 1.9 %copy-start = (bf16[1,1,1024,1024]{3,2,1,0:T(8,128)(2,1)S(1)}, bf16[1,1,1024,1024]{3,2,1,0:T(8,128)(2,1)}, u32[]{:S(2)}) copy-start(bf16[1,1,1024,1024]{3,2,1,0:T(8,128)(2,1)} %param.6) | copy-start | bytes 6291460
  3.4 15.0 %collective-permute-start = (bf16[512,256]{0,1:T(8,128)(2,1)S(1)}, bf16[512,256]{0,1:T(8,128)(2,1)S(1)}, u32[]{:S(2)}, u32[]{:S(2)}) collective-permute-start(bf16[512,256]{0,1:T(8,128)(2,1)S(1)} %get-tuple-element.17), channel_id=1, source_target_pairs={{0,4},{4,8},{8,12},{12,16},{16,20},{20,24},{24,28},{1,5},{5,9},{9,... | collective-permute-start | bytes 786440 | tf_op jit(solution)/shard_map/ppermute | solution.py:12
  7.3 11.1 %collective-permute-start.1 = (bf16[512,256]{0,1:T(8,128)(2,1)S(1)}, bf16[512,256]{0,1:T(8,128)(2,1)S(1)}, u32[]{:S(2)}, u32[]{:S(2)}) collective-permute-start(bf16[512,256]{0,1:T(8,128)(2,1)S(1)} %get-tuple-element.18), channel_id=1, source_target_pairs={{0,1},{1,2},{2,3},{4,5},{5,6},{6,7},{8,9},{9,10},{10,11},{12,13},{... | collective-permute-start | bytes 786440 | tf_op jit(solution)/shard_map/ppermute | solution.py:12
  11.3 6.2 %copy-start.3 = (s32[16,16]{1,0:T(8,128)S(1)}, s32[16,16]{1,0:T(8,128)}, u32[]{:S(2)}) copy-start(s32[16,16]{1,0:T(8,128)} %param.10) | copy-start | bytes 3076
  11.3 6.2 %copy-start.4 = (f32[16]{0:T(128)S(1)}, f32[16]{0:T(128)}, u32[]{:S(2)}) copy-start(f32[16]{0:T(128)} %param.11) | copy-start | bytes 196
  12.2 12.3 %collective-permute-start.6 = (bf16[512,256]{0,1:T(8,128)(2,1)S(1)}, bf16[512,256]{0,1:T(8,128)(2,1)S(1)}, u32[]{:S(2)}, u32[]{:S(2)}) collective-permute-start(bf16[512,256]{0,1:T(8,128)(2,1)S(1)} %get-tuple-element.27), channel_id=1, source_target_pairs={{0,4},{4,8},{8,12},{12,16},{16,20},{20,24},{24,28},{1,5},{5,9},{9,... | collective-permute-start | bytes 786440 | tf_op jit(solution)/shard_map/ppermute | solution.py:12
  15.4 9.2 %collective-permute-start.7 = (bf16[512,256]{0,1:T(8,128)(2,1)S(1)}, bf16[512,256]{0,1:T(8,128)(2,1)S(1)}, u32[]{:S(2)}, u32[]{:S(2)}) collective-permute-start(bf16[512,256]{0,1:T(8,128)(2,1)S(1)} %get-tuple-element.28), channel_id=1, source_target_pairs={{0,1},{1,2},{2,3},{4,5},{5,6},{6,7},{8,9},{9,10},{10,11},{12,13},{... | collective-permute-start | bytes 786440 | tf_op jit(solution)/shard_map/ppermute | solution.py:12
  19.2 11.5 %collective-permute-start.2 = (bf16[512,256]{0,1:T(8,128)(2,1)S(1)}, bf16[512,256]{0,1:T(8,128)(2,1)S(1)}, u32[]{:S(2)}, u32[]{:S(2)}) collective-permute-start(bf16[512,256]{0,1:T(8,128)(2,1)S(1)} %get-tuple-element.15), channel_id=1, source_target_pairs={{0,4},{4,8},{8,12},{12,16},{16,20},{20,24},{24,28},{1,5},{5,9},{9,... | collective-permute-start | bytes 786440 | tf_op jit(solution)/shard_map/ppermute | solution.py:12
  22.3 8.4 %collective-permute-start.3 = (bf16[512,256]{0,1:T(8,128)(2,1)S(1)}, bf16[512,256]{0,1:T(8,128)(2,1)S(1)}, u32[]{:S(2)}, u32[]{:S(2)}) collective-permute-start(bf16[512,256]{0,1:T(8,128)(2,1)S(1)} %get-tuple-element.16), channel_id=1, source_target_pairs={{0,1},{1,2},{2,3},{4,5},{5,6},{6,7},{8,9},{9,10},{10,11},{12,13},{... | collective-permute-start | bytes 786440 | tf_op jit(solution)/shard_map/ppermute | solution.py:12
  25.3 11.6 %collective-permute-start.8 = (bf16[512,256]{0,1:T(8,128)(2,1)S(1)}, bf16[512,256]{0,1:T(8,128)(2,1)S(1)}, u32[]{:S(2)}, u32[]{:S(2)}) collective-permute-start(bf16[512,256]{0,1:T(8,128)(2,1)S(1)} %get-tuple-element.25), channel_id=1, source_target_pairs={{0,4},{4,8},{8,12},{12,16},{16,20},{20,24},{24,28},{1,5},{5,9},{9,... | collective-permute-start | bytes 786440 | tf_op jit(solution)/shard_map/ppermute | solution.py:12
  28.5 8.4 %collective-permute-start.9 = (bf16[512,256]{0,1:T(8,128)(2,1)S(1)}, bf16[512,256]{0,1:T(8,128)(2,1)S(1)}, u32[]{:S(2)}, u32[]{:S(2)}) collective-permute-start(bf16[512,256]{0,1:T(8,128)(2,1)S(1)} %get-tuple-element.26), channel_id=1, source_target_pairs={{0,1},{1,2},{2,3},{4,5},{5,6},{6,7},{8,9},{9,10},{10,11},{12,13},{... | collective-permute-start | bytes 786440 | tf_op jit(solution)/shard_map/ppermute | solution.py:12
  31.5 11.6 %collective-permute-start.4 = (bf16[512,256]{0,1:T(8,128)(2,1)S(1)}, bf16[512,256]{0,1:T(8,128)(2,1)S(1)}, u32[]{:S(2)}, u32[]{:S(2)}) collective-permute-start(bf16[512,256]{0,1:T(8,128)(2,1)S(1)} %get-tuple-element.13), channel_id=1, source_target_pairs={{0,4},{4,8},{8,12},{12,16},{16,20},{20,24},{24,28},{1,5},{5,9},{9,... | collective-permute-start | bytes 786440 | tf_op jit(solution)/shard_map/ppermute | solution.py:12
  34.7 8.5 %collective-permute-start.5 = (bf16[512,256]{0,1:T(8,128)(2,1)S(1)}, bf16[512,256]{0,1:T(8,128)(2,1)S(1)}, u32[]{:S(2)}, u32[]{:S(2)}) collective-permute-start(bf16[512,256]{0,1:T(8,128)(2,1)S(1)} %get-tuple-element.14), channel_id=1, source_target_pairs={{0,1},{1,2},{2,3},{4,5},{5,6},{6,7},{8,9},{9,10},{10,11},{12,13},{... | collective-permute-start | bytes 786440 | tf_op jit(solution)/shard_map/ppermute | solution.py:12
  37.8 8.6 %collective-permute-start.10 = (bf16[512,256]{0,1:T(8,128)(2,1)S(1)}, bf16[512,256]{0,1:T(8,128)(2,1)S(1)}, u32[]{:S(2)}, u32[]{:S(2)}) collective-permute-start(bf16[512,256]{0,1:T(8,128)(2,1)S(1)} %get-tuple-element.23), channel_id=1, source_target_pairs={{0,4},{4,8},{8,12},{12,16},{16,20},{20,24},{24,28},{1,5},{5,9},{9,... | collective-permute-start | bytes 786440 | tf_op jit(solution)/shard_map/ppermute | solution.py:12
  40.9 5.5 %collective-permute-start.11 = (bf16[512,256]{0,1:T(8,128)(2,1)S(1)}, bf16[512,256]{0,1:T(8,128)(2,1)S(1)}, u32[]{:S(2)}, u32[]{:S(2)}) collective-permute-start(bf16[512,256]{0,1:T(8,128)(2,1)S(1)} %get-tuple-element.24), channel_id=1, source_target_pairs={{0,1},{1,2},{2,3},{4,5},{5,6},{6,7},{8,9},{9,10},{10,11},{12,13},{... | collective-permute-start | bytes 786440 | tf_op jit(solution)/shard_map/ppermute | solution.py:12
  44.0 3.3 %copy-start.5 = (bf16[1,1,256,1024]{3,2,1,0:T(8,128)(2,1)S(1)}, bf16[1,1,256,1024]{3,2,1,0:T(8,128)(2,1)}, u32[]{:S(2)}) copy-start(bf16[1,1,256,1024]{3,2,1,0:T(8,128)(2,1)} %param.7) | copy-start | bytes 1572868
  47.7 16.1 %copy-start.1 = (f32[512,256]{0,1:T(8,128)}, f32[512,256]{0,1:T(8,128)S(1)}, u32[]{:S(2)}) copy-start(f32[512,256]{0,1:T(8,128)S(1)} %fusion.64) | copy-start | bytes 1572868
  47.8 5.4 %collective-permute-start.12 = (bf16[1,16,512]{2,1,0:T(8,128)(2,1)S(1)}, bf16[1,16,512]{2,1,0:T(8,128)(2,1)S(1)}, u32[]{:S(2)}, u32[]{:S(2)}) collective-permute-start(bf16[1,16,512]{2,1,0:T(8,128)(2,1)S(1)} %get-tuple-element.31), channel_id=1, source_target_pairs={{0,4},{4,8},{8,12},{12,16},{16,20},{20,24},{24,28},{1,5},{5,9},{9,... | collective-permute-start | bytes 49160 | tf_op jit(solution)/shard_map/ppermute | solution.py:23
  51.8 5.1 %collective-permute-start.13 = (bf16[1,16,512]{2,1,0:T(8,128)(2,1)S(1)}, bf16[1,16,512]{2,1,0:T(8,128)(2,1)S(1)}, u32[]{:S(2)}, u32[]{:S(2)}) collective-permute-start(bf16[1,16,512]{2,1,0:T(8,128)(2,1)S(1)} %get-tuple-element.32), channel_id=1, source_target_pairs={{4,0},{8,4},{12,8},{16,12},{20,16},{24,20},{28,24},{5,1},{9,5},{13... | collective-permute-start | bytes 49160 | tf_op jit(solution)/shard_map/ppermute | solution.py:25
  57.6 8.3 %collective-permute-start.14 = (bf16[18,1,512]{2,1,0:T(2,128)(2,1)}, bf16[18,1,512]{2,1,0:T(2,128)(2,1)S(1)}, u32[]{:S(2)}, u32[]{:S(2)}) collective-permute-start(bf16[18,1,512]{2,1,0:T(2,128)(2,1)} %get-tuple-element.29), channel_id=1, source_target_pairs={{0,1},{1,2},{2,3},{4,5},{5,6},{6,7},{8,9},{9,10},{10,11},{12,13},{... | collective-permute-start | bytes 55304 | tf_op jit(solution)/shard_map/ppermute | solution.py:23
  61.9 5.3 %collective-permute-start.15 = (bf16[18,1,512]{2,1,0:T(2,128)(2,1)S(1)}, bf16[18,1,512]{2,1,0:T(2,128)(2,1)S(1)}, u32[]{:S(2)}, u32[]{:S(2)}) collective-permute-start(bf16[18,1,512]{2,1,0:T(2,128)(2,1)S(1)} %get-tuple-element.30), channel_id=1, source_target_pairs={{1,0},{2,1},{3,2},{5,4},{6,5},{7,6},{9,8},{10,9},{11,10},{13,12},{... | collective-permute-start | bytes 55304 | tf_op jit(solution)/shard_map/ppermute | solution.py:25
  64.9 2.5 %copy-start.2 = (f32[512,256]{0,1:T(8,128)S(1)}, f32[512,256]{0,1:T(8,128)}, u32[]{:S(2)}) copy-start(f32[512,256]{0,1:T(8,128)} %copy-done.1) | copy-start | bytes 1572868
where the time goes:
time: 69.7 us; the launch traced here: 69.1 us
  starting transfers between devices  46.2 us (66%)
  waiting for transfers between devices  7.52 us (11%)
  matrix products  6.62 us (9%)
  local copies, waits for them, and re-layouts  4.23 us (6%)
  other arithmetic  3.47 us (5%)
  between operations  1.09 us (2%)
    ppermute x12, starting transfers between devices, from_behind(): return lax.ppermute(block, axis, route)  34.7 us
    ppermute x2, starting transfers between devices, extended(): lax.ppermute(tail, axis, [(i, (i + 1) % count) for i in range(ends)])  8.25 us
    dot_general x8, matrix products, advance(): jnp.dot(mapping, stacked, preferred_element_type=jnp.float32)  6.16 us
    ppermute x2, waiting for transfers between devices, extended(): lax.ppermute(head, axis, [((i + 1) % count, i) for i in range(ends)])  5.07 us
    ppermute x2, starting transfers between devices, extended(): lax.ppermute(head, axis, [((i + 1) % count, i) for i in range(ends)])  3.21 us
    unnamed x14, local copies, waits for them, and re-layouts  2.53 us
    ppermute x12, waiting for transfers between devices, from_behind(): return lax.ppermute(block, axis, route)  2.45 us
    add x1, other arithmetic, per_device(): residual = beside - 4.0 * volume + wavenum[:, :, None] * volume  1.73 us
  transfers between devices with their start and end apart: 16, of which 4 were waited for; matrix products, arithmetic and copies ran while one was open for 11% of the time, Pallas kernels for 0%

commit v1 on v0

v1 whole, which is shorter than its diff:
```python
import jax
import jax.numpy as jnp
from jax import lax
from jax.sharding import PartitionSpec as P

STEPS = 4
CHUNKS = 2


def shifted(block, axis, step):
    count = lax.axis_size(axis)
    end = count - 1 if step > 0 else 0
    block = jnp.where(lax.axis_index(axis) == end, jnp.zeros_like(block), block)
    return lax.ppermute(block, axis, [(i, (i + step) % count) for i in range(count)])


def advance(mapping, left_in, lower_in):
    stacked = jnp.concatenate([left_in, lower_in], axis=0)
    outgoing = jnp.dot(mapping, stacked, preferred_element_type=jnp.float32).astype(jnp.bfloat16)
    rows = left_in.shape[0]
    return (outgoing[:rows], outgoing[rows:])


def per_device(impedance, rebuild_map, left_trace, lower_trace, cell_kind, kind_wavenum):
    mapping = impedance[0, 0]
    sources = left_trace.shape[3]
    width = sources // CHUNKS
    left_in = [left_trace[0, 0, :, c * width : (c + 1) * width] for c in range(CHUNKS)]
    lower_in = [lower_trace[0, 0, :, c * width : (c + 1) * width] for c in range(CHUNKS)]
    for _ in range(STEPS - 1):
        for c in range(CHUNKS):
            right, upper = advance(mapping, left_in[c], lower_in[c])
            left_in[c] = shifted(right, "gx", 1)
            lower_in[c] = shifted(upper, "gy", 1)
    left_in = jnp.concatenate(left_in, axis=1)
    lower_in = jnp.concatenate(lower_in, axis=1)
    cells_x, cells_y = cell_kind.shape
    stacked = jnp.concatenate([left_in, lower_in], axis=0)
    volume = jnp.dot(rebuild_map[0, 0], stacked, preferred_element_type=jnp.float32).reshape(
        cells_x, cells_y, sources
    )
    low = volume.astype(jnp.bfloat16)
    from_left = shifted(low[-1], "gx", 1)
    from_right = shifted(low[0], "gx", -1)
    from_below = shifted(low[:, -1], "gy", 1)
    from_above = shifted(low[:, 0], "gy", -1)
    right_out, upper_out = advance(mapping, left_in, lower_in)
    f32 = jnp.float32
    along_x = jnp.concatenate([from_left[None].astype(f32), volume, from_right[None].astype(f32)], axis=0)
    along_y = jnp.concatenate([from_below[:, None].astype(f32), volume, from_above[:, None].astype(f32)], axis=1)
    beside = along_x[2:] + along_x[:-2] + along_y[:, 2:] + along_y[:, :-2]
    kind_ids = jnp.arange(kind_wavenum.shape[0], dtype=jnp.int32)
    wavenum = jnp.sum(
        jnp.where(
            cell_kind[:, :, None] == kind_ids[None, None, :],
            kind_wavenum[None, None, :],
            jnp.float32(0.0),
        ),
        axis=-1,
    )
    residual = beside - 4.0 * volume + wavenum[:, :, None] * volume
    return (right_out[None, None], upper_out[None, None], residual)


def solution(mesh):
    return jax.shard_map(
        per_device,
        mesh=mesh,
        in_specs=(
            P("gx", "gy", None, None),
            P("gx", "gy", None, None),
            P("gx", "gy", None, None),
            P("gx", "gy", None, None),
            P("gx", "gy"),
            P(),
        ),
        out_specs=(P("gx", "gy", None, None), P("gx", "gy", None, None), P("gx", "gy", None)),
        check_vma=False,
    )
```

time: 69.7 us -> 60.8 us (0.87)
  the two profiles are of different devices: /device:TPU:1 before, /device:TPU:0 now
where the time goes in v1:
time: 60.8 us; the launch traced here: 60.6 us
  waiting for transfers between devices  31.1 us (51%)
  starting transfers between devices  12.2 us (20%)
  matrix products  8.8 us (14%)
  local copies, waits for them, and re-layouts  5.86 us (10%)
  other arithmetic  1.62 us (3%)
  between operations  0.97 us (2%)
    ppermute x16, waiting for transfers between devices, shifted(): lax.ppermute(block, axis, [(i, (i + step) % count) for i in range(count)])  31.1 us
    ppermute x16, starting transfers between devices, shifted(): lax.ppermute(block, axis, [(i, (i + step) % count) for i in range(count)])  12.2 us
    dot_general x7, matrix products, advance(): jnp.dot(mapping, stacked, preferred_element_type=jnp.float32)  7.06 us
    unnamed x10, local copies, waits for them, and re-layouts  3.56 us
    dot_general x1, matrix products, per_device(): jnp.dot(rebuild_map[0, 0], stacked, preferred_element_type=jnp.float32)  1.74 us
    squeeze x1, local copies, waits for them, and re-layouts, per_device(): lower_trace[0, 0, :, c * width:(c + 1) * width]  1.4 us
  transfers between devices with their start and end apart: 16, of which 7 were waited for; matrix products, arithmetic and copies ran while one was open for 18% of the time, Pallas kernels for 0%

profile of v1, /device:TPU:0, one launch (start us, length us, event | category | flops | bytes accessed | tf_op | source)
XLA Modules:
  0.0 60.6 jit_solution(9645929193913346786)
XLA Ops:
  0.6 0.0 copy-start
  0.7 1.4 %slice_bitcast_fusion.4 = (bf16[512,256]{1,0:T(8,128)(2,1)S(1)}, bf16[512,256]{1,0:T(8,128)(2,1)S(1)}, bf16[512,256]{1,0:T(8,128)(2,1)S(1)}, bf16[512,256]{1,0:T(8,128)(2,1)S(1)}) fusion(bf16[1,1,512,512]{3,2,1,0:T(8,128)(2,1)} %param.9, bf16[1,1,512,512]{3,2,1,0:T(8,128)(2,1)} %param.8), kind=kLoop, calls=%fused_computation.74 | loop fusion | bytes 2097152 | tf_op jit(solution)/shard_map/squeeze | solution.py:29
  2.1 0.5 copy-done
  2.5 0.8 %fusion.53 = bf16[1024,256]{0,1:T(8,128)(2,1)S(1)} fusion(bf16[1,1,1024,1024]{3,2,1,0:T(8,128)(2,1)S(1)} %copy-done, bf16[512,256]{1,0:T(8,128)(2,1)S(1)} %get-tuple-element.27, bf16[512,256]{1,0:T(8,128)(2,1)S(1)} %get-tuple-element.38), kind=kOutput, calls=%fused_computation.27 | convolution fusion | flops 538181632 | bytes 3145728 | tf_op jit(solution)/shard_map/dot_general | solution.py:19
  3.4 3.0 %collective-permute-start = (bf16[512,256]{0,1:T(8,128)(2,1)S(1)}, bf16[512,256]{0,1:T(8,128)(2,1)S(1)}, u32[]{:S(2)}, u32[]{:S(2)}) collective-permute-start(bf16[512,256]{0,1:T(8,128)(2,1)S(1)} %get-tuple-element.23), channel_id=1, source_target_pairs={{0,4},{4,8},{8,12},{12,16},{16,20},{20,24},{24,28},{28,0},{1,5},{5... | collective-permute-start | bytes 786440 | tf_op jit(solution)/shard_map/ppermute | solution.py:14
  6.4 0.0 collective-permute-start.1
  6.4 0.8 %fusion.44 = bf16[1024,256]{0,1:T(8,128)(2,1)S(1)} fusion(bf16[1,1,1024,1024]{3,2,1,0:T(8,128)(2,1)S(1)} %copy-done, bf16[512,256]{1,0:T(8,128)(2,1)S(1)} %get-tuple-element.28, bf16[512,256]{1,0:T(8,128)(2,1)S(1)} %get-tuple-element.37), kind=kOutput, calls=%fused_computation.24 | convolution fusion | flops 538181632 | bytes 3145728 | tf_op jit(solution)/shard_map/dot_general | solution.py:19
  7.2 1.6 %collective-permute-start.5 = (bf16[512,256]{0,1:T(8,128)(2,1)S(1)}, bf16[512,256]{0,1:T(8,128)(2,1)S(1)}, u32[]{:S(2)}, u32[]{:S(2)}) collective-permute-start(bf16[512,256]{0,1:T(8,128)(2,1)S(1)} %get-tuple-element.31), channel_id=1, source_target_pairs={{0,4},{4,8},{8,12},{12,16},{16,20},{20,24},{24,28},{28,0},{1,5},{5... | collective-permute-start | bytes 786440 | tf_op jit(solution)/shard_map/ppermute | solution.py:14
  8.8 1.3 %collective-permute-start.6 = (bf16[512,256]{0,1:T(8,128)(2,1)S(1)}, bf16[512,256]{0,1:T(8,128)(2,1)S(1)}, u32[]{:S(2)}, u32[]{:S(2)}) collective-permute-start(bf16[512,256]{0,1:T(8,128)(2,1)S(1)} %get-tuple-element.32), channel_id=1, source_target_pairs={{0,1},{1,2},{2,3},{3,0},{4,5},{5,6},{6,7},{7,4},{8,9},{9,10},{10,1... | collective-permute-start | bytes 786440 | tf_op jit(solution)/shard_map/ppermute | solution.py:14
  10.2 6.4 %collective-permute-done = bf16[512,256]{0,1:T(8,128)(2,1)S(1)} collective-permute-done((bf16[512,256]{0,1:T(8,128)(2,1)S(1)}, bf16[512,256]{0,1:T(8,128)(2,1)S(1)}, u32[]{:S(2)}, u32[]{:S(2)}) %collective-permute-start) | collective-permute-done | bytes 262176 | tf_op jit(solution)/shard_map/ppermute | solution.py:14
  16.6 0.0 collective-permute-done.1
  16.6 0.8 %fusion.50 = bf16[1024,256]{0,1:T(8,128)(2,1)S(1)} fusion(bf16[1,1,1024,1024]{3,2,1,0:T(8,128)(2,1)S(1)} %copy-done, bf16[512,256]{0,1:T(8,128)(2,1)S(1)} %collective-permute-done.1, bf16[512,256]{0,1:T(8,128)(2,1)S(1)} %collective-permute-done), kind=kOutput, calls=%fused_computation.26 | convolution fusion | flops 538181632 | bytes 3145728 | tf_op jit(solution)/shard_map/dot_general | solution.py:19
  17.4 0.1 collective-permute-start.2
  17.5 0.1 collective-permute-start.3
  17.6 4.0 %collective-permute-done.5 = bf16[512,256]{0,1:T(8,128)(2,1)S(1)} collective-permute-done((bf16[512,256]{0,1:T(8,128)(2,1)S(1)}, bf16[512,256]{0,1:T(8,128)(2,1)S(1)}, u32[]{:S(2)}, u32[]{:S(2)}) %collective-permute-start.5) | collective-permute-done | bytes 262176 | tf_op jit(solution)/shard_map/ppermute | solution.py:14
  21.5 0.0 collective-permute-done.6
  21.5 0.8 %fusion.41 = bf16[1024,256]{0,1:T(8,128)(2,1)S(1)} fusion(bf16[1,1,1024,1024]{3,2,1,0:T(8,128)(2,1)S(1)} %copy-done, bf16[512,256]{0,1:T(8,128)(2,1)S(1)} %collective-permute-done.6, bf16[512,256]{0,1:T(8,128)(2,1)S(1)} %collective-permute-done.5), kind=kOutput, calls=%fused_computation.23 | convolution fusion | flops 538181632 | bytes 3145728 | tf_op jit(solution)/shard_map/dot_general | solution.py:19
  22.4 0.1 collective-permute-start.7
  22.4 0.1 collective-permute-start.8
  22.5 4.6 %collective-permute-done.2 = bf16[512,256]{0,1:T(8,128)(2,1)S(1)} collective-permute-done((bf16[512,256]{0,1:T(8,128)(2,1)S(1)}, bf16[512,256]{0,1:T(8,128)(2,1)S(1)}, u32[]{:S(2)}, u32[]{:S(2)}) %collective-permute-start.2) | collective-permute-done | bytes 262176 | tf_op jit(solution)/shard_map/ppermute | solution.py:14
  27.1 0.0 collective-permute-done.3
  27.1 0.8 %fusion.47 = bf16[1024,256]{0,1:T(8,128)(2,1)S(1)} fusion(bf16[1,1,1024,1024]{3,2,1,0:T(8,128)(2,1)S(1)} %copy-done, bf16[512,256]{0,1:T(8,128)(2,1)S(1)} %collective-permute-done.3, bf16[512,256]{0,1:T(8,128)(2,1)S(1)} %collective-permute-done.2), kind=kOutput, calls=%fused_computation.25 | convolution fusion | flops 538181632 | bytes 3145728 | tf_op jit(solution)/shard_map/dot_general | solution.py:19
  28.0 0.1 collective-permute-start.10
  28.0 0.0 copy-start.1
  28.1 0.0 copy-start.2
  28.1 0.1 collective-permute-start.4
  28.1 4.4 %collective-permute-done.7 = bf16[512,256]{0,1:T(8,128)(2,1)S(1)} collective-permute-done((bf16[512,256]{0,1:T(8,128)(2,1)S(1)}, bf16[512,256]{0,1:T(8,128)(2,1)S(1)}, u32[]{:S(2)}, u32[]{:S(2)}) %collective-permute-start.7) | collective-permute-done | bytes 262176 | tf_op jit(solution)/shard_map/ppermute | solution.py:14
  32.6 0.0 collective-permute-done.8
  32.6 0.8 %fusion.38 = bf16[1024,256]{0,1:T(8,128)(2,1)S(1)} fusion(bf16[1,1,1024,1024]{3,2,1,0:T(8,128)(2,1)S(1)} %copy-done, bf16[512,256]{0,1:T(8,128)(2,1)S(1)} %collective-permute-done.8, bf16[512,256]{0,1:T(8,128)(2,1)S(1)} %collective-permute-done.7), kind=kOutput, calls=%fused_computation.22 | convolution fusion | flops 538181632 | bytes 3145728 | tf_op jit(solution)/shard_map/dot_general | solution.py:19
  33.4 0.1 collective-permute-start.11
  33.5 0.1 collective-permute-start.9
  33.5 0.0 copy-done.1
  33.6 0.0 copy-done.2
  33.6 0.2 select_reduce_fusion
  33.8 0.1 collective-permute-done.10
  33.8 5.5 %collective-permute-done.4 = bf16[512,256]{0,1:T(8,128)(2,1)} collective-permute-done((bf16[512,256]{0,1:T(8,128)(2,1)S(1)}, bf16[512,256]{0,1:T(8,128)(2,1)}, u32[]{:S(2)}, u32[]{:S(2)}) %collective-permute-start.4) | collective-permute-done | bytes 262176 | tf_op jit(solution)/shard_map/ppermute | solution.py:14
  39.3 0.0 collective-permute-done.11
  39.4 6.0 %collective-permute-done.9 = bf16[512,256]{0,1:T(8,128)(2,1)} collective-permute-done((bf16[512,256]{0,1:T(8,128)(2,1)S(1)}, bf16[512,256]{0,1:T(8,128)(2,1)}, u32[]{:S(2)}, u32[]{:S(2)}) %collective-permute-start.9) | collective-permute-done | bytes 262176 | tf_op jit(solution)/shard_map/ppermute | solution.py:14
  45.3 1.7 %fusion.79 = f32[512,256]{0,1:T(8,128)S(1)} fusion(bf16[1,1,256,1024]{3,2,1,0:T(8,128)(2,1)} %param.7, bf16[512,256]{0,1:T(8,128)(2,1)} %collective-permute-done.11, bf16[512,256]{0,1:T(8,128)(2,1)S(1)} %collective-permute-done.10, bf16[512,256]{0,1:T(8,128)(2,1)} %collective-permute-done.9, bf16[512,256]{0,1:T(8,128)(2,1)} %collective-permute-done.4), kind=kOutput, calls=%fused_computation.58 | convolution fusion | flops 272629760 | bytes 2097152 | tf_op jit(solution)/shard_map/dot_general | solution.py:39
  47.1 0.1 broadcast_select_fusion.1
  47.2 1.0 %collective-permute-start.14 = (bf16[16,512]{1,0:T(8,128)(2,1)S(1)}, bf16[16,512]{1,0:T(8,128)(2,1)S(1)}, u32[]{:S(2)}, u32[]{:S(2)}) collective-permute-start(bf16[16,512]{1,0:T(8,128)(2,1)S(1)} %bitcast.93), channel_id=1, source_target_pairs={{0,3},{1,0},{2,1},{3,2},{4,7},{5,4},{6,5},{7,6},{8,11},{9,8},{10,9... | collective-permute-start | bytes 49160 | tf_op jit(solution)/shard_map/ppermute | solution.py:14
  48.3 0.0 collective-permute-start.15
  48.3 0.1 collective-permute-start.13
  48.4 4.7 %collective-permute-start.12 = (bf16[16,512]{1,0:T(8,128)(2,1)S(1)}, bf16[16,512]{1,0:T(8,128)(2,1)S(1)}, u32[]{:S(2)}, u32[]{:S(2)}) collective-permute-start(bf16[16,512]{1,0:T(8,128)(2,1)S(1)} %get-tuple-element.33), channel_id=1, source_target_pairs={{0,28},{4,0},{8,4},{12,8},{16,12},{20,16},{24,20},{28,24},{1,29},{... | collective-permute-start | bytes 49160 | tf_op jit(solution)/shard_map/ppermute | solution.py:14
  53.1 2.4 %fusion.17 = bf16[1024,512]{0,1:T(8,128)(2,1)S(1)} fusion(bf16[1,1,1024,1024]{3,2,1,0:T(8,128)(2,1)S(1)} %copy-done, bf16[512,256]{0,1:T(8,128)(2,1)} %collective-permute-done.11, bf16[512,256]{0,1:T(8,128)(2,1)S(1)} %collective-permute-done.10, bf16[512,256]{0,1:T(8,128)(2,1)} %collective-permute-done.9, bf16[512,256]{0,1:T(8,128)(2,1)} %collective-permute-done.4), kind=kOutput, calls=%fused_computation.15 | convolution fusion | flops 1078460416 | bytes 4194304 | tf_op jit(solution)/shard_map/dot_general | solution.py:19
  55.5 0.9 %slice_bitcast_fusion = (bf16[1,1,512,512]{2,3,1,0:T(8,128)(2,1)S(1)}, bf16[1,1,512,512]{2,3,1,0:T(8,128)(2,1)}) fusion(bf16[1024,512]{0,1:T(8,128)(2,1)S(1)} %fusion.17), kind=kLoop, calls=%fused_computation.38 | loop fusion | bytes 2097152 | tf_op jit(solution)/shard_map/broadcast_in_dim | solution.py:62
  56.4 2.0 %copy.19 = bf16[1,1,512,512]{3,2,1,0:T(8,128)(2,1)} copy(bf16[1,1,512,512]{2,3,1,0:T(8,128)(2,1)} %get-tuple-element.16) | data formatting | bytes 1048576
  58.4 1.0 %copy.20 = bf16[1,1,512,512]{3,2,1,0:T(8,128)(2,1)} copy(bf16[1,1,512,512]{2,3,1,0:T(8,128)(2,1)S(1)} %get-tuple-element.15) | data formatting | bytes 1048576
  59.4 0.0 collective-permute-done.13
  59.4 0.0 collective-permute-done.14
  59.4 0.0 collective-permute-done.15
  59.5 0.0 collective-permute-done.12
  59.5 1.1 %fusion.58 = f32[16,16,512]{2,1,0:T(8,128)} fusion(f32[16,16,512]{2,1,0:T(8,128)S(1)} %bitcast.92, f32[16,1,512]{2,1,0:T(1,128)S(1)} %reshape.36, f32[16,1,512]{2,1,0:T(1,128)S(1)} %reshape.35, f32[1,16,512]{2,1,0:T(8,128)S(1)} %bitcast_convert_fusion, f32[1,16,512]{2,1,0:T(8,128)S(1)} %bitcast_convert_fusion.1, f32[16,16]{1,0:T(8,128)S(1)} %select_reduce_fusion), kind=kLoop, calls=%fused_computation.32 | loop fusion | flops 1441792 | bytes 1180672 | tf_op jit(solution)/shard_map/add | solution.py:61
  (14 shorter events, 0.4 us)
Async XLA Ops:
  0.6 1.9 %copy-start = (bf16[1,1,1024,1024]{3,2,1,0:T(8,128)(2,1)S(1)}, bf16[1,1,1024,1024]{3,2,1,0:T(8,128)(2,1)}, u32[]{:S(2)}) copy-start(bf16[1,1,1024,1024]{3,2,1,0:T(8,128)(2,1)} %param.6) | copy-start | bytes 6291460
  3.4 13.2 %collective-permute-start = (bf16[512,256]{0,1:T(8,128)(2,1)S(1)}, bf16[512,256]{0,1:T(8,128)(2,1)S(1)}, u32[]{:S(2)}, u32[]{:S(2)}) collective-permute-start(bf16[512,256]{0,1:T(8,128)(2,1)S(1)} %get-tuple-element.23), channel_id=1, source_target_pairs={{0,4},{4,8},{8,12},{12,16},{16,20},{20,24},{24,28},{28,0},{1,5},{5... | collective-permute-start | bytes 786440 | tf_op jit(solution)/shard_map/ppermute | solution.py:14
  6.4 10.2 %collective-permute-start.1 = (bf16[512,256]{0,1:T(8,128)(2,1)S(1)}, bf16[512,256]{0,1:T(8,128)(2,1)S(1)}, u32[]{:S(2)}, u32[]{:S(2)}) collective-permute-start(bf16[512,256]{0,1:T(8,128)(2,1)S(1)} %get-tuple-element.24), channel_id=1, source_target_pairs={{0,1},{1,2},{2,3},{3,0},{4,5},{5,6},{6,7},{7,4},{8,9},{9,10},{10,1... | collective-permute-start | bytes 786440 | tf_op jit(solution)/shard_map/ppermute | solution.py:14
  7.2 14.3 %collective-permute-start.5 = (bf16[512,256]{0,1:T(8,128)(2,1)S(1)}, bf16[512,256]{0,1:T(8,128)(2,1)S(1)}, u32[]{:S(2)}, u32[]{:S(2)}) collective-permute-start(bf16[512,256]{0,1:T(8,128)(2,1)S(1)} %get-tuple-element.31), channel_id=1, source_target_pairs={{0,4},{4,8},{8,12},{12,16},{16,20},{20,24},{24,28},{28,0},{1,5},{5... | collective-permute-start | bytes 786440 | tf_op jit(solution)/shard_map/ppermute | solution.py:14
  8.8 12.7 %collective-permute-start.6 = (bf16[512,256]{0,1:T(8,128)(2,1)S(1)}, bf16[512,256]{0,1:T(8,128)(2,1)S(1)}, u32[]{:S(2)}, u32[]{:S(2)}) collective-permute-start(bf16[512,256]{0,1:T(8,128)(2,1)S(1)} %get-tuple-element.32), channel_id=1, source_target_pairs={{0,1},{1,2},{2,3},{3,0},{4,5},{5,6},{6,7},{7,4},{8,9},{9,10},{10,1... | collective-permute-start | bytes 786440 | tf_op jit(solution)/shard_map/ppermute | solution.py:14
  17.4 9.7 %collective-permute-start.2 = (bf16[512,256]{0,1:T(8,128)(2,1)S(1)}, bf16[512,256]{0,1:T(8,128)(2,1)S(1)}, u32[]{:S(2)}, u32[]{:S(2)}) collective-permute-start(bf16[512,256]{0,1:T(8,128)(2,1)S(1)} %get-tuple-element.21), channel_id=1, source_target_pairs={{0,4},{4,8},{8,12},{12,16},{16,20},{20,24},{24,28},{28,0},{1,5},{5... | collective-permute-start | bytes 786440 | tf_op jit(solution)/shard_map/ppermute | solution.py:14
  17.5 9.6 %collective-permute-start.3 = (bf16[512,256]{0,1:T(8,128)(2,1)S(1)}, bf16[512,256]{0,1:T(8,128)(2,1)S(1)}, u32[]{:S(2)}, u32[]{:S(2)}) collective-permute-start(bf16[512,256]{0,1:T(8,128)(2,1)S(1)} %get-tuple-element.22), channel_id=1, source_target_pairs={{0,1},{1,2},{2,3},{3,0},{4,5},{5,6},{6,7},{7,4},{8,9},{9,10},{10,1... | collective-permute-start | bytes 786440 | tf_op jit(solution)/shard_map/ppermute | solution.py:14
  22.4 10.2 %collective-permute-start.7 = (bf16[512,256]{0,1:T(8,128)(2,1)S(1)}, bf16[512,256]{0,1:T(8,128)(2,1)S(1)}, u32[]{:S(2)}, u32[]{:S(2)}) collective-permute-start(bf16[512,256]{0,1:T(8,128)(2,1)S(1)} %get-tuple-element.29), channel_id=1, source_target_pairs={{0,4},{4,8},{8,12},{12,16},{16,20},{20,24},{24,28},{28,0},{1,5},{5... | collective-permute-start | bytes 786440 | tf_op jit(solution)/shard_map/ppermute | solution.py:14
  22.4 10.1 %collective-permute-start.8 = (bf16[512,256]{0,1:T(8,128)(2,1)S(1)}, bf16[512,256]{0,1:T(8,128)(2,1)S(1)}, u32[]{:S(2)}, u32[]{:S(2)}) collective-permute-start(bf16[512,256]{0,1:T(8,128)(2,1)S(1)} %get-tuple-element.30), channel_id=1, source_target_pairs={{0,1},{1,2},{2,3},{3,0},{4,5},{5,6},{6,7},{7,4},{8,9},{9,10},{10,1... | collective-permute-start | bytes 786440 | tf_op jit(solution)/shard_map/ppermute | solution.py:14
  28.0 5.8 %collective-permute-start.10 = (bf16[512,256]{0,1:T(8,128)(2,1)S(1)}, bf16[512,256]{0,1:T(8,128)(2,1)S(1)}, u32[]{:S(2)}, u32[]{:S(2)}) collective-permute-start(bf16[512,256]{0,1:T(8,128)(2,1)S(1)} %get-tuple-element.18), channel_id=1, source_target_pairs={{0,1},{1,2},{2,3},{3,0},{4,5},{5,6},{6,7},{7,4},{8,9},{9,10},{10,1... | collective-permute-start | bytes 786440 | tf_op jit(solution)/shard_map/ppermute | solution.py:14
  28.0 5.5 %copy-start.1 = (s32[16,16]{1,0:T(8,128)S(1)}, s32[16,16]{1,0:T(8,128)}, u32[]{:S(2)}) copy-start(s32[16,16]{1,0:T(8,128)} %param.10) | copy-start | bytes 3076
  28.1 5.5 %copy-start.2 = (f32[16]{0:T(128)S(1)}, f32[16]{0:T(128)}, u32[]{:S(2)}) copy-start(f32[16]{0:T(128)} %param.11) | copy-start | bytes 196
  28.1 11.3 %collective-permute-start.4 = (bf16[512,256]{0,1:T(8,128)(2,1)S(1)}, bf16[512,256]{0,1:T(8,128)(2,1)}, u32[]{:S(2)}, u32[]{:S(2)}) collective-permute-start(bf16[512,256]{0,1:T(8,128)(2,1)S(1)} %get-tuple-element.17), channel_id=1, source_target_pairs={{0,4},{4,8},{8,12},{12,16},{16,20},{20,24},{24,28},{28,0},{1,5},{5... | collective-permute-start | bytes 786440 | tf_op jit(solution)/shard_map/ppermute | solution.py:14
  33.4 6.0 %collective-permute-start.11 = (bf16[512,256]{0,1:T(8,128)(2,1)S(1)}, bf16[512,256]{0,1:T(8,128)(2,1)}, u32[]{:S(2)}, u32[]{:S(2)}) collective-permute-start(bf16[512,256]{0,1:T(8,128)(2,1)S(1)} %get-tuple-element.20), channel_id=1, source_target_pairs={{0,1},{1,2},{2,3},{3,0},{4,5},{5,6},{6,7},{7,4},{8,9},{9,10},{10,1... | collective-permute-start | bytes 786440 | tf_op jit(solution)/shard_map/ppermute | solution.py:14
  33.5 11.9 %collective-permute-start.9 = (bf16[512,256]{0,1:T(8,128)(2,1)S(1)}, bf16[512,256]{0,1:T(8,128)(2,1)}, u32[]{:S(2)}, u32[]{:S(2)}) collective-permute-start(bf16[512,256]{0,1:T(8,128)(2,1)S(1)} %get-tuple-element.19), channel_id=1, source_target_pairs={{0,4},{4,8},{8,12},{12,16},{16,20},{20,24},{24,28},{28,0},{1,5},{5... | collective-permute-start | bytes 786440 | tf_op jit(solution)/shard_map/ppermute | solution.py:14
  47.2 12.2 %collective-permute-start.14 = (bf16[16,512]{1,0:T(8,128)(2,1)S(1)}, bf16[16,512]{1,0:T(8,128)(2,1)S(1)}, u32[]{:S(2)}, u32[]{:S(2)}) collective-permute-start(bf16[16,512]{1,0:T(8,128)(2,1)S(1)} %bitcast.93), channel_id=1, source_target_pairs={{0,3},{1,0},{2,1},{3,2},{4,7},{5,4},{6,5},{7,6},{8,11},{9,8},{10,9... | collective-permute-start | bytes 49160 | tf_op jit(solution)/shard_map/ppermute | solution.py:14
  48.3 11.2 %collective-permute-start.15 = (bf16[16,512]{1,0:T(8,128)(2,1)S(1)}, bf16[16,512]{1,0:T(8,128)(2,1)S(1)}, u32[]{:S(2)}, u32[]{:S(2)}) collective-permute-start(bf16[16,512]{1,0:T(8,128)(2,1)S(1)} %bitcast.94), channel_id=1, source_target_pairs={{0,1},{1,2},{2,3},{3,0},{4,5},{5,6},{6,7},{7,4},{8,9},{9,10},{10,1... | collective-permute-start | bytes 49160 | tf_op jit(solution)/shard_map/ppermute | solution.py:14
  48.3 11.1 %collective-permute-start.13 = (bf16[16,512]{1,0:T(8,128)(2,1)S(1)}, bf16[16,512]{1,0:T(8,128)(2,1)S(1)}, u32[]{:S(2)}, u32[]{:S(2)}) collective-permute-start(bf16[16,512]{1,0:T(8,128)(2,1)S(1)} %get-tuple-element.34), channel_id=1, source_target_pairs={{0,4},{4,8},{8,12},{12,16},{16,20},{20,24},{24,28},{28,0},{1,5},{5... | collective-permute-start | bytes 49160 | tf_op jit(solution)/shard_map/ppermute | solution.py:14
  48.4 11.1 %collective-permute-start.12 = (bf16[16,512]{1,0:T(8,128)(2,1)S(1)}, bf16[16,512]{1,0:T(8,128)(2,1)S(1)}, u32[]{:S(2)}, u32[]{:S(2)}) collective-permute-start(bf16[16,512]{1,0:T(8,128)(2,1)S(1)} %get-tuple-element.33), channel_id=1, source_target_pairs={{0,28},{4,0},{8,4},{12,8},{16,12},{20,16},{24,20},{28,24},{1,29},{... | collective-permute-start | bytes 49160 | tf_op jit(solution)/shard_map/ppermute | solution.py:14

commit v2 on v1

v2 whole, which is shorter than its diff:
```python
import functools

import jax
import jax.numpy as jnp
from jax import lax
from jax.experimental import pallas as pl
from jax.experimental.pallas import tpu as pltpu
from jax.sharding import PartitionSpec as P

STEPS = 4
CHUNKS = 2
F32 = jnp.float32
BF16 = jnp.bfloat16
VMEM = pl.BlockSpec(memory_space=pltpu.VMEM)
HBM = pl.BlockSpec(memory_space=pltpu.HBM)


def around(block, axis):
    count = lax.axis_size(axis)
    return lax.ppermute(block, axis, [(i, (i + 1) % count) for i in range(count)])


def swapped(block, axis, first):
    count = lax.axis_size(axis)
    pairs = [((first + i) % count, (first + (i ^ 1)) % count) for i in range(count)]
    return lax.ppermute(block, axis, sorted(pairs))


def is_last(axis):
    return lax.axis_index(axis) == lax.axis_size(axis) - 1


PARAMS = pltpu.CompilerParams(vmem_limit_bytes=6 * 2**20)


def cost(flops, moved):
    return pl.CostEstimate(flops=flops, bytes_accessed=moved, transcendentals=0)


def product(weights, left, lower):
    half = left.shape[0]
    return jnp.dot(weights[:, :half], left[...], preferred_element_type=F32) + jnp.dot(
        weights[:, half:], lower[...], preferred_element_type=F32
    )


def first_right_kernel(base, width, z_hbm, left_hbm, lower_hbm, out, z_top, left, lower, sem):
    rows = z_top.shape[0]
    block = rows // 2
    loads = [
        pltpu.make_async_copy(left_hbm.at[:, pl.ds(base, width)], left, sem.at[0]),
        pltpu.make_async_copy(lower_hbm.at[:, pl.ds(base, width)], lower, sem.at[1]),
    ]
    parts = [
        pltpu.make_async_copy(z_hbm.at[pl.ds(r * block, block)], z_top.at[pl.ds(r * block, block)], sem.at[2 + r])
        for r in range(2)
    ]
    for copy in loads + parts:
        copy.start()
    for copy in loads:
        copy.wait()
    at_end = is_last("gx")
    for r in range(2):
        parts[r].wait()
        here = pl.ds(r * block, block)
        out[here] = jnp.where(at_end, 0.0, product(z_top.at[here], left, lower)).astype(BF16)


def first_right(z, left, lower, base, width):
    trace = left.shape[0]
    vmem = lambda *shape: jax.ShapeDtypeStruct(shape, BF16)
    return pl.pallas_call(
        functools.partial(first_right_kernel, base, width),
        out_shape=(vmem(trace, width), vmem(trace, 2 * trace), vmem(trace, width), vmem(trace, width)),
        in_specs=[HBM, HBM, HBM],
        out_specs=(VMEM,) * 4,
        scratch_shapes=[pltpu.SemaphoreType.DMA((4,))],
        cost_estimate=cost(4 * trace * trace * width, 3 * trace * trace),
        compiler_params=PARAMS,
        name="first_right",
    )(z, left, lower)


def first_upper_kernel(z_hbm, left, lower, out, z_low, sem):
    rows = z_low.shape[0]
    block = rows // 2
    parts = [
        pltpu.make_async_copy(z_hbm.at[pl.ds(rows + r * block, block)], z_low.at[pl.ds(r * block, block)], sem.at[r])
        for r in range(2)
    ]
    for copy in parts:
        copy.start()
    at_end = is_last("gy")
    for r in range(2):
        parts[r].wait()
        here = pl.ds(r * block, block)
        out[here] = jnp.where(at_end, 0.0, product(z_low.at[here], left, lower)).astype(BF16)


def first_upper(z, left, lower):
    trace, width = left.shape
    vmem = lambda *shape: jax.ShapeDtypeStruct(shape, BF16)
    return pl.pallas_call(
        first_upper_kernel,
        out_shape=(vmem(trace, width), vmem(trace, 2 * trace)),
        in_specs=[HBM, VMEM, VMEM],
        out_specs=(VMEM,) * 2,
        scratch_shapes=[pltpu.SemaphoreType.DMA((2,))],
        cost_estimate=cost(4 * trace * trace * width, 3 * trace * trace),
        compiler_params=PARAMS,
        name="first_upper",
    )(z, left, lower)


def write_both(z_top, z_low, left, lower, right, upper):
    half = left.shape[0] // 2
    for axis, z, out in (("gx", z_top, right), ("gy", z_low, upper)):
        at_end = is_last(axis)
        for r in range(2):
            here = pl.ds(r * half, half)
            out[here] = jnp.where(at_end, 0.0, product(z.at[here], left, lower)).astype(BF16)


def both_loading_kernel(base, z_top, z_low, left_hbm, lower_hbm, right, upper, left, lower, sem):
    width = left.shape[1]
    loads = [
        pltpu.make_async_copy(left_hbm.at[:, pl.ds(base, width)], left, sem.at[0]),
        pltpu.make_async_copy(lower_hbm.at[:, pl.ds(base, width)], lower, sem.at[1]),
    ]
    for copy in loads:
        copy.start()
    for copy in loads:
        copy.wait()
    write_both(z_top, z_low, left, lower, right, upper)


def both_loading(z_top, z_low, left, lower, base, width):
    trace = left.shape[0]
    out = jax.ShapeDtypeStruct((trace, width), BF16)
    return pl.pallas_call(
        functools.partial(both_loading_kernel, base),
        out_shape=(out, out),
        in_specs=[VMEM, VMEM, HBM, HBM],
        out_specs=(VMEM, VMEM),
        scratch_shapes=[
            pltpu.VMEM((trace, width), BF16),
            pltpu.VMEM((trace, width), BF16),
            pltpu.SemaphoreType.DMA((2,)),
        ],
        cost_estimate=cost(8 * trace * trace * width, 4 * trace * trace),
        compiler_params=PARAMS,
        name="both_loading",
    )(z_top, z_low, left, lower)


def both(z_top, z_low, left, lower):
    trace, width = left.shape
    out = jax.ShapeDtypeStruct((trace, width), BF16)
    return pl.pallas_call(
        write_both,
        out_shape=(out, out),
        in_specs=[VMEM] * 4,
        out_specs=(VMEM, VMEM),
        cost_estimate=cost(8 * trace * trace * width, 4 * trace * trace),
        compiler_params=PARAMS,
        name="both",
    )(z_top, z_low, left, lower)


def volume_kernel(weights, left, lower, volume):
    volume[...] = product(weights, left, lower)


def volume_of(weights, left, lower):
    width = left.shape[1]
    return pl.pallas_call(
        volume_kernel,
        out_shape=jax.ShapeDtypeStruct((weights.shape[0], width), F32),
        in_specs=[VMEM] * 3,
        out_specs=VMEM,
        cost_estimate=cost(2 * weights.size * width, weights.size),
        compiler_params=PARAMS,
        name="volume",
    )(weights, left, lower)


def edges_kernel(cells_y, weights, left, lower, done, volume, x_pair, x_cross, y_pair, y_cross):
    cells = weights.shape[0]
    old = done.shape[1]
    volume[...] = product(weights, left, lower)
    even_x = lax.rem(lax.axis_index("gx"), 2) == 0
    even_y = lax.rem(lax.axis_index("gy"), 2) == 0
    for where, block in ((pl.ds(0, old), done), (pl.ds(old, volume.shape[1]), volume)):
        first = block[pl.ds(0, cells_y)]
        last = block[pl.ds(cells - cells_y, cells_y)]
        x_pair[:, where] = jnp.where(even_x, last, first).astype(BF16)
        x_cross[:, where] = jnp.where(even_x, first, last).astype(BF16)
        first = jnp.concatenate([block[pl.ds(x, 1)] for x in range(0, cells, cells_y)], axis=0)
        last = jnp.concatenate([block[pl.ds(x + cells_y - 1, 1)] for x in range(0, cells, cells_y)], axis=0)
        y_pair[:, where] = jnp.where(even_y, last, first).astype(BF16)
        y_cross[:, where] = jnp.where(even_y, first, last).astype(BF16)


def edges_of(weights, left, lower, done, cells_y):
    cells = weights.shape[0]
    width = left.shape[1]
    total = width + done.shape[1]
    line = lambda n: jax.ShapeDtypeStruct((n, total), BF16)
    return pl.pallas_call(
        functools.partial(edges_kernel, cells_y),
        out_shape=(
            jax.ShapeDtypeStruct((cells, width), F32),
            line(cells_y),
            line(cells_y),
            line(cells // cells_y),
            line(cells // cells_y),
        ),
        in_specs=[VMEM] * 4,
        out_specs=(VMEM,) * 5,
        cost_estimate=cost(2 * weights.size * width, weights.size),
        compiler_params=PARAMS,
        name="edges",
    )(weights, left, lower, done)


def last_kernel(base, z_top, z_low, left, lower, *refs):
    right_hbm, upper_hbm, right, upper, sem = refs[-5:]
    width = left.shape[1]
    half = left.shape[0] // 2
    copies = []
    for z, out, out_hbm in ((z_top, right, right_hbm), (z_low, upper, upper_hbm)):
        for r in range(2):
            here = pl.ds(r * half, half)
            out[here] = product(z.at[here], left, lower).astype(BF16)
            copies.append(
                pltpu.make_async_copy(out.at[here], out_hbm.at[here, pl.ds(base, width)], sem.at[len(copies)])
            )
            copies[-1].start()
    for copy in copies:
        copy.wait()


def last(z_top, z_low, left, lower, before, base, total):
    trace, width = left.shape
    out = jax.ShapeDtypeStruct((trace, total), BF16)
    return pl.pallas_call(
        functools.partial(last_kernel, base),
        out_shape=(out, out),
        in_specs=[VMEM] * 4 + [HBM] * len(before),
        out_specs=(HBM, HBM),
        scratch_shapes=[
            pltpu.VMEM((trace, width), BF16),
            pltpu.VMEM((trace, width), BF16),
            pltpu.SemaphoreType.DMA((4,)),
        ],
        input_output_aliases={4 + k: k for k in range(len(before))},
        cost_estimate=cost(8 * trace * trace * width, 4 * trace * trace),
        compiler_params=PARAMS,
        name="last",
    )(z_top, z_low, left, lower, *before)


def beside(axis, pair, cross):
    place = lax.axis_index(axis)
    even = lax.rem(place, 2) == 0
    pair, cross = pair[...].astype(F32), cross[...].astype(F32)
    before = jnp.where(place == 0, 0.0, jnp.where(even, cross, pair))
    after = jnp.where(is_last(axis), 0.0, jnp.where(even, pair, cross))
    return before, after


def residual_kernel(cells_y, wavenum, *refs):
    volumes = refs[:-5]
    x_pair, x_cross, y_pair, y_cross, out = refs[-5:]
    cells = volumes[0].shape[0]
    start = 0
    for volume in volumes:
        width = volume.shape[1]
        where = pl.ds(start, width)
        start += width
        before_x, after_x = beside("gx", x_pair.at[:, where], x_cross.at[:, where])
        before_y, after_y = beside("gy", y_pair.at[:, where], y_cross.at[:, where])
        place = lax.broadcasted_iota(jnp.int32, (cells_y, width), 0)
        for x in range(cells // cells_y):
            here = volume[pl.ds(x * cells_y, cells_y)]
            left = volume[pl.ds((x - 1) * cells_y, cells_y)] if x else before_x
            right = volume[pl.ds((x + 1) * cells_y, cells_y)] if (x + 1) * cells_y < cells else after_x
            below = jnp.where(place == 0, before_y[x : x + 1], pltpu.roll(here, 1, 0))
            above = jnp.where(place == cells_y - 1, after_y[x : x + 1], pltpu.roll(here, cells_y - 1, 0))
            scale = wavenum[pl.ds(x * cells_y, cells_y)][:, :1]
            out[x, :, where] = (right + left + above + below - 4.0 * here) + scale * here


def residual_of(wavenum, volumes, halos, cells_y):
    cells = volumes[0].shape[0]
    total = halos[0].shape[1]
    return pl.pallas_call(
        functools.partial(residual_kernel, cells_y),
        out_shape=jax.ShapeDtypeStruct((cells // cells_y, cells_y, total), F32),
        in_specs=[VMEM] * (5 + len(volumes)),
        out_specs=VMEM,
        cost_estimate=cost(10 * cells * total, 8 * cells * total),
        compiler_params=PARAMS,
        name="residual",
    )(wavenum, *volumes, *halos)


def per_device(impedance, rebuild_map, left_trace, lower_trace, cell_kind, kind_wavenum):
    z = pltpu.with_memory_space_constraint(impedance[0, 0], pltpu.HBM)
    weights = rebuild_map[0, 0]
    left_all = pltpu.with_memory_space_constraint(left_trace[0, 0], pltpu.HBM)
    lower_all = pltpu.with_memory_space_constraint(lower_trace[0, 0], pltpu.HBM)
    sources = left_all.shape[1]
    width = sources // CHUNKS
    cells_x, cells_y = cell_kind.shape
    left_in, lower_in = [None] * CHUNKS, [None] * CHUNKS
    for step in range(STEPS - 1):
        for c in range(CHUNKS):
            if step == 0 and c == 0:
                right, z_top, left_first, lower_first = first_right(z, left_all, lower_all, 0, width)
                left_in[c] = around(right, "gx")
                upper, z_low = first_upper(z, left_first, lower_first)
            else:
                if step == 0:
                    right, upper = both_loading(z_top, z_low, left_all, lower_all, c * width, width)
                else:
                    right, upper = both(z_top, z_low, left_in[c], lower_in[c])
                left_in[c] = around(right, "gx")
            lower_in[c] = around(upper, "gy")

    kind_ids = jnp.arange(kind_wavenum.shape[0], dtype=jnp.int32)
    wavenum = jnp.sum(
        jnp.where(cell_kind[:, :, None] == kind_ids[None, None, :], kind_wavenum[None, None, :], F32(0.0)),
        axis=-1,
    )
    wavenum = jnp.broadcast_to(wavenum.reshape(cells_x * cells_y, 1), (cells_x * cells_y, 128))

    volume_a = volume_of(weights, left_in[0], lower_in[0])
    outs = last(z_top, z_low, left_in[0], lower_in[0], (), 0, sources)
    volume_a, left_in[1], lower_in[1], *outs = lax.optimization_barrier((volume_a, left_in[1], lower_in[1], *outs))
    volume_b, x_pair, x_cross, y_pair, y_cross = edges_of(weights, left_in[1], lower_in[1], volume_a, cells_y)
    halos = (
        swapped(x_pair, "gx", 0),
        swapped(x_cross, "gx", 1),
        swapped(y_pair, "gy", 0),
        swapped(y_cross, "gy", 1),
    )
    right_out, upper_out = last(z_top, z_low, left_in[1], lower_in[1], outs, width, sources)
    residual = residual_of(wavenum, (volume_a, volume_b), halos, cells_y)
    return (right_out[None, None], upper_out[None, None], residual)


def solution(mesh):
    return jax.shard_map(
        per_device,
        mesh=mesh,
        in_specs=(
            P("gx", "gy", None, None),
            P("gx", "gy", None, None),
            P("gx", "gy", None, None),
            P("gx", "gy", None, None),
            P("gx", "gy"),
            P(),
        ),
        out_specs=(P("gx", "gy", None, None), P("gx", "gy", None, None), P("gx", "gy", None)),
        check_vma=False,
    )
```

time: 60.8 us -> 53.4 us (0.88)
  Pallas kernels: 0 us -> 16.5 us
  matrix products: 8.8 us -> 0 us
  waiting for transfers between devices: 31.1 us -> 25.4 us
  local copies, waits for them, and re-layouts: 5.86 us -> 0.19 us
  starting transfers between devices: 12.2 us -> 10.1 us
  other arithmetic: 1.62 us -> 0.19 us
    pallas_call x0 -> x12, Pallas kernels: none -> 16.5 us  [the longest x4 4.26 us: both(): pl.pallas_call(write_both, out_shape=(out, out), in_specs=[VMEM] * 4, out...]
    dot_general x8 -> x0, matrix products: 8.8 us -> none  [the longest x7 7.06 us: advance(): jnp.dot(mapping, stacked, preferred_element_type=jnp.float32)]
    ppermute x16, waiting for transfers between devices: 31.1 us -> 25.4 us  [the longest x12 23.6 us: around(): lax.ppermute(block, axis, [(i, (i + 1) % count) for i in range(count)])]
    unnamed x10 -> x6, local copies, waits for them, and re-layouts: 3.56 us -> 0.02 us
    ppermute x16, starting transfers between devices: 12.2 us -> 10.1 us  [the longest x12 6.72 us: around(): lax.ppermute(block, axis, [(i, (i + 1) % count) for i in range(count)])]
    squeeze x1 -> x0, local copies, waits for them, and re-layouts: 1.4 us -> none  [per_device(): lower_trace[0, 0, :, c * width:(c + 1) * width]]
    add x1 -> x0, other arithmetic: 1.05 us -> none  [per_device(): residual = beside - 4.0 * volume + wavenum[:, :, None] * volume]
    broadcast_in_dim x1 -> x2, local copies, waits for them, and re-layouts: 0.86 us -> 0.17 us  [per_device(): jnp.broadcast_to(wavenum.reshape(cells_x * cells_y, 1), (cells_x * cells_...]
  transfers between devices with their start and end apart: 16 -> 16, of which waited for: 7 -> 7; matrix products, arithmetic and copies ran while one was open for 18% -> 1% of each run, Pallas kernels for 0% -> 24%
where the time goes in v2:
time: 53.4 us; the launch traced here: 53.1 us
  waiting for transfers between devices  25.4 us (48%)
  Pallas kernels  16.5 us (31%)
  starting transfers between devices  10.1 us (19%)
  between operations  0.81 us (2%)
    ppermute x12, waiting for transfers between devices, around(): lax.ppermute(block, axis, [(i, (i + 1) % count) for i in range(count)])  23.6 us
    ppermute x12, starting transfers between devices, around(): lax.ppermute(block, axis, [(i, (i + 1) % count) for i in range(count)])  6.72 us
    pallas_call x4, Pallas kernels, both(): pl.pallas_call(write_both, out_shape=(out, out), in_specs=[VMEM] * 4, out...  4.26 us
    pallas_call x2, Pallas kernels, last(): pl.pallas_call(functools.partial(last_kernel, base), out_shape=(out, out)...  3.84 us
    ppermute x4, starting transfers between devices, swapped(): return lax.ppermute(block, axis, sorted(pairs))  3.4 us
    pallas_call x1, Pallas kernels, first_right(): pl.pallas_call(functools.partial(first_right_kernel, base, width), out_sh...  2.08 us
    pallas_call x1, Pallas kernels, first_upper(): pl.pallas_call(first_upper_kernel, out_shape=(vmem(trace, width), vmem(tr...  1.9 us
    pallas_call x1, Pallas kernels, both_loading(): pl.pallas_call(functools.partial(both_loading_kernel, base), out_shape=(o...  1.76 us
  transfers between devices with their start and end apart: 16, of which 7 were waited for; matrix products, arithmetic and copies ran while one was open for 1% of the time, Pallas kernels for 24%

profile of v2, /device:TPU:0, one launch (start us, length us, event | category | flops | bytes accessed | tf_op | source)
XLA Modules:
  0.0 53.1 jit_solution(4301840783593759408)
XLA Ops:
  0.6 2.1 %first_right.1 = (bf16[512,256]{1,0:T(8,128)(2,1)S(1)}, bf16[512,1024]{1,0:T(8,128)(2,1)S(1)}, bf16[512,256]{1,0:T(8,128)(2,1)S(1)}, bf16[512,256]{1,0:T(8,128)(2,1)S(1)}) custom-call(bf16[1024,1024]{1,0:T(8,128)(2,1)} %bitcast.8, bf16[512,512]{1,0:T(8,128)(2,1)} %bitcast.10, bf16[512,512]{1,0:T(8,128)(2,1)} %bitcast.12), custom_call_target="tpu_custom_call" | custom-call | flops 268435456 | bytes 786432 | tf_op jit(solution)/shard_map/first_right/pallas_call | solution.py:72
  2.7 3.0 %collective-permute-start = (bf16[512,256]{1,0:T(8,128)(2,1)S(1)}, bf16[512,256]{1,0:T(8,128)(2,1)S(1)}, u32[]{:S(2)}, u32[]{:S(2)}) collective-permute-start(bf16[512,256]{1,0:T(8,128)(2,1)S(1)} %get-tuple-element.37), channel_id=1, source_target_pairs={{0,4},{4,8},{8,12},{12,16},{16,20},{20,24},{24,28},{28,0},{1,5},{5... | collective-permute-start | bytes 786440 | tf_op jit(solution)/shard_map/ppermute | solution.py:20
  5.7 1.9 %first_upper.1 = (bf16[512,256]{1,0:T(8,128)(2,1)S(1)}, bf16[512,1024]{1,0:T(8,128)(2,1)S(1)}) custom-call(bf16[1024,1024]{1,0:T(8,128)(2,1)} %bitcast.9, bf16[512,256]{1,0:T(8,128)(2,1)S(1)} %get-tuple-element.34.left, bf16[512,256]{1,0:T(8,128)(2,1)S(1)} %get-tuple-element.35.lower), custom_call_target="tpu_custom_call" | custom-call | flops 268435456 | bytes 786432 | tf_op jit(solution)/shard_map/first_upper/pallas_call | solution.py:103
  7.6 0.1 collective-permute-start.1
  7.7 1.8 %both_loading.1 = (bf16[512,256]{1,0:T(8,128)(2,1)S(1)}, bf16[512,256]{1,0:T(8,128)(2,1)S(1)}) custom-call(bf16[512,1024]{1,0:T(8,128)(2,1)S(1)} %get-tuple-element.33.z_top, bf16[512,1024]{1,0:T(8,128)(2,1)S(1)} %get-tuple-element.36.z_low, bf16[512,512]{1,0:T(8,128)(2,1)} %bitcast.11, bf16[512,512]{1,0:T(8,128)(2,1)} %bitcast.13), custom_call_target="tpu_custom_call" | custom-call | flops 536870912 | bytes 1048576 | tf_op jit(solution)/shard_map/both_loading/pallas_call | solution.py:140
  9.5 1.6 %collective-permute-start.6 = (bf16[512,256]{1,0:T(8,128)(2,1)S(1)}, bf16[512,256]{1,0:T(8,128)(2,1)S(1)}, u32[]{:S(2)}, u32[]{:S(2)}) collective-permute-start(bf16[512,256]{1,0:T(8,128)(2,1)S(1)} %get-tuple-element.43), channel_id=1, source_target_pairs={{0,4},{4,8},{8,12},{12,16},{16,20},{20,24},{24,28},{28,0},{1,5},{5... | collective-permute-start | bytes 786440 | tf_op jit(solution)/shard_map/ppermute | solution.py:20
  11.1 1.3 %collective-permute-start.7 = (bf16[512,256]{1,0:T(8,128)(2,1)S(1)}, bf16[512,256]{1,0:T(8,128)(2,1)S(1)}, u32[]{:S(2)}, u32[]{:S(2)}) collective-permute-start(bf16[512,256]{1,0:T(8,128)(2,1)S(1)} %get-tuple-element.44), channel_id=1, source_target_pairs={{0,1},{1,2},{2,3},{3,0},{4,5},{5,6},{6,7},{7,4},{8,9},{9,10},{10,1... | collective-permute-start | bytes 786440 | tf_op jit(solution)/shard_map/ppermute | solution.py:20
  12.4 2.7 %collective-permute-done.left = bf16[512,256]{1,0:T(8,128)(2,1)S(1)} collective-permute-done((bf16[512,256]{1,0:T(8,128)(2,1)S(1)}, bf16[512,256]{1,0:T(8,128)(2,1)S(1)}, u32[]{:S(2)}, u32[]{:S(2)}) %collective-permute-start) | collective-permute-done | bytes 262176 | tf_op jit(solution)/shard_map/ppermute | solution.py:20
  15.1 0.0 collective-permute-done.1.lower
  15.1 0.7 %both.4 = (bf16[512,256]{1,0:T(8,128)(2,1)S(1)}, bf16[512,256]{1,0:T(8,128)(2,1)S(1)}) custom-call(bf16[512,1024]{1,0:T(8,128)(2,1)S(1)} %get-tuple-element.33.z_top, bf16[512,1024]{1,0:T(8,128)(2,1)S(1)} %get-tuple-element.36.z_low, bf16[512,256]{1,0:T(8,128)(2,1)S(1)} %collective-permute-done.left, bf16[512,256]{1,0:T(8,128)(2,1)S(1)} %collective-permute-done.1.lower), custom_call_target="tpu_custom_call" | custom-call | flops 536870912 | bytes 1048576 | tf_op jit(solution)/shard_map/both/pallas_call | solution.py:159
  15.8 0.1 collective-permute-start.2
  15.9 0.1 collective-permute-start.3
  15.9 4.8 %collective-permute-done.6.left = bf16[512,256]{1,0:T(8,128)(2,1)S(1)} collective-permute-done((bf16[512,256]{1,0:T(8,128)(2,1)S(1)}, bf16[512,256]{1,0:T(8,128)(2,1)S(1)}, u32[]{:S(2)}, u32[]{:S(2)}) %collective-permute-start.6) | collective-permute-done | bytes 262176 | tf_op jit(solution)/shard_map/ppermute | solution.py:20
  20.8 0.0 collective-permute-done.7.lower
  20.8 0.7 %both.6 = (bf16[512,256]{1,0:T(8,128)(2,1)S(1)}, bf16[512,256]{1,0:T(8,128)(2,1)S(1)}) custom-call(bf16[512,1024]{1,0:T(8,128)(2,1)S(1)} %get-tuple-element.33.z_top, bf16[512,1024]{1,0:T(8,128)(2,1)S(1)} %get-tuple-element.36.z_low, bf16[512,256]{1,0:T(8,128)(2,1)S(1)} %collective-permute-done.6.left, bf16[512,256]{1,0:T(8,128)(2,1)S(1)} %collective-permute-done.7.lower), custom_call_target="tpu_custom_call" | custom-call | flops 536870912 | bytes 1048576 | tf_op jit(solution)/shard_map/both/pallas_call | solution.py:159
  21.5 0.1 collective-permute-start.8
  21.5 0.0 copy-start.1
  21.6 0.0 copy-start.2
  21.6 0.0 copy-start
  21.6 0.5 collective-permute-start.9
  22.1 4.9 %collective-permute-done.2.left = bf16[512,256]{1,0:T(8,128)(2,1)S(1)} collective-permute-done((bf16[512,256]{1,0:T(8,128)(2,1)S(1)}, bf16[512,256]{1,0:T(8,128)(2,1)S(1)}, u32[]{:S(2)}, u32[]{:S(2)}) %collective-permute-start.2) | collective-permute-done | bytes 262176 | tf_op jit(solution)/shard_map/ppermute | solution.py:20
  27.0 0.0 collective-permute-done.3.lower
  27.0 1.4 %both.5 = (bf16[512,256]{1,0:T(8,128)(2,1)}, bf16[512,256]{1,0:T(8,128)(2,1)}) custom-call(bf16[512,1024]{1,0:T(8,128)(2,1)S(1)} %get-tuple-element.33.z_top, bf16[512,1024]{1,0:T(8,128)(2,1)S(1)} %get-tuple-element.36.z_low, bf16[512,256]{1,0:T(8,128)(2,1)S(1)} %collective-permute-done.2.left, bf16[512,256]{1,0:T(8,128)(2,1)S(1)} %collective-permute-done.3.lower), custom_call_target="tpu_custom_call" | custom-call | flops 536870912 | bytes 1048576 | tf_op jit(solution)/shard_map/both/pallas_call | solution.py:159
  28.5 0.0 collective-permute-start.4
  28.5 0.0 collective-permute-start.5
  28.5 4.4 %collective-permute-done.8.left = bf16[512,256]{1,0:T(8,128)(2,1)S(1)} collective-permute-done((bf16[512,256]{1,0:T(8,128)(2,1)S(1)}, bf16[512,256]{1,0:T(8,128)(2,1)S(1)}, u32[]{:S(2)}, u32[]{:S(2)}) %collective-permute-start.8) | collective-permute-done | bytes 262176 | tf_op jit(solution)/shard_map/ppermute | solution.py:20
  32.9 0.0 collective-permute-done.9.lower
  32.9 1.4 %both.7 = (bf16[512,256]{1,0:T(8,128)(2,1)}, bf16[512,256]{1,0:T(8,128)(2,1)}) custom-call(bf16[512,1024]{1,0:T(8,128)(2,1)S(1)} %get-tuple-element.33.z_top, bf16[512,1024]{1,0:T(8,128)(2,1)S(1)} %get-tuple-element.36.z_low, bf16[512,256]{1,0:T(8,128)(2,1)S(1)} %collective-permute-done.8.left, bf16[512,256]{1,0:T(8,128)(2,1)S(1)} %collective-permute-done.9.lower), custom_call_target="tpu_custom_call" | custom-call | flops 536870912 | bytes 1048576 | tf_op jit(solution)/shard_map/both/pallas_call | solution.py:159
  34.3 0.0 collective-permute-start.10
  34.3 0.0 collective-permute-start.11
  34.3 0.0 copy-done.1
  34.3 0.0 copy-done.2
  34.4 0.2 select_reduce_fusion
  34.6 0.1 broadcast_in_dim.32
  34.6 4.4 %collective-permute-done.4.left = bf16[512,256]{1,0:T(8,128)(2,1)S(1)} collective-permute-done((bf16[512,256]{1,0:T(8,128)(2,1)}, bf16[512,256]{1,0:T(8,128)(2,1)S(1)}, u32[]{:S(2)}, u32[]{:S(2)}) %collective-permute-start.4) | collective-permute-done | bytes 262176 | tf_op jit(solution)/shard_map/ppermute | solution.py:20
  39.0 0.0 collective-permute-done.5.lower
  39.0 0.0 copy-done
  39.0 1.3 %volume.1.done.refs_0_ = f32[256,256]{1,0:T(8,128)S(1)} custom-call(bf16[256,1024]{1,0:T(8,128)(2,1)S(1)} %bitcast.6, bf16[512,256]{1,0:T(8,128)(2,1)S(1)} %collective-permute-done.4.left, bf16[512,256]{1,0:T(8,128)(2,1)} %collective-permute-done.5.lower), custom_call_target="tpu_custom_call" | custom-call | flops 134217728 | bytes 262144 | tf_op jit(solution)/shard_map/volume/pallas_call | solution.py:176
  40.2 2.4 %last.2 = (bf16[512,512]{1,0:T(8,128)(2,1)}, bf16[512,512]{1,0:T(8,128)(2,1)}) custom-call(bf16[512,1024]{1,0:T(8,128)(2,1)S(1)} %get-tuple-element.33.z_top, bf16[512,1024]{1,0:T(8,128)(2,1)S(1)} %get-tuple-element.36.z_low, bf16[512,256]{1,0:T(8,128)(2,1)S(1)} %collective-permute-done.4.left, bf16[512,256]{1,0:T(8,128)(2,1)} %collective-permute-done.5.lower), custom_call_target="tpu_custom_call" | custom-call | flops 536870912 | bytes 1048576 | tf_op jit(solution)/shard_map/last/pallas_call | solution.py:246
  42.6 2.4 %collective-permute-done.10.left = bf16[512,256]{1,0:T(8,128)(2,1)S(1)} collective-permute-done((bf16[512,256]{1,0:T(8,128)(2,1)}, bf16[512,256]{1,0:T(8,128)(2,1)S(1)}, u32[]{:S(2)}, u32[]{:S(2)}) %collective-permute-start.10) | collective-permute-done | bytes 262176 | tf_op jit(solution)/shard_map/ppermute | solution.py:20
  45.1 0.0 collective-permute-done.11.lower
  45.1 0.3 edges.1
  45.4 0.1 collective-permute-start.12
  45.5 1.9 %collective-permute-start.13 = (bf16[16,512]{1,0:T(8,128)(2,1)S(1)}, bf16[16,512]{1,0:T(8,128)(2,1)S(1)}, u32[]{:S(2)}, u32[]{:S(2)}) collective-permute-start(bf16[16,512]{1,0:T(8,128)(2,1)S(1)} %get-tuple-element.60), channel_id=1, source_target_pairs={{0,28},{4,8},{8,4},{12,16},{16,12},{20,24},{24,20},{28,0},{1,29},{... | collective-permute-start | bytes 49160 | tf_op jit(solution)/shard_map/ppermute | solution.py:26
  47.4 0.0 collective-permute-start.14
  47.4 1.4 %collective-permute-start.15 = (bf16[16,512]{1,0:T(8,128)(2,1)S(1)}, bf16[16,512]{1,0:T(8,128)(2,1)S(1)}, u32[]{:S(2)}, u32[]{:S(2)}) collective-permute-start(bf16[16,512]{1,0:T(8,128)(2,1)S(1)} %get-tuple-element.62), channel_id=1, source_target_pairs={{0,3},{1,2},{2,1},{3,0},{4,7},{5,6},{6,5},{7,4},{8,11},{9,10},{10,... | collective-permute-start | bytes 49160 | tf_op jit(solution)/shard_map/ppermute | solution.py:26
  48.8 1.4 %last.3 = (bf16[512,512]{1,0:T(8,128)(2,1)}, bf16[512,512]{1,0:T(8,128)(2,1)}) custom-call(bf16[512,1024]{1,0:T(8,128)(2,1)S(1)} %get-tuple-element.33.z_top, bf16[512,1024]{1,0:T(8,128)(2,1)S(1)} %get-tuple-element.36.z_low, bf16[512,256]{1,0:T(8,128)(2,1)S(1)} %collective-permute-done.10.left, ...), custom_call_target="tpu_custom_call", output_to_operand_aliasing={{0}: (4, {}), {1}: (5, {})} | custom-call | flops 536870912 | bytes 1048576 | tf_op jit(solution)/shard_map/last/pallas_call | solution.py:246
  50.3 0.0 collective-permute-done.12.refs_2_
  50.3 1.7 %collective-permute-done.13.refs_3_ = bf16[16,512]{1,0:T(8,128)(2,1)S(1)} collective-permute-done((bf16[16,512]{1,0:T(8,128)(2,1)S(1)}, bf16[16,512]{1,0:T(8,128)(2,1)S(1)}, u32[]{:S(2)}, u32[]{:S(2)}) %collective-permute-start.13) | collective-permute-done | bytes 16416 | tf_op jit(solution)/shard_map/ppermute | solution.py:26
  52.0 0.0 collective-permute-done.14.refs_4_
  52.0 0.0 collective-permute-done.15.refs_5_
  52.0 0.1 broadcast_in_dim.33.wavenum
  52.1 1.1 %residual.1 = f32[16,16,512]{2,1,0:T(8,128)} custom-call(f32[256,128]{1,0:T(8,128)S(1)} %broadcast_in_dim.33.wavenum, f32[256,256]{1,0:T(8,128)S(1)} %volume.1.done.refs_0_, f32[256,256]{1,0:T(8,128)S(1)} %get-tuple-element.58.refs_1_, bf16[16,512]{1,0:T(8,128)(2,1)S(1)} %collective-permute-done.12.refs_2_, ...), custom_call_target="tpu_custom_call" | custom-call | flops 1310720 | bytes 1048576 | tf_op jit(solution)/shard_map/residual/pallas_call | solution.py:297
Async XLA Ops:
  2.7 12.4 %collective-permute-start = (bf16[512,256]{1,0:T(8,128)(2,1)S(1)}, bf16[512,256]{1,0:T(8,128)(2,1)S(1)}, u32[]{:S(2)}, u32[]{:S(2)}) collective-permute-start(bf16[512,256]{1,0:T(8,128)(2,1)S(1)} %get-tuple-element.37), channel_id=1, source_target_pairs={{0,4},{4,8},{8,12},{12,16},{16,20},{20,24},{24,28},{28,0},{1,5},{5... | collective-permute-start | bytes 786440 | tf_op jit(solution)/shard_map/ppermute | solution.py:20
  7.6 7.4 %collective-permute-start.1 = (bf16[512,256]{1,0:T(8,128)(2,1)S(1)}, bf16[512,256]{1,0:T(8,128)(2,1)S(1)}, u32[]{:S(2)}, u32[]{:S(2)}) collective-permute-start(bf16[512,256]{1,0:T(8,128)(2,1)S(1)} %get-tuple-element.38), channel_id=1, source_target_pairs={{0,1},{1,2},{2,3},{3,0},{4,5},{5,6},{6,7},{7,4},{8,9},{9,10},{10,1... | collective-permute-start | bytes 786440 | tf_op jit(solution)/shard_map/ppermute | solution.py:20
  9.5 11.3 %collective-permute-start.6 = (bf16[512,256]{1,0:T(8,128)(2,1)S(1)}, bf16[512,256]{1,0:T(8,128)(2,1)S(1)}, u32[]{:S(2)}, u32[]{:S(2)}) collective-permute-start(bf16[512,256]{1,0:T(8,128)(2,1)S(1)} %get-tuple-element.43), channel_id=1, source_target_pairs={{0,4},{4,8},{8,12},{12,16},{16,20},{20,24},{24,28},{28,0},{1,5},{5... | collective-permute-start | bytes 786440 | tf_op jit(solution)/shard_map/ppermute | solution.py:20
  11.1 9.7 %collective-permute-start.7 = (bf16[512,256]{1,0:T(8,128)(2,1)S(1)}, bf16[512,256]{1,0:T(8,128)(2,1)S(1)}, u32[]{:S(2)}, u32[]{:S(2)}) collective-permute-start(bf16[512,256]{1,0:T(8,128)(2,1)S(1)} %get-tuple-element.44), channel_id=1, source_target_pairs={{0,1},{1,2},{2,3},{3,0},{4,5},{5,6},{6,7},{7,4},{8,9},{9,10},{10,1... | collective-permute-start | bytes 786440 | tf_op jit(solution)/shard_map/ppermute | solution.py:20
  15.8 11.2 %collective-permute-start.2 = (bf16[512,256]{1,0:T(8,128)(2,1)S(1)}, bf16[512,256]{1,0:T(8,128)(2,1)S(1)}, u32[]{:S(2)}, u32[]{:S(2)}) collective-permute-start(bf16[512,256]{1,0:T(8,128)(2,1)S(1)} %get-tuple-element.39), channel_id=1, source_target_pairs={{0,4},{4,8},{8,12},{12,16},{16,20},{20,24},{24,28},{28,0},{1,5},{5... | collective-permute-start | bytes 786440 | tf_op jit(solution)/shard_map/ppermute | solution.py:20
  15.9 11.2 %collective-permute-start.3 = (bf16[512,256]{1,0:T(8,128)(2,1)S(1)}, bf16[512,256]{1,0:T(8,128)(2,1)S(1)}, u32[]{:S(2)}, u32[]{:S(2)}) collective-permute-start(bf16[512,256]{1,0:T(8,128)(2,1)S(1)} %get-tuple-element.40), channel_id=1, source_target_pairs={{0,1},{1,2},{2,3},{3,0},{4,5},{5,6},{6,7},{7,4},{8,9},{9,10},{10,1... | collective-permute-start | bytes 786440 | tf_op jit(solution)/shard_map/ppermute | solution.py:20
  21.5 11.4 %collective-permute-start.8 = (bf16[512,256]{1,0:T(8,128)(2,1)S(1)}, bf16[512,256]{1,0:T(8,128)(2,1)S(1)}, u32[]{:S(2)}, u32[]{:S(2)}) collective-permute-start(bf16[512,256]{1,0:T(8,128)(2,1)S(1)} %get-tuple-element.45), channel_id=1, source_target_pairs={{0,4},{4,8},{8,12},{12,16},{16,20},{20,24},{24,28},{28,0},{1,5},{5... | collective-permute-start | bytes 786440 | tf_op jit(solution)/shard_map/ppermute | solution.py:20
  21.5 12.8 %copy-start.1 = (s32[16,16]{1,0:T(8,128)S(1)}, s32[16,16]{1,0:T(8,128)}, u32[]{:S(2)}) copy-start(s32[16,16]{1,0:T(8,128)} %param.10) | copy-start | bytes 3076
  21.6 12.8 %copy-start.2 = (f32[16]{0:T(128)S(1)}, f32[16]{0:T(128)}, u32[]{:S(2)}) copy-start(f32[16]{0:T(128)} %param.11) | copy-start | bytes 196
  21.6 17.4 %copy-start = (bf16[1,1,256,1024]{3,2,1,0:T(8,128)(2,1)S(1)}, bf16[1,1,256,1024]{3,2,1,0:T(8,128)(2,1)}, u32[]{:S(2)}) copy-start(bf16[1,1,256,1024]{3,2,1,0:T(8,128)(2,1)} %param.7) | copy-start | bytes 1572868
  21.6 11.3 %collective-permute-start.9 = (bf16[512,256]{1,0:T(8,128)(2,1)S(1)}, bf16[512,256]{1,0:T(8,128)(2,1)S(1)}, u32[]{:S(2)}, u32[]{:S(2)}) collective-permute-start(bf16[512,256]{1,0:T(8,128)(2,1)S(1)} %get-tuple-element.46), channel_id=1, source_target_pairs={{0,1},{1,2},{2,3},{3,0},{4,5},{5,6},{6,7},{7,4},{8,9},{9,10},{10,1... | collective-permute-start | bytes 786440 | tf_op jit(solution)/shard_map/ppermute | solution.py:20
  28.5 10.5 %collective-permute-start.4 = (bf16[512,256]{1,0:T(8,128)(2,1)}, bf16[512,256]{1,0:T(8,128)(2,1)S(1)}, u32[]{:S(2)}, u32[]{:S(2)}) collective-permute-start(bf16[512,256]{1,0:T(8,128)(2,1)} %get-tuple-element.41), channel_id=1, source_target_pairs={{0,4},{4,8},{8,12},{12,16},{16,20},{20,24},{24,28},{28,0},{1,5},{5... | collective-permute-start | bytes 786440 | tf_op jit(solution)/shard_map/ppermute | solution.py:20
  28.5 10.5 %collective-permute-start.5 = (bf16[512,256]{1,0:T(8,128)(2,1)}, bf16[512,256]{1,0:T(8,128)(2,1)}, u32[]{:S(2)}, u32[]{:S(2)}) collective-permute-start(bf16[512,256]{1,0:T(8,128)(2,1)} %get-tuple-element.42), channel_id=1, source_target_pairs={{0,1},{1,2},{2,3},{3,0},{4,5},{5,6},{6,7},{7,4},{8,9},{9,10},{10,1... | collective-permute-start | bytes 786440 | tf_op jit(solution)/shard_map/ppermute | solution.py:20
  34.3 10.7 %collective-permute-start.10 = (bf16[512,256]{1,0:T(8,128)(2,1)}, bf16[512,256]{1,0:T(8,128)(2,1)S(1)}, u32[]{:S(2)}, u32[]{:S(2)}) collective-permute-start(bf16[512,256]{1,0:T(8,128)(2,1)} %get-tuple-element.47), channel_id=1, source_target_pairs={{0,4},{4,8},{8,12},{12,16},{16,20},{20,24},{24,28},{28,0},{1,5},{5... | collective-permute-start | bytes 786440 | tf_op jit(solution)/shard_map/ppermute | solution.py:20
  34.3 10.7 %collective-permute-start.11 = (bf16[512,256]{1,0:T(8,128)(2,1)}, bf16[512,256]{1,0:T(8,128)(2,1)S(1)}, u32[]{:S(2)}, u32[]{:S(2)}) collective-permute-start(bf16[512,256]{1,0:T(8,128)(2,1)} %get-tuple-element.48), channel_id=1, source_target_pairs={{0,1},{1,2},{2,3},{3,0},{4,5},{5,6},{6,7},{7,4},{8,9},{9,10},{10,1... | collective-permute-start | bytes 786440 | tf_op jit(solution)/shard_map/ppermute | solution.py:20
  45.4 4.9 %collective-permute-start.12 = (bf16[16,512]{1,0:T(8,128)(2,1)S(1)}, bf16[16,512]{1,0:T(8,128)(2,1)S(1)}, u32[]{:S(2)}, u32[]{:S(2)}) collective-permute-start(bf16[16,512]{1,0:T(8,128)(2,1)S(1)} %get-tuple-element.59), channel_id=1, source_target_pairs={{0,4},{4,0},{8,12},{12,8},{16,20},{20,16},{24,28},{28,24},{1,5},{5... | collective-permute-start | bytes 49160 | tf_op jit(solution)/shard_map/ppermute | solution.py:26
  45.5 6.5 %collective-permute-start.13 = (bf16[16,512]{1,0:T(8,128)(2,1)S(1)}, bf16[16,512]{1,0:T(8,128)(2,1)S(1)}, u32[]{:S(2)}, u32[]{:S(2)}) collective-permute-start(bf16[16,512]{1,0:T(8,128)(2,1)S(1)} %get-tuple-element.60), channel_id=1, source_target_pairs={{0,28},{4,8},{8,4},{12,16},{16,12},{20,24},{24,20},{28,0},{1,29},{... | collective-permute-start | bytes 49160 | tf_op jit(solution)/shard_map/ppermute | solution.py:26
  47.4 4.6 %collective-permute-start.14 = (bf16[16,512]{1,0:T(8,128)(2,1)S(1)}, bf16[16,512]{1,0:T(8,128)(2,1)S(1)}, u32[]{:S(2)}, u32[]{:S(2)}) collective-permute-start(bf16[16,512]{1,0:T(8,128)(2,1)S(1)} %get-tuple-element.61), channel_id=1, source_target_pairs={{0,1},{1,0},{2,3},{3,2},{4,5},{5,4},{6,7},{7,6},{8,9},{9,8},{10,11... | collective-permute-start | bytes 49160 | tf_op jit(solution)/shard_map/ppermute | solution.py:26
  47.4 4.6 %collective-permute-start.15 = (bf16[16,512]{1,0:T(8,128)(2,1)S(1)}, bf16[16,512]{1,0:T(8,128)(2,1)S(1)}, u32[]{:S(2)}, u32[]{:S(2)}) collective-permute-start(bf16[16,512]{1,0:T(8,128)(2,1)S(1)} %get-tuple-element.62), channel_id=1, source_target_pairs={{0,3},{1,2},{2,1},{3,0},{4,7},{5,6},{6,5},{7,4},{8,11},{9,10},{10,... | collective-permute-start | bytes 49160 | tf_op jit(solution)/shard_map/ppermute | solution.py:26

commit v3 on v2

--- a/solution.py
+++ b/solution.py
@@ -21,9 +21,19 @@
 
 
 def swapped(block, axis, first):
-    count = lax.axis_size(axis)
-    pairs = [((first + i) % count, (first + (i ^ 1)) % count) for i in range(count)]
-    return lax.ppermute(block, axis, sorted(pairs))
+    names = ("gx", "gy")
+    along = names.index(axis)
+    sizes = tuple(lax.axis_size(name) for name in names)
+    pairs = []
+    for place in range(sizes[0] * sizes[1]):
+        where = [place // sizes[1], place % sizes[1]]
+        mate = first + ((where[along] - first) ^ 1)
+        if 0 <= mate < sizes[along]:
+            where[along] = mate
+        else:
+            where[1 - along] ^= 1
+        pairs.append((place, where[0] * sizes[1] + where[1]))
+    return lax.ppermute(block, names, pairs)
 
 
 def is_last(axis):
@@ -34,7 +44,7 @@
 
 
 def cost(flops, moved):
-    return pl.CostEstimate(flops=flops, bytes_accessed=moved, transcendentals=0)
+    return pl.CostEstimate(flops=int(flops), bytes_accessed=int(moved), transcendentals=0)
 
 
 def product(weights, left, lower):
@@ -75,7 +85,7 @@
         in_specs=[HBM, HBM, HBM],
         out_specs=(VMEM,) * 4,
         scratch_shapes=[pltpu.SemaphoreType.DMA((4,))],
-        cost_estimate=cost(4 * trace * trace * width, 3 * trace * trace),
+        cost_estimate=cost(4 * trace * trace * width, 4 * trace * trace + 6 * trace * width),
         compiler_params=PARAMS,
         name="first_right",
     )(z, left, lower)
@@ -106,22 +116,34 @@
         in_specs=[HBM, VMEM, VMEM],
         out_specs=(VMEM,) * 2,
         scratch_shapes=[pltpu.SemaphoreType.DMA((2,))],
-        cost_estimate=cost(4 * trace * trace * width, 3 * trace * trace),
+        cost_estimate=cost(4 * trace * trace * width, 4 * trace * trace + 6 * trace * width),
         compiler_params=PARAMS,
         name="first_upper",
     )(z, left, lower)
 
 
-def write_both(z_top, z_low, left, lower, right, upper):
+def part_kernel(axis, z, left, lower, out):
     half = left.shape[0] // 2
-    for axis, z, out in (("gx", z_top, right), ("gy", z_low, upper)):
-        at_end = is_last(axis)
-        for r in range(2):
-            here = pl.ds(r * half, half)
-            out[here] = jnp.where(at_end, 0.0, product(z.at[here], left, lower)).astype(BF16)
-
-
-def both_loading_kernel(base, z_top, z_low, left_hbm, lower_hbm, right, upper, left, lower, sem):
+    at_end = is_last(axis)
+    for r in range(2):
+        here = pl.ds(r * half, half)
+        out[here] = jnp.where(at_end, 0.0, product(z.at[here], left, lower)).astype(BF16)
+
+
+def part(axis, z, left, lower):
+    trace, width = left.shape
+    return pl.pallas_call(
+        functools.partial(part_kernel, axis),
+        out_shape=jax.ShapeDtypeStruct((trace, width), BF16),
+        in_specs=[VMEM] * 3,
+        out_specs=VMEM,
+        cost_estimate=cost(4 * trace * trace * width, 4 * trace * trace + 6 * trace * width),
+        compiler_params=PARAMS,
+        name="part",
+    )(z, left, lower)
+
+
+def part_loading_kernel(axis, base, z, left_hbm, lower_hbm, out, left, lower, sem):
     width = left.shape[1]
     loads = [
         pltpu.make_async_copy(left_hbm.at[:, pl.ds(base, width)], left, sem.at[0]),
@@ -131,40 +153,46 @@
         copy.start()
     for copy in loads:
         copy.wait()
-    write_both(z_top, z_low, left, lower, right, upper)
-
-
-def both_loading(z_top, z_low, left, lower, base, width):
+    part_kernel(axis, z, left, lower, out)
+
+
+def part_loading(axis, z, left, lower, base, width):
     trace = left.shape[0]
-    out = jax.ShapeDtypeStruct((trace, width), BF16)
-    return pl.pallas_call(
-        functools.partial(both_loading_kernel, base),
-        out_shape=(out, out),
-        in_specs=[VMEM, VMEM, HBM, HBM],
-        out_specs=(VMEM, VMEM),
-        scratch_shapes=[
-            pltpu.VMEM((trace, width), BF16),
-            pltpu.VMEM((trace, width), BF16),
-            pltpu.SemaphoreType.DMA((2,)),
-        ],
-        cost_estimate=cost(8 * trace * trace * width, 4 * trace * trace),
-        compiler_params=PARAMS,
-        name="both_loading",
-    )(z_top, z_low, left, lower)
-
-
-def both(z_top, z_low, left, lower):
-    trace, width = left.shape
-    out = jax.ShapeDtypeStruct((trace, width), BF16)
-    return pl.pallas_call(
-        write_both,
-        out_shape=(out, out),
-        in_specs=[VMEM] * 4,
-        out_specs=(VMEM, VMEM),
-        cost_estimate=cost(8 * trace * trace * width, 4 * trace * trace),
-        compiler_params=PARAMS,
-        name="both",
-    )(z_top, z_low, left, lower)
+    block = jax.ShapeDtypeStruct((trace, width), BF16)
+    return pl.pallas_call(
+        functools.partial(part_loading_kernel, axis, base),
+        out_shape=(block,) * 3,
+        in_specs=[VMEM, HBM, HBM],
+        out_specs=(VMEM,) * 3,
+        scratch_shapes=[pltpu.SemaphoreType.DMA((2,))],
+        cost_estimate=cost(4 * trace * trace * width, 4 * trace * trace + 6 * trace * width),
+        compiler_params=PARAMS,
+        name="part_loading",
+    )(z, left, lower)
+
+
+def wavenum_kernel(table, kinds, out):
+    cells_x, cells_y = kinds.shape
+    kind = kinds[...]
+    value = jnp.zeros(kind.shape, F32)
+    for k in range(table.shape[0]):
+        value = jnp.where(kind == k, table[k], value)
+    shape = (cells_y, cells_y)
+    diagonal = lax.broadcasted_iota(jnp.int32, shape, 0) == lax.broadcasted_iota(jnp.int32, shape, 1)
+    for x in range(cells_x):
+        column = jnp.sum(jnp.where(diagonal, value[x : x + 1], 0.0), axis=1, keepdims=True)
+        out[pl.ds(x * cells_y, cells_y)] = jnp.broadcast_to(column, (cells_y, out.shape[1]))
+
+
+def wavenum_of(table, kinds):
+    return pl.pallas_call(
+        wavenum_kernel,
+        out_shape=jax.ShapeDtypeStruct((kinds.size, 128), F32),
+        in_specs=[pl.BlockSpec(memory_space=pltpu.SMEM), VMEM],
+        out_specs=VMEM,
+        compiler_params=PARAMS,
+        name="wavenum",
+    )(table, kinds)
 
 
 def volume_kernel(weights, left, lower, volume):
@@ -178,7 +206,7 @@
         out_shape=jax.ShapeDtypeStruct((weights.shape[0], width), F32),
         in_specs=[VMEM] * 3,
         out_specs=VMEM,
-        cost_estimate=cost(2 * weights.size * width, weights.size),
+        cost_estimate=cost(2 * weights.size * width, 2 * weights.size + 4 * weights.shape[1] * width),
         compiler_params=PARAMS,
         name="volume",
     )(weights, left, lower)
@@ -217,14 +245,13 @@
         ),
         in_specs=[VMEM] * 4,
         out_specs=(VMEM,) * 5,
-        cost_estimate=cost(2 * weights.size * width, weights.size),
+        cost_estimate=cost(2 * weights.size * width, 2 * weights.size + 4 * weights.shape[1] * width),
         compiler_params=PARAMS,
         name="edges",
     )(weights, left, lower, done)
 
 
-def last_kernel(base, z_top, z_low, left, lower, *refs):
-    right_hbm, upper_hbm, right, upper, sem = refs[-5:]
+def last_kernel(z_top, z_low, left, lower, right_hbm, upper_hbm, right, upper, sem):
     width = left.shape[1]
     half = left.shape[0] // 2
     copies = []
@@ -233,31 +260,52 @@
             here = pl.ds(r * half, half)
             out[here] = product(z.at[here], left, lower).astype(BF16)
             copies.append(
-                pltpu.make_async_copy(out.at[here], out_hbm.at[here, pl.ds(base, width)], sem.at[len(copies)])
+                pltpu.make_async_copy(out.at[here], out_hbm.at[here, pl.ds(0, width)], sem.at[len(copies)])
             )
             copies[-1].start()
     for copy in copies:
         copy.wait()
 
 
-def last(z_top, z_low, left, lower, before, base, total):
+def last(z_top, z_low, left, lower, total):
     trace, width = left.shape
     out = jax.ShapeDtypeStruct((trace, total), BF16)
     return pl.pallas_call(
-        functools.partial(last_kernel, base),
+        last_kernel,
         out_shape=(out, out),
-        in_specs=[VMEM] * 4 + [HBM] * len(before),
+        in_specs=[VMEM] * 4,
         out_specs=(HBM, HBM),
         scratch_shapes=[
             pltpu.VMEM((trace, width), BF16),
             pltpu.VMEM((trace, width), BF16),
             pltpu.SemaphoreType.DMA((4,)),
         ],
-        input_output_aliases={4 + k: k for k in range(len(before))},
-        cost_estimate=cost(8 * trace * trace * width, 4 * trace * trace),
+        cost_estimate=cost(8 * trace * trace * width, 8 * trace * trace + 8 * trace * width),
         compiler_params=PARAMS,
         name="last",
-    )(z_top, z_low, left, lower, *before)
+    )(z_top, z_low, left, lower)
+
+
+def plain_kernel(z_top, z_low, left, lower, right, upper):
+    half = left.shape[0] // 2
+    for z, out in ((z_top, right), (z_low, upper)):
+        for r in range(2):
+            here = pl.ds(r * half, half)
+            out[here] = product(z.at[here], left, lower).astype(BF16)
+
+
+def plain(z_top, z_low, left, lower):
+    trace, width = left.shape
+    out = jax.ShapeDtypeStruct((trace, width), BF16)
+    return pl.pallas_call(
+        plain_kernel,
+        out_shape=(out, out),
+        in_specs=[VMEM] * 4,
+        out_specs=(VMEM, VMEM),
+        cost_estimate=cost(8 * trace * trace * width, 8 * trace * trace + 8 * trace * width),
+        compiler_params=PARAMS,
+        name="plain",
+    )(z_top, z_low, left, lower)
 
 
 def beside(axis, pair, cross):
@@ -269,9 +317,17 @@
     return before, after
 
 
-def residual_kernel(cells_y, wavenum, *refs):
-    volumes = refs[:-5]
-    x_pair, x_cross, y_pair, y_cross, out = refs[-5:]
+def finish_kernel(cells_y, *refs):
+    wavenum, right, upper, x_pair, x_cross, y_pair, y_cross = refs[:7]
+    right_hbm, upper_hbm, residual_hbm, out, sem = refs[-5:]
+    volumes = refs[7:-7]
+    base = right_hbm.shape[1] - right.shape[1]
+    copies = [
+        pltpu.make_async_copy(right, right_hbm.at[:, pl.ds(base, right.shape[1])], sem.at[0]),
+        pltpu.make_async_copy(upper, upper_hbm.at[:, pl.ds(base, upper.shape[1])], sem.at[1]),
+    ]
+    for copy in copies:
+        copy.start()
     cells = volumes[0].shape[0]
     start = 0
     for volume in volumes:
@@ -284,25 +340,35 @@
         for x in range(cells // cells_y):
             here = volume[pl.ds(x * cells_y, cells_y)]
             left = volume[pl.ds((x - 1) * cells_y, cells_y)] if x else before_x
-            right = volume[pl.ds((x + 1) * cells_y, cells_y)] if (x + 1) * cells_y < cells else after_x
+            after = volume[pl.ds((x + 1) * cells_y, cells_y)] if (x + 1) * cells_y < cells else after_x
             below = jnp.where(place == 0, before_y[x : x + 1], pltpu.roll(here, 1, 0))
             above = jnp.where(place == cells_y - 1, after_y[x : x + 1], pltpu.roll(here, cells_y - 1, 0))
             scale = wavenum[pl.ds(x * cells_y, cells_y)][:, :1]
-            out[x, :, where] = (right + left + above + below - 4.0 * here) + scale * here
-
-
-def residual_of(wavenum, volumes, halos, cells_y):
+            out[x, :, where] = (after + left + above + below - 4.0 * here) + scale * here
+        copies.append(
+            pltpu.make_async_copy(out.at[:, :, where], residual_hbm.at[:, :, where], sem.at[len(copies)])
+        )
+        copies[-1].start()
+    for copy in copies:
+        copy.wait()
+
+
+def finish(wavenum, right, upper, halos, volumes, outs, cells_y):
     cells = volumes[0].shape[0]
-    total = halos[0].shape[1]
-    return pl.pallas_call(
-        functools.partial(residual_kernel, cells_y),
-        out_shape=jax.ShapeDtypeStruct((cells // cells_y, cells_y, total), F32),
-        in_specs=[VMEM] * (5 + len(volumes)),
-        out_specs=VMEM,
+    total = outs[0].shape[1]
+    whole = (cells // cells_y, cells_y, total)
+    given = 3 + len(halos) + len(volumes)
+    return pl.pallas_call(
+        functools.partial(finish_kernel, cells_y),
+        out_shape=tuple(jax.ShapeDtypeStruct(o.shape, o.dtype) for o in outs) + (jax.ShapeDtypeStruct(whole, F32),),
+        in_specs=[VMEM] * given + [HBM] * 2,
+        out_specs=(HBM,) * 3,
+        scratch_shapes=[pltpu.VMEM(whole, F32), pltpu.SemaphoreType.DMA((2 + len(volumes),))],
+        input_output_aliases={given: 0, given + 1: 1},
         cost_estimate=cost(10 * cells * total, 8 * cells * total),
         compiler_params=PARAMS,
-        name="residual",
-    )(wavenum, *volumes, *halos)
+        name="finish",
+    )(wavenum, right, upper, *halos, *volumes, *outs)
 
 
 def per_device(impedance, rebuild_map, left_trace, lower_trace, cell_kind, kind_wavenum):
@@ -317,36 +383,35 @@
     for step in range(STEPS - 1):
         for c in range(CHUNKS):
             if step == 0 and c == 0:
-                right, z_top, left_first, lower_first = first_right(z, left_all, lower_all, 0, width)
-                left_in[c] = around(right, "gx")
-                upper, z_low = first_upper(z, left_first, lower_first)
+                right, z_top, left, lower = first_right(z, left_all, lower_all, 0, width)
+            elif step == 0:
+                right, left, lower = part_loading("gx", z_top, left_all, lower_all, c * width, width)
             else:
-                if step == 0:
-                    right, upper = both_loading(z_top, z_low, left_all, lower_all, c * width, width)
-                else:
-                    right, upper = both(z_top, z_low, left_in[c], lower_in[c])
-                left_in[c] = around(right, "gx")
+                left, lower = left_in[c], lower_in[c]
+                right = part("gx", z_top, left, lower)
+            left_in[c] = around(right, "gx")
+            if step == 0 and c == 0:
+                upper, z_low = first_upper(z, left, lower)
+            else:
+                upper = part("gy", z_low, left, lower)
             lower_in[c] = around(upper, "gy")
 
-    kind_ids = jnp.arange(kind_wavenum.shape[0], dtype=jnp.int32)
-    wavenum = jnp.sum(
-        jnp.where(cell_kind[:, :, None] == kind_ids[None, None, :], kind_wavenum[None, None, :], F32(0.0)),
-        axis=-1,
+    wavenum = wavenum_of(kind_wavenum, cell_kind)
+    volume_a = volume_of(weights, left_in[0], lower_in[0])
+    outs = last(z_top, z_low, left_in[0], lower_in[0], sources)
+    volume_a, wavenum, left_in[1], lower_in[1], *outs = lax.optimization_barrier(
+        (volume_a, wavenum, left_in[1], lower_in[1], *outs)
     )
-    wavenum = jnp.broadcast_to(wavenum.reshape(cells_x * cells_y, 1), (cells_x * cells_y, 128))
-
-    volume_a = volume_of(weights, left_in[0], lower_in[0])
-    outs = last(z_top, z_low, left_in[0], lower_in[0], (), 0, sources)
-    volume_a, left_in[1], lower_in[1], *outs = lax.optimization_barrier((volume_a, left_in[1], lower_in[1], *outs))
     volume_b, x_pair, x_cross, y_pair, y_cross = edges_of(weights, left_in[1], lower_in[1], volume_a, cells_y)
-    halos = (
-        swapped(x_pair, "gx", 0),
-        swapped(x_cross, "gx", 1),
-        swapped(y_pair, "gy", 0),
-        swapped(y_cross, "gy", 1),
+    x_cross = swapped(x_cross, "gx", 1)
+    x_pair = swapped(x_pair, "gx", 0)
+    y_cross = swapped(y_cross, "gy", 1)
+    y_pair = swapped(y_pair, "gy", 0)
+    halos = (x_pair, x_cross, y_pair, y_cross)
+    right, upper = plain(z_top, z_low, left_in[1], lower_in[1])
+    right_out, upper_out, residual = finish(
+        wavenum, right, upper, halos, (volume_a, volume_b), outs, cells_y
     )
-    right_out, upper_out = last(z_top, z_low, left_in[1], lower_in[1], outs, width, sources)
-    residual = residual_of(wavenum, (volume_a, volume_b), halos, cells_y)
     return (right_out[None, None], upper_out[None, None], residual)
 
 

time: 53.4 us -> 49.7 us (0.931)
  Pallas kernels: 16.5 us -> 13.8 us
  starting transfers between devices: 10.1 us -> 9.07 us
    pallas_call x8 -> x14, Pallas kernels: 10.9 us -> 9.23 us  [the longest x9 3.92 us: part(): pl.pallas_call(functools.partial(part_kernel, axis), out_shape=jax.ShapeD...]
    ppermute x4, starting transfers between devices: 3.4 us -> 2.08 us  [swapped(): return lax.ppermute(block, names, pairs)]
    pallas_call x1, Pallas kernels: 1.25 us -> 0.3 us  [volume_of(): pl.pallas_call(volume_kernel, out_shape=jax.ShapeDtypeStruct((weights.sha...]
  transfers between devices with their start and end apart: 16 -> 16, of which waited for: 7 -> 8; matrix products, arithmetic and copies ran while one was open for 1% -> 0% of each run, Pallas kernels for 24% -> 21%
where the time goes in v3:
time: 49.7 us; the launch traced here: 49.4 us
  waiting for transfers between devices  25.5 us (51%)
  Pallas kernels  13.8 us (28%)
  starting transfers between devices  9.07 us (18%)
  between operations  0.89 us (2%)
    ppermute x12, waiting for transfers between devices, around(): lax.ppermute(block, axis, [(i, (i + 1) % count) for i in range(count)])  24 us
    ppermute x12, starting transfers between devices, around(): lax.ppermute(block, axis, [(i, (i + 1) % count) for i in range(count)])  6.99 us
    pallas_call x9, Pallas kernels, part(): pl.pallas_call(functools.partial(part_kernel, axis), out_shape=jax.ShapeD...  3.92 us
    ppermute x4, starting transfers between devices, swapped(): return lax.ppermute(block, names, pairs)  2.08 us
    pallas_call x1, Pallas kernels, first_right(): pl.pallas_call(functools.partial(first_right_kernel, base, width), out_sh...  2.08 us
    pallas_call x1, Pallas kernels, first_upper(): pl.pallas_call(first_upper_kernel, out_shape=(vmem(trace, width), vmem(tr...  1.9 us
    ppermute x4, waiting for transfers between devices, swapped(): return lax.ppermute(block, names, pairs)  1.58 us
    pallas_call x1, Pallas kernels, part_loading(): pl.pallas_call(functools.partial(part_loading_kernel, axis, base), out_sh...  1.49 us
  transfers between devices with their start and end apart: 16, of which 8 were waited for; matrix products, arithmetic and copies ran while one was open for 0% of the time, Pallas kernels for 21%

profile of v3, /device:TPU:0, one launch (start us, length us, event | category | flops | bytes accessed | tf_op | source)
XLA Modules:
  0.0 49.4 jit_solution(10274960273963607798)
XLA Ops:
  0.6 2.1 %first_right.1 = (bf16[512,256]{1,0:T(8,128)(2,1)S(1)}, bf16[512,1024]{1,0:T(8,128)(2,1)S(1)}, bf16[512,256]{1,0:T(8,128)(2,1)S(1)}, bf16[512,256]{1,0:T(8,128)(2,1)S(1)}) custom-call(bf16[1024,1024]{1,0:T(8,128)(2,1)} %bitcast.8, bf16[512,512]{1,0:T(8,128)(2,1)} %bitcast.10, bf16[512,512]{1,0:T(8,128)(2,1)} %bitcast.12), custom_call_target="tpu_custom_call" | custom-call | flops 268435456 | bytes 1835008 | tf_op jit(solution)/shard_map/first_right/pallas_call | solution.py:82
  2.7 3.0 %collective-permute-start = (bf16[512,256]{1,0:T(8,128)(2,1)S(1)}, bf16[512,256]{1,0:T(8,128)(2,1)S(1)}, u32[]{:S(2)}, u32[]{:S(2)}) collective-permute-start(bf16[512,256]{1,0:T(8,128)(2,1)S(1)} %get-tuple-element.31), channel_id=1, source_target_pairs={{0,4},{4,8},{8,12},{12,16},{16,20},{20,24},{24,28},{28,0},{1,5},{5... | collective-permute-start | bytes 786440 | tf_op jit(solution)/shard_map/ppermute | solution.py:20
  5.7 1.9 %first_upper.1 = (bf16[512,256]{1,0:T(8,128)(2,1)S(1)}, bf16[512,1024]{1,0:T(8,128)(2,1)S(1)}) custom-call(bf16[1024,1024]{1,0:T(8,128)(2,1)} %bitcast.9, bf16[512,256]{1,0:T(8,128)(2,1)S(1)} %get-tuple-element.32.left, bf16[512,256]{1,0:T(8,128)(2,1)S(1)} %get-tuple-element.33.lower), custom_call_target="tpu_custom_call" | custom-call | flops 268435456 | bytes 1835008 | tf_op jit(solution)/shard_map/first_upper/pallas_call | solution.py:113
  7.6 0.1 collective-permute-start.1
  7.7 1.5 %part_loading.1 = (bf16[512,256]{1,0:T(8,128)(2,1)S(1)}, bf16[512,256]{1,0:T(8,128)(2,1)S(1)}, bf16[512,256]{1,0:T(8,128)(2,1)S(1)}) custom-call(bf16[512,1024]{1,0:T(8,128)(2,1)S(1)} %get-tuple-element.30.z.z_top, bf16[512,512]{1,0:T(8,128)(2,1)} %bitcast.11, bf16[512,512]{1,0:T(8,128)(2,1)} %bitcast.13), custom_call_target="tpu_custom_call" | custom-call | flops 268435456 | bytes 1835008 | tf_op jit(solution)/shard_map/part_loading/pallas_call | solution.py:162
  9.2 1.6 %collective-permute-start.6 = (bf16[512,256]{1,0:T(8,128)(2,1)S(1)}, bf16[512,256]{1,0:T(8,128)(2,1)S(1)}, u32[]{:S(2)}, u32[]{:S(2)}) collective-permute-start(bf16[512,256]{1,0:T(8,128)(2,1)S(1)} %get-tuple-element.36), channel_id=1, source_target_pairs={{0,4},{4,8},{8,12},{12,16},{16,20},{20,24},{24,28},{28,0},{1,5},{5... | collective-permute-start | bytes 786440 | tf_op jit(solution)/shard_map/ppermute | solution.py:20
  10.8 0.4 part.13
  11.3 1.4 %collective-permute-start.7 = (bf16[512,256]{1,0:T(8,128)(2,1)S(1)}, bf16[512,256]{1,0:T(8,128)(2,1)S(1)}, u32[]{:S(2)}, u32[]{:S(2)}) collective-permute-start(bf16[512,256]{1,0:T(8,128)(2,1)S(1)} %part.13), channel_id=1, source_target_pairs={{0,1},{1,2},{2,3},{3,0},{4,5},{5,6},{6,7},{7,4},{8,9},{9,10},{10,1... | collective-permute-start | bytes 786440 | tf_op jit(solution)/shard_map/ppermute | solution.py:20
  12.6 2.4 %collective-permute-done.left = bf16[512,256]{1,0:T(8,128)(2,1)S(1)} collective-permute-done((bf16[512,256]{1,0:T(8,128)(2,1)S(1)}, bf16[512,256]{1,0:T(8,128)(2,1)S(1)}, u32[]{:S(2)}, u32[]{:S(2)}) %collective-permute-start) | collective-permute-done | bytes 262176 | tf_op jit(solution)/shard_map/ppermute | solution.py:20
  15.1 0.0 collective-permute-done.1.lower
  15.1 0.4 part.9
  15.5 0.1 collective-permute-start.2
  15.6 0.4 part.10
  16.0 0.1 collective-permute-start.3
  16.1 4.4 %collective-permute-done.6.left = bf16[512,256]{1,0:T(8,128)(2,1)S(1)} collective-permute-done((bf16[512,256]{1,0:T(8,128)(2,1)S(1)}, bf16[512,256]{1,0:T(8,128)(2,1)S(1)}, u32[]{:S(2)}, u32[]{:S(2)}) %collective-permute-start.6) | collective-permute-done | bytes 262176 | tf_op jit(solution)/shard_map/ppermute | solution.py:20
  20.5 0.0 collective-permute-done.7.lower
  20.5 0.4 part.14
  20.9 0.1 collective-permute-start.8
  21.0 0.4 part.15
  21.4 0.5 %collective-permute-start.9 = (bf16[512,256]{1,0:T(8,128)(2,1)S(1)}, bf16[512,256]{1,0:T(8,128)(2,1)S(1)}, u32[]{:S(2)}, u32[]{:S(2)}) collective-permute-start(bf16[512,256]{1,0:T(8,128)(2,1)S(1)} %part.15), channel_id=1, source_target_pairs={{0,1},{1,2},{2,3},{3,0},{4,5},{5,6},{6,7},{7,4},{8,9},{9,10},{10,1... | collective-permute-start | bytes 786440 | tf_op jit(solution)/shard_map/ppermute | solution.py:20
  22.0 4.8 %collective-permute-done.2.left = bf16[512,256]{1,0:T(8,128)(2,1)S(1)} collective-permute-done((bf16[512,256]{1,0:T(8,128)(2,1)S(1)}, bf16[512,256]{1,0:T(8,128)(2,1)S(1)}, u32[]{:S(2)}, u32[]{:S(2)}) %collective-permute-start.2) | collective-permute-done | bytes 262176 | tf_op jit(solution)/shard_map/ppermute | solution.py:20
  26.8 0.0 collective-permute-done.3.lower
  26.8 0.4 part.11
  27.2 0.1 collective-permute-start.4
  27.3 0.4 part.12
  27.7 0.0 copy-start.1
  27.7 0.0 copy-start.2
  27.7 0.0 copy-start
  27.8 0.1 collective-permute-start.5
  27.8 5.0 %collective-permute-done.8.left = bf16[512,256]{1,0:T(8,128)(2,1)S(1)} collective-permute-done((bf16[512,256]{1,0:T(8,128)(2,1)S(1)}, bf16[512,256]{1,0:T(8,128)(2,1)S(1)}, u32[]{:S(2)}, u32[]{:S(2)}) %collective-permute-start.8) | collective-permute-done | bytes 262176 | tf_op jit(solution)/shard_map/ppermute | solution.py:20
  32.8 0.0 collective-permute-done.9.lower
  32.8 0.4 part.16
  33.2 0.1 collective-permute-start.10
  33.3 0.4 part.17
  33.7 0.1 collective-permute-start.11
  33.8 0.0 copy-done.1
  33.8 0.0 copy-done.2
  33.8 0.7 %wavenum.1.refs_0_ = f32[256,128]{1,0:T(8,128)S(1)} custom-call(f32[16]{0:T(128)S(1)} %copy-done.2, s32[16,16]{1,0:T(8,128)S(1)} %copy-done.1), custom_call_target="tpu_custom_call" | custom-call | tf_op jit(solution)/shard_map/wavenum/pallas_call | solution.py:188
  34.5 3.7 %collective-permute-done.4.left = bf16[512,256]{1,0:T(8,128)(2,1)S(1)} collective-permute-done((bf16[512,256]{1,0:T(8,128)(2,1)S(1)}, bf16[512,256]{1,0:T(8,128)(2,1)S(1)}, u32[]{:S(2)}, u32[]{:S(2)}) %collective-permute-start.4) | collective-permute-done | bytes 262176 | tf_op jit(solution)/shard_map/ppermute | solution.py:20
  38.2 0.0 collective-permute-done.5.lower
  38.2 0.0 copy-done
  38.2 0.3 volume.1.done.refs_7_
  38.5 1.4 %last.1 = (bf16[512,512]{1,0:T(8,128)(2,1)}, bf16[512,512]{1,0:T(8,128)(2,1)}) custom-call(bf16[512,1024]{1,0:T(8,128)(2,1)S(1)} %get-tuple-element.30.z.z_top, bf16[512,1024]{1,0:T(8,128)(2,1)S(1)} %get-tuple-element.35.z.z_low, bf16[512,256]{1,0:T(8,128)(2,1)S(1)} %collective-permute-done.4.left, bf16[512,256]{1,0:T(8,128)(2,1)S(1)} %collective-permute-done.5.lower), custom_call_target="tpu_custom_call" | custom-call | flops 536870912 | bytes 3145728 | tf_op jit(solution)/shard_map/last/pallas_call | solution.py:273
  40.0 3.6 %collective-permute-done.10.left = bf16[512,256]{1,0:T(8,128)(2,1)S(1)} collective-permute-done((bf16[512,256]{1,0:T(8,128)(2,1)S(1)}, bf16[512,256]{1,0:T(8,128)(2,1)S(1)}, u32[]{:S(2)}, u32[]{:S(2)}) %collective-permute-start.10) | collective-permute-done | bytes 262176 | tf_op jit(solution)/shard_map/ppermute | solution.py:20
  43.6 0.0 collective-permute-done.11.lower
  43.6 0.3 edges.1
  43.9 0.1 collective-permute-start.12
  44.0 0.1 collective-permute-start.13
  44.1 0.5 %collective-permute-start.14 = (bf16[16,512]{1,0:T(8,128)(2,1)S(1)}, bf16[16,512]{1,0:T(8,128)(2,1)S(1)}, u32[]{:S(2)}, u32[]{:S(2)}) collective-permute-start(bf16[16,512]{1,0:T(8,128)(2,1)S(1)} %get-tuple-element.49), channel_id=1, source_target_pairs={{0,1},{1,0},{2,3},{3,2},{4,5},{5,4},{6,7},{7,6},{8,9},{9,8},{10,11... | collective-permute-start | bytes 49160 | tf_op jit(solution)/shard_map/ppermute | solution.py:36
  44.6 1.4 %collective-permute-start.15 = (bf16[16,512]{1,0:T(8,128)(2,1)S(1)}, bf16[16,512]{1,0:T(8,128)(2,1)S(1)}, u32[]{:S(2)}, u32[]{:S(2)}) collective-permute-start(bf16[16,512]{1,0:T(8,128)(2,1)S(1)} %get-tuple-element.50), channel_id=1, source_target_pairs={{0,4},{1,2},{2,1},{3,7},{4,0},{5,6},{6,5},{7,3},{8,12},{9,10},{10,... | collective-permute-start | bytes 49160 | tf_op jit(solution)/shard_map/ppermute | solution.py:36
  46.0 0.7 %plain.1 = (bf16[512,256]{1,0:T(8,128)(2,1)S(1)}, bf16[512,256]{1,0:T(8,128)(2,1)S(1)}) custom-call(bf16[512,1024]{1,0:T(8,128)(2,1)S(1)} %get-tuple-element.30.z.z_top, bf16[512,1024]{1,0:T(8,128)(2,1)S(1)} %get-tuple-element.35.z.z_low, bf16[512,256]{1,0:T(8,128)(2,1)S(1)} %collective-permute-done.10.left, bf16[512,256]{1,0:T(8,128)(2,1)S(1)} %collective-permute-done.11.lower), custom_call_target="tpu_custom_call" | custom-call | flops 536870912 | bytes 3145728 | tf_op jit(solution)/shard_map/plain/pallas_call | solution.py:300
  46.8 1.0 %collective-permute-done.12.refs_3_ = bf16[16,512]{1,0:T(8,128)(2,1)S(1)} collective-permute-done((bf16[16,512]{1,0:T(8,128)(2,1)S(1)}, bf16[16,512]{1,0:T(8,128)(2,1)S(1)}, u32[]{:S(2)}, u32[]{:S(2)}) %collective-permute-start.12) | collective-permute-done | bytes 16416 | tf_op jit(solution)/shard_map/ppermute | solution.py:36
  47.7 0.0 collective-permute-done.13.refs_4_
  47.8 0.0 collective-permute-done.14.refs_5_
  47.8 0.6 %collective-permute-done.15.refs_6_ = bf16[16,512]{1,0:T(8,128)(2,1)S(1)} collective-permute-done((bf16[16,512]{1,0:T(8,128)(2,1)S(1)}, bf16[16,512]{1,0:T(8,128)(2,1)S(1)}, u32[]{:S(2)}, u32[]{:S(2)}) %collective-permute-start.15) | collective-permute-done | bytes 16416 | tf_op jit(solution)/shard_map/ppermute | solution.py:36
  48.3 1.0 %finish.1 = (bf16[512,512]{1,0:T(8,128)(2,1)}, bf16[512,512]{1,0:T(8,128)(2,1)}, f32[16,16,512]{2,1,0:T(8,128)}) custom-call(f32[256,128]{1,0:T(8,128)S(1)} %wavenum.1.refs_0_, bf16[512,256]{1,0:T(8,128)(2,1)S(1)} %get-tuple-element.44.refs_1_, bf16[512,256]{1,0:T(8,128)(2,1)S(1)} %get-tuple-element.45.refs_2_, ...), custom_call_target="tpu_custom_call", output_to_operand_aliasing={{0}: (9, {}), {1}: (10, {})} | custom-call | flops 1310720 | bytes 1048576 | tf_op jit(solution)/shard_map/finish/pallas_call | solution.py:361
Async XLA Ops:
  2.7 12.4 %collective-permute-start = (bf16[512,256]{1,0:T(8,128)(2,1)S(1)}, bf16[512,256]{1,0:T(8,128)(2,1)S(1)}, u32[]{:S(2)}, u32[]{:S(2)}) collective-permute-start(bf16[512,256]{1,0:T(8,128)(2,1)S(1)} %get-tuple-element.31), channel_id=1, source_target_pairs={{0,4},{4,8},{8,12},{12,16},{16,20},{20,24},{24,28},{28,0},{1,5},{5... | collective-permute-start | bytes 786440 | tf_op jit(solution)/shard_map/ppermute | solution.py:20
  7.6 7.4 %collective-permute-start.1 = (bf16[512,256]{1,0:T(8,128)(2,1)S(1)}, bf16[512,256]{1,0:T(8,128)(2,1)S(1)}, u32[]{:S(2)}, u32[]{:S(2)}) collective-permute-start(bf16[512,256]{1,0:T(8,128)(2,1)S(1)} %get-tuple-element.34), channel_id=1, source_target_pairs={{0,1},{1,2},{2,3},{3,0},{4,5},{5,6},{6,7},{7,4},{8,9},{9,10},{10,1... | collective-permute-start | bytes 786440 | tf_op jit(solution)/shard_map/ppermute | solution.py:20
  9.2 11.3 %collective-permute-start.6 = (bf16[512,256]{1,0:T(8,128)(2,1)S(1)}, bf16[512,256]{1,0:T(8,128)(2,1)S(1)}, u32[]{:S(2)}, u32[]{:S(2)}) collective-permute-start(bf16[512,256]{1,0:T(8,128)(2,1)S(1)} %get-tuple-element.36), channel_id=1, source_target_pairs={{0,4},{4,8},{8,12},{12,16},{16,20},{20,24},{24,28},{28,0},{1,5},{5... | collective-permute-start | bytes 786440 | tf_op jit(solution)/shard_map/ppermute | solution.py:20
  11.3 9.2 %collective-permute-start.7 = (bf16[512,256]{1,0:T(8,128)(2,1)S(1)}, bf16[512,256]{1,0:T(8,128)(2,1)S(1)}, u32[]{:S(2)}, u32[]{:S(2)}) collective-permute-start(bf16[512,256]{1,0:T(8,128)(2,1)S(1)} %part.13), channel_id=1, source_target_pairs={{0,1},{1,2},{2,3},{3,0},{4,5},{5,6},{6,7},{7,4},{8,9},{9,10},{10,1... | collective-permute-start | bytes 786440 | tf_op jit(solution)/shard_map/ppermute | solution.py:20
  15.5 11.2 %collective-permute-start.2 = (bf16[512,256]{1,0:T(8,128)(2,1)S(1)}, bf16[512,256]{1,0:T(8,128)(2,1)S(1)}, u32[]{:S(2)}, u32[]{:S(2)}) collective-permute-start(bf16[512,256]{1,0:T(8,128)(2,1)S(1)} %part.9), channel_id=1, source_target_pairs={{0,4},{4,8},{8,12},{12,16},{16,20},{20,24},{24,28},{28,0},{1,5},{5... | collective-permute-start | bytes 786440 | tf_op jit(solution)/shard_map/ppermute | solution.py:20
  16.0 10.7 %collective-permute-start.3 = (bf16[512,256]{1,0:T(8,128)(2,1)S(1)}, bf16[512,256]{1,0:T(8,128)(2,1)S(1)}, u32[]{:S(2)}, u32[]{:S(2)}) collective-permute-start(bf16[512,256]{1,0:T(8,128)(2,1)S(1)} %part.10), channel_id=1, source_target_pairs={{0,1},{1,2},{2,3},{3,0},{4,5},{5,6},{6,7},{7,4},{8,9},{9,10},{10,1... | collective-permute-start | bytes 786440 | tf_op jit(solution)/shard_map/ppermute | solution.py:20
  20.9 11.9 %collective-permute-start.8 = (bf16[512,256]{1,0:T(8,128)(2,1)S(1)}, bf16[512,256]{1,0:T(8,128)(2,1)S(1)}, u32[]{:S(2)}, u32[]{:S(2)}) collective-permute-start(bf16[512,256]{1,0:T(8,128)(2,1)S(1)} %part.14), channel_id=1, source_target_pairs={{0,4},{4,8},{8,12},{12,16},{16,20},{20,24},{24,28},{28,0},{1,5},{5... | collective-permute-start | bytes 786440 | tf_op jit(solution)/shard_map/ppermute | solution.py:20
  21.4 11.3 %collective-permute-start.9 = (bf16[512,256]{1,0:T(8,128)(2,1)S(1)}, bf16[512,256]{1,0:T(8,128)(2,1)S(1)}, u32[]{:S(2)}, u32[]{:S(2)}) collective-permute-start(bf16[512,256]{1,0:T(8,128)(2,1)S(1)} %part.15), channel_id=1, source_target_pairs={{0,1},{1,2},{2,3},{3,0},{4,5},{5,6},{6,7},{7,4},{8,9},{9,10},{10,1... | collective-permute-start | bytes 786440 | tf_op jit(solution)/shard_map/ppermute | solution.py:20
  27.2 11.0 %collective-permute-start.4 = (bf16[512,256]{1,0:T(8,128)(2,1)S(1)}, bf16[512,256]{1,0:T(8,128)(2,1)S(1)}, u32[]{:S(2)}, u32[]{:S(2)}) collective-permute-start(bf16[512,256]{1,0:T(8,128)(2,1)S(1)} %part.11), channel_id=1, source_target_pairs={{0,4},{4,8},{8,12},{12,16},{16,20},{20,24},{24,28},{28,0},{1,5},{5... | collective-permute-start | bytes 786440 | tf_op jit(solution)/shard_map/ppermute | solution.py:20
  27.7 6.1 %copy-start.1 = (s32[16,16]{1,0:T(8,128)S(1)}, s32[16,16]{1,0:T(8,128)}, u32[]{:S(2)}) copy-start(s32[16,16]{1,0:T(8,128)} %kinds.1) | copy-start | bytes 3076
  27.7 6.1 %copy-start.2 = (f32[16]{0:T(128)S(1)}, f32[16]{0:T(128)}, u32[]{:S(2)}) copy-start(f32[16]{0:T(128)} %table.1) | copy-start | bytes 196
  27.7 10.5 %copy-start = (bf16[1,1,256,1024]{3,2,1,0:T(8,128)(2,1)S(1)}, bf16[1,1,256,1024]{3,2,1,0:T(8,128)(2,1)}, u32[]{:S(2)}) copy-start(bf16[1,1,256,1024]{3,2,1,0:T(8,128)(2,1)} %param.7) | copy-start | bytes 1572868
  27.8 10.4 %collective-permute-start.5 = (bf16[512,256]{1,0:T(8,128)(2,1)S(1)}, bf16[512,256]{1,0:T(8,128)(2,1)S(1)}, u32[]{:S(2)}, u32[]{:S(2)}) collective-permute-start(bf16[512,256]{1,0:T(8,128)(2,1)S(1)} %part.12), channel_id=1, source_target_pairs={{0,1},{1,2},{2,3},{3,0},{4,5},{5,6},{6,7},{7,4},{8,9},{9,10},{10,1... | collective-permute-start | bytes 786440 | tf_op jit(solution)/shard_map/ppermute | solution.py:20
  33.2 10.4 %collective-permute-start.10 = (bf16[512,256]{1,0:T(8,128)(2,1)S(1)}, bf16[512,256]{1,0:T(8,128)(2,1)S(1)}, u32[]{:S(2)}, u32[]{:S(2)}) collective-permute-start(bf16[512,256]{1,0:T(8,128)(2,1)S(1)} %part.16), channel_id=1, source_target_pairs={{0,4},{4,8},{8,12},{12,16},{16,20},{20,24},{24,28},{28,0},{1,5},{5... | collective-permute-start | bytes 786440 | tf_op jit(solution)/shard_map/ppermute | solution.py:20
  33.7 9.9 %collective-permute-start.11 = (bf16[512,256]{1,0:T(8,128)(2,1)S(1)}, bf16[512,256]{1,0:T(8,128)(2,1)S(1)}, u32[]{:S(2)}, u32[]{:S(2)}) collective-permute-start(bf16[512,256]{1,0:T(8,128)(2,1)S(1)} %part.17), channel_id=1, source_target_pairs={{0,1},{1,2},{2,3},{3,0},{4,5},{5,6},{6,7},{7,4},{8,9},{9,10},{10,1... | collective-permute-start | bytes 786440 | tf_op jit(solution)/shard_map/ppermute | solution.py:20
  43.9 3.8 %collective-permute-start.12 = (bf16[16,512]{1,0:T(8,128)(2,1)S(1)}, bf16[16,512]{1,0:T(8,128)(2,1)S(1)}, u32[]{:S(2)}, u32[]{:S(2)}) collective-permute-start(bf16[16,512]{1,0:T(8,128)(2,1)S(1)} %get-tuple-element.47), channel_id=1, source_target_pairs={{0,4},{1,5},{2,6},{3,7},{4,0},{5,1},{6,2},{7,3},{8,12},{9,13},{10,... | collective-permute-start | bytes 49160 | tf_op jit(solution)/shard_map/ppermute | solution.py:36
  44.0 3.7 %collective-permute-start.13 = (bf16[16,512]{1,0:T(8,128)(2,1)S(1)}, bf16[16,512]{1,0:T(8,128)(2,1)S(1)}, u32[]{:S(2)}, u32[]{:S(2)}) collective-permute-start(bf16[16,512]{1,0:T(8,128)(2,1)S(1)} %get-tuple-element.48), channel_id=1, source_target_pairs={{0,1},{1,0},{2,3},{3,2},{4,8},{5,9},{6,10},{7,11},{8,4},{9,5},{10,... | collective-permute-start | bytes 49160 | tf_op jit(solution)/shard_map/ppermute | solution.py:36
  44.1 3.7 %collective-permute-start.14 = (bf16[16,512]{1,0:T(8,128)(2,1)S(1)}, bf16[16,512]{1,0:T(8,128)(2,1)S(1)}, u32[]{:S(2)}, u32[]{:S(2)}) collective-permute-start(bf16[16,512]{1,0:T(8,128)(2,1)S(1)} %get-tuple-element.49), channel_id=1, source_target_pairs={{0,1},{1,0},{2,3},{3,2},{4,5},{5,4},{6,7},{7,6},{8,9},{9,8},{10,11... | collective-permute-start | bytes 49160 | tf_op jit(solution)/shard_map/ppermute | solution.py:36
  44.6 3.7 %collective-permute-start.15 = (bf16[16,512]{1,0:T(8,128)(2,1)S(1)}, bf16[16,512]{1,0:T(8,128)(2,1)S(1)}, u32[]{:S(2)}, u32[]{:S(2)}) collective-permute-start(bf16[16,512]{1,0:T(8,128)(2,1)S(1)} %get-tuple-element.50), channel_id=1, source_target_pairs={{0,4},{1,2},{2,1},{3,7},{4,0},{5,6},{6,5},{7,3},{8,12},{9,10},{10,... | collective-permute-start | bytes 49160 | tf_op jit(solution)/shard_map/ppermute | solution.py:36

commit v4 on v3

--- a/solution.py
+++ b/solution.py
@@ -7,6 +7,7 @@
 from jax.experimental.pallas import tpu as pltpu
 from jax.sharding import PartitionSpec as P
 
+
 STEPS = 4
 CHUNKS = 2
 F32 = jnp.float32
@@ -18,6 +19,11 @@
 def around(block, axis):
     count = lax.axis_size(axis)
     return lax.ppermute(block, axis, [(i, (i + 1) % count) for i in range(count)])
+
+
+def onward(block, axis):
+    count = lax.axis_size(axis)
+    return lax.ppermute(block, axis, [(i, i + 1) for i in range(count - 1)])
 
 
 def swapped(block, axis, first):
@@ -30,6 +36,8 @@
         mate = first + ((where[along] - first) ^ 1)
         if 0 <= mate < sizes[along]:
             where[along] = mate
+        elif axis == "gy":
+            where[along] = sizes[along] - 1 - where[along]
         else:
             where[1 - along] ^= 1
         pairs.append((place, where[0] * sizes[1] + where[1]))
@@ -378,7 +386,7 @@
     lower_all = pltpu.with_memory_space_constraint(lower_trace[0, 0], pltpu.HBM)
     sources = left_all.shape[1]
     width = sources // CHUNKS
-    cells_x, cells_y = cell_kind.shape
+    _, cells_y = cell_kind.shape
     left_in, lower_in = [None] * CHUNKS, [None] * CHUNKS
     for step in range(STEPS - 1):
         for c in range(CHUNKS):
@@ -389,7 +397,8 @@
             else:
                 left, lower = left_in[c], lower_in[c]
                 right = part("gx", z_top, left, lower)
-            left_in[c] = around(right, "gx")
+            final = step == STEPS - 2 and c == CHUNKS - 1
+            left_in[c] = onward(right, "gx") if final else around(right, "gx")
             if step == 0 and c == 0:
                 upper, z_low = first_upper(z, left, lower)
             else:
@@ -403,8 +412,8 @@
         (volume_a, wavenum, left_in[1], lower_in[1], *outs)
     )
     volume_b, x_pair, x_cross, y_pair, y_cross = edges_of(weights, left_in[1], lower_in[1], volume_a, cells_y)
+    x_pair = swapped(x_pair, "gx", 0)
     x_cross = swapped(x_cross, "gx", 1)
-    x_pair = swapped(x_pair, "gx", 0)
     y_cross = swapped(y_cross, "gy", 1)
     y_pair = swapped(y_pair, "gy", 0)
     halos = (x_pair, x_cross, y_pair, y_cross)

time: 49.7 us -> 47.8 us (0.962)
  waiting for transfers between devices: 25.5 us -> 21.4 us
  starting transfers between devices: 9.07 us -> 11.4 us
    ppermute x12 -> x11, waiting for transfers between devices: 24 us -> 19.7 us  [around(): lax.ppermute(block, axis, [(i, (i + 1) % count) for i in range(count)])]
    ppermute x0 -> x1, starting transfers between devices: none -> 1.31 us  [onward(): return lax.ppermute(block, axis, [(i, i + 1) for i in range(count - 1)])]
    ppermute x4, starting transfers between devices: 2.08 us -> 3.13 us  [swapped(): return lax.ppermute(block, names, pairs)]
    ppermute x12 -> x11, starting transfers between devices: 6.99 us -> 6.93 us  [around(): lax.ppermute(block, axis, [(i, (i + 1) % count) for i in range(count)])]
  transfers between devices with their start and end apart: 16 -> 16, of which waited for: 8 -> 8; matrix products, arithmetic and copies ran while one was open for 0% -> 0% of each run, Pallas kernels for 21% -> 22%
where the time goes in v4:
time: 47.8 us; the launch traced here: 47.6 us
  waiting for transfers between devices  21.4 us (45%)
  Pallas kernels  13.8 us (29%)
  starting transfers between devices  11.4 us (24%)
  between operations  0.89 us (2%)
    ppermute x11, waiting for transfers between devices, around(): lax.ppermute(block, axis, [(i, (i + 1) % count) for i in range(count)])  19.7 us
    ppermute x11, starting transfers between devices, around(): lax.ppermute(block, axis, [(i, (i + 1) % count) for i in range(count)])  6.93 us
    pallas_call x9, Pallas kernels, part(): pl.pallas_call(functools.partial(part_kernel, axis), out_shape=jax.ShapeD...  3.92 us
    ppermute x4, starting transfers between devices, swapped(): return lax.ppermute(block, names, pairs)  3.13 us
    pallas_call x1, Pallas kernels, first_right(): pl.pallas_call(functools.partial(first_right_kernel, base, width), out_sh...  2.08 us
    pallas_call x1, Pallas kernels, first_upper(): pl.pallas_call(first_upper_kernel, out_shape=(vmem(trace, width), vmem(tr...  1.9 us
    ppermute x4, waiting for transfers between devices, swapped(): return lax.ppermute(block, names, pairs)  1.5 us
    pallas_call x1, Pallas kernels, part_loading(): pl.pallas_call(functools.partial(part_loading_kernel, axis, base), out_sh...  1.49 us
  transfers between devices with their start and end apart: 16, of which 8 were waited for; matrix products, arithmetic and copies ran while one was open for 0% of the time, Pallas kernels for 22%

profile of v4, /device:TPU:0, one launch (start us, length us, event | category | flops | bytes accessed | tf_op | source)
XLA Modules:
  0.0 47.6 jit_solution(16588060265704386081)
XLA Ops:
  0.6 2.1 %first_right.1 = (bf16[512,256]{1,0:T(8,128)(2,1)S(1)}, bf16[512,1024]{1,0:T(8,128)(2,1)S(1)}, bf16[512,256]{1,0:T(8,128)(2,1)S(1)}, bf16[512,256]{1,0:T(8,128)(2,1)S(1)}) custom-call(bf16[1024,1024]{1,0:T(8,128)(2,1)} %bitcast.8, bf16[512,512]{1,0:T(8,128)(2,1)} %bitcast.10, bf16[512,512]{1,0:T(8,128)(2,1)} %bitcast.12), custom_call_target="tpu_custom_call" | custom-call | flops 268435456 | bytes 1835008 | tf_op jit(solution)/shard_map/first_right/pallas_call | solution.py:90
  2.7 3.0 %collective-permute-start = (bf16[512,256]{1,0:T(8,128)(2,1)S(1)}, bf16[512,256]{1,0:T(8,128)(2,1)S(1)}, u32[]{:S(2)}, u32[]{:S(2)}) collective-permute-start(bf16[512,256]{1,0:T(8,128)(2,1)S(1)} %get-tuple-element.31), channel_id=1, source_target_pairs={{0,4},{4,8},{8,12},{12,16},{16,20},{20,24},{24,28},{28,0},{1,5},{5... | collective-permute-start | bytes 786440 | tf_op jit(solution)/shard_map/ppermute | solution.py:21
  5.7 1.9 %first_upper.1 = (bf16[512,256]{1,0:T(8,128)(2,1)S(1)}, bf16[512,1024]{1,0:T(8,128)(2,1)S(1)}) custom-call(bf16[1024,1024]{1,0:T(8,128)(2,1)} %bitcast.9, bf16[512,256]{1,0:T(8,128)(2,1)S(1)} %get-tuple-element.32.left, bf16[512,256]{1,0:T(8,128)(2,1)S(1)} %get-tuple-element.33.lower), custom_call_target="tpu_custom_call" | custom-call | flops 268435456 | bytes 1835008 | tf_op jit(solution)/shard_map/first_upper/pallas_call | solution.py:121
  7.6 0.1 collective-permute-start.1
  7.7 1.5 %part_loading.1 = (bf16[512,256]{1,0:T(8,128)(2,1)S(1)}, bf16[512,256]{1,0:T(8,128)(2,1)S(1)}, bf16[512,256]{1,0:T(8,128)(2,1)S(1)}) custom-call(bf16[512,1024]{1,0:T(8,128)(2,1)S(1)} %get-tuple-element.30.z.z_top, bf16[512,512]{1,0:T(8,128)(2,1)} %bitcast.11, bf16[512,512]{1,0:T(8,128)(2,1)} %bitcast.13), custom_call_target="tpu_custom_call" | custom-call | flops 268435456 | bytes 1835008 | tf_op jit(solution)/shard_map/part_loading/pallas_call | solution.py:170
  9.2 1.6 %collective-permute-start.6 = (bf16[512,256]{1,0:T(8,128)(2,1)S(1)}, bf16[512,256]{1,0:T(8,128)(2,1)S(1)}, u32[]{:S(2)}, u32[]{:S(2)}) collective-permute-start(bf16[512,256]{1,0:T(8,128)(2,1)S(1)} %get-tuple-element.36), channel_id=1, source_target_pairs={{0,4},{4,8},{8,12},{12,16},{16,20},{20,24},{24,28},{28,0},{1,5},{5... | collective-permute-start | bytes 786440 | tf_op jit(solution)/shard_map/ppermute | solution.py:21
  10.8 0.4 part.13
  11.3 1.4 %collective-permute-start.7 = (bf16[512,256]{1,0:T(8,128)(2,1)S(1)}, bf16[512,256]{1,0:T(8,128)(2,1)S(1)}, u32[]{:S(2)}, u32[]{:S(2)}) collective-permute-start(bf16[512,256]{1,0:T(8,128)(2,1)S(1)} %part.13), channel_id=1, source_target_pairs={{0,1},{1,2},{2,3},{3,0},{4,5},{5,6},{6,7},{7,4},{8,9},{9,10},{10,1... | collective-permute-start | bytes 786440 | tf_op jit(solution)/shard_map/ppermute | solution.py:21
  12.6 2.4 %collective-permute-done.left = bf16[512,256]{1,0:T(8,128)(2,1)S(1)} collective-permute-done((bf16[512,256]{1,0:T(8,128)(2,1)S(1)}, bf16[512,256]{1,0:T(8,128)(2,1)S(1)}, u32[]{:S(2)}, u32[]{:S(2)}) %collective-permute-start) | collective-permute-done | bytes 262176 | tf_op jit(solution)/shard_map/ppermute | solution.py:21
  15.1 0.0 collective-permute-done.1.lower
  15.1 0.4 part.9
  15.5 0.1 collective-permute-start.2
  15.6 0.4 part.10
  16.0 0.1 collective-permute-start.3
  16.1 4.4 %collective-permute-done.6.left = bf16[512,256]{1,0:T(8,128)(2,1)S(1)} collective-permute-done((bf16[512,256]{1,0:T(8,128)(2,1)S(1)}, bf16[512,256]{1,0:T(8,128)(2,1)S(1)}, u32[]{:S(2)}, u32[]{:S(2)}) %collective-permute-start.6) | collective-permute-done | bytes 262176 | tf_op jit(solution)/shard_map/ppermute | solution.py:21
  20.5 0.0 collective-permute-done.7.lower
  20.5 0.4 part.14
  20.9 0.1 collective-permute-start.8
  21.0 0.4 part.15
  21.4 0.5 %collective-permute-start.9 = (bf16[512,256]{1,0:T(8,128)(2,1)S(1)}, bf16[512,256]{1,0:T(8,128)(2,1)S(1)}, u32[]{:S(2)}, u32[]{:S(2)}) collective-permute-start(bf16[512,256]{1,0:T(8,128)(2,1)S(1)} %part.15), channel_id=1, source_target_pairs={{0,1},{1,2},{2,3},{3,0},{4,5},{5,6},{6,7},{7,4},{8,9},{9,10},{10,1... | collective-permute-start | bytes 786440 | tf_op jit(solution)/shard_map/ppermute | solution.py:21
  22.0 4.8 %collective-permute-done.2.left = bf16[512,256]{1,0:T(8,128)(2,1)S(1)} collective-permute-done((bf16[512,256]{1,0:T(8,128)(2,1)S(1)}, bf16[512,256]{1,0:T(8,128)(2,1)S(1)}, u32[]{:S(2)}, u32[]{:S(2)}) %collective-permute-start.2) | collective-permute-done | bytes 262176 | tf_op jit(solution)/shard_map/ppermute | solution.py:21
  26.8 0.0 collective-permute-done.3.lower
  26.8 0.4 part.11
  27.2 0.1 collective-permute-start.4
  27.3 0.4 part.12
  27.7 0.0 copy-start.1
  27.7 0.0 copy-start.2
  27.7 0.0 copy-start
  27.8 0.1 collective-permute-start.5
  27.8 5.0 %collective-permute-done.8.left = bf16[512,256]{1,0:T(8,128)(2,1)S(1)} collective-permute-done((bf16[512,256]{1,0:T(8,128)(2,1)S(1)}, bf16[512,256]{1,0:T(8,128)(2,1)S(1)}, u32[]{:S(2)}, u32[]{:S(2)}) %collective-permute-start.8) | collective-permute-done | bytes 262176 | tf_op jit(solution)/shard_map/ppermute | solution.py:21
  32.8 0.0 collective-permute-done.9.lower
  32.8 0.4 part.16
  33.2 1.3 %collective-permute-start.10 = (bf16[512,256]{1,0:T(8,128)(2,1)S(1)}, bf16[512,256]{1,0:T(8,128)(2,1)S(1)}, u32[]{:S(2)}, u32[]{:S(2)}) collective-permute-start(bf16[512,256]{1,0:T(8,128)(2,1)S(1)} %part.16), channel_id=1, source_target_pairs={{0,4},{4,8},{8,12},{12,16},{16,20},{20,24},{24,28},{1,5},{5,9},{9,... | collective-permute-start | bytes 786440 | tf_op jit(solution)/shard_map/ppermute | solution.py:26
  34.6 0.4 part.17
  35.0 0.1 collective-permute-start.11
  35.1 0.0 copy-done.1
  35.1 0.0 copy-done.2
  35.1 0.7 %wavenum.1.refs_0_ = f32[256,128]{1,0:T(8,128)S(1)} custom-call(f32[16]{0:T(128)S(1)} %copy-done.2, s32[16,16]{1,0:T(8,128)S(1)} %copy-done.1), custom_call_target="tpu_custom_call" | custom-call | tf_op jit(solution)/shard_map/wavenum/pallas_call | solution.py:196
  35.7 2.3 %collective-permute-done.4.left = bf16[512,256]{1,0:T(8,128)(2,1)S(1)} collective-permute-done((bf16[512,256]{1,0:T(8,128)(2,1)S(1)}, bf16[512,256]{1,0:T(8,128)(2,1)S(1)}, u32[]{:S(2)}, u32[]{:S(2)}) %collective-permute-start.4) | collective-permute-done | bytes 262176 | tf_op jit(solution)/shard_map/ppermute | solution.py:21
  38.0 0.0 collective-permute-done.5.lower
  38.0 0.0 copy-done
  38.0 0.3 volume.1.done.refs_7_
  38.3 1.4 %last.1 = (bf16[512,512]{1,0:T(8,128)(2,1)}, bf16[512,512]{1,0:T(8,128)(2,1)}) custom-call(bf16[512,1024]{1,0:T(8,128)(2,1)S(1)} %get-tuple-element.30.z.z_top, bf16[512,1024]{1,0:T(8,128)(2,1)S(1)} %get-tuple-element.35.z.z_low, bf16[512,256]{1,0:T(8,128)(2,1)S(1)} %collective-permute-done.4.left, bf16[512,256]{1,0:T(8,128)(2,1)S(1)} %collective-permute-done.5.lower), custom_call_target="tpu_custom_call" | custom-call | flops 536870912 | bytes 3145728 | tf_op jit(solution)/shard_map/last/pallas_call | solution.py:281
  39.8 0.2 collective-permute-done.10.left
  40.0 0.9 %collective-permute-done.11.lower = bf16[512,256]{1,0:T(8,128)(2,1)S(1)} collective-permute-done((bf16[512,256]{1,0:T(8,128)(2,1)S(1)}, bf16[512,256]{1,0:T(8,128)(2,1)S(1)}, u32[]{:S(2)}, u32[]{:S(2)}) %collective-permute-start.11) | collective-permute-done | bytes 262176 | tf_op jit(solution)/shard_map/ppermute | solution.py:21
  40.8 0.3 edges.1
  41.2 1.7 %collective-permute-start.12 = (bf16[16,512]{1,0:T(8,128)(2,1)S(1)}, bf16[16,512]{1,0:T(8,128)(2,1)S(1)}, u32[]{:S(2)}, u32[]{:S(2)}) collective-permute-start(bf16[16,512]{1,0:T(8,128)(2,1)S(1)} %get-tuple-element.47), channel_id=1, source_target_pairs={{0,4},{1,5},{2,6},{3,7},{4,0},{5,1},{6,2},{7,3},{8,12},{9,13},{10,... | collective-permute-start | bytes 49160 | tf_op jit(solution)/shard_map/ppermute | solution.py:44
  42.9 0.0 collective-permute-start.13
  42.9 0.5 %collective-permute-start.14 = (bf16[16,512]{1,0:T(8,128)(2,1)S(1)}, bf16[16,512]{1,0:T(8,128)(2,1)S(1)}, u32[]{:S(2)}, u32[]{:S(2)}) collective-permute-start(bf16[16,512]{1,0:T(8,128)(2,1)S(1)} %get-tuple-element.49), channel_id=1, source_target_pairs={{0,1},{1,0},{2,3},{3,2},{4,5},{5,4},{6,7},{7,6},{8,9},{9,8},{10,11... | collective-permute-start | bytes 49160 | tf_op jit(solution)/shard_map/ppermute | solution.py:44
  43.4 0.9 %collective-permute-start.15 = (bf16[16,512]{1,0:T(8,128)(2,1)S(1)}, bf16[16,512]{1,0:T(8,128)(2,1)S(1)}, u32[]{:S(2)}, u32[]{:S(2)}) collective-permute-start(bf16[16,512]{1,0:T(8,128)(2,1)S(1)} %get-tuple-element.50), channel_id=1, source_target_pairs={{0,3},{1,2},{2,1},{3,0},{4,7},{5,6},{6,5},{7,4},{8,11},{9,10},{10,... | collective-permute-start | bytes 49160 | tf_op jit(solution)/shard_map/ppermute | solution.py:44
  44.3 0.7 %plain.1 = (bf16[512,256]{1,0:T(8,128)(2,1)S(1)}, bf16[512,256]{1,0:T(8,128)(2,1)S(1)}) custom-call(bf16[512,1024]{1,0:T(8,128)(2,1)S(1)} %get-tuple-element.30.z.z_top, bf16[512,1024]{1,0:T(8,128)(2,1)S(1)} %get-tuple-element.35.z.z_low, bf16[512,256]{1,0:T(8,128)(2,1)S(1)} %collective-permute-done.10.left, bf16[512,256]{1,0:T(8,128)(2,1)S(1)} %collective-permute-done.11.lower), custom_call_target="tpu_custom_call" | custom-call | flops 536870912 | bytes 3145728 | tf_op jit(solution)/shard_map/plain/pallas_call | solution.py:308
  45.0 0.0 collective-permute-done.12.refs_3_
  45.0 0.0 collective-permute-done.13.refs_4_
  45.0 0.0 collective-permute-done.14.refs_5_
  45.0 1.5 %collective-permute-done.15.refs_6_ = bf16[16,512]{1,0:T(8,128)(2,1)S(1)} collective-permute-done((bf16[16,512]{1,0:T(8,128)(2,1)S(1)}, bf16[16,512]{1,0:T(8,128)(2,1)S(1)}, u32[]{:S(2)}, u32[]{:S(2)}) %collective-permute-start.15) | collective-permute-done | bytes 16416 | tf_op jit(solution)/shard_map/ppermute | solution.py:44
  46.5 1.0 %finish.1 = (bf16[512,512]{1,0:T(8,128)(2,1)}, bf16[512,512]{1,0:T(8,128)(2,1)}, f32[16,16,512]{2,1,0:T(8,128)}) custom-call(f32[256,128]{1,0:T(8,128)S(1)} %wavenum.1.refs_0_, bf16[512,256]{1,0:T(8,128)(2,1)S(1)} %get-tuple-element.44.refs_1_, bf16[512,256]{1,0:T(8,128)(2,1)S(1)} %get-tuple-element.45.refs_2_, ...), custom_call_target="tpu_custom_call", output_to_operand_aliasing={{0}: (9, {}), {1}: (10, {})} | custom-call | flops 1310720 | bytes 1048576 | tf_op jit(solution)/shard_map/finish/pallas_call | solution.py:369
Async XLA Ops:
  2.7 12.4 %collective-permute-start = (bf16[512,256]{1,0:T(8,128)(2,1)S(1)}, bf16[512,256]{1,0:T(8,128)(2,1)S(1)}, u32[]{:S(2)}, u32[]{:S(2)}) collective-permute-start(bf16[512,256]{1,0:T(8,128)(2,1)S(1)} %get-tuple-element.31), channel_id=1, source_target_pairs={{0,4},{4,8},{8,12},{12,16},{16,20},{20,24},{24,28},{28,0},{1,5},{5... | collective-permute-start | bytes 786440 | tf_op jit(solution)/shard_map/ppermute | solution.py:21
  7.6 7.4 %collective-permute-start.1 = (bf16[512,256]{1,0:T(8,128)(2,1)S(1)}, bf16[512,256]{1,0:T(8,128)(2,1)S(1)}, u32[]{:S(2)}, u32[]{:S(2)}) collective-permute-start(bf16[512,256]{1,0:T(8,128)(2,1)S(1)} %get-tuple-element.34), channel_id=1, source_target_pairs={{0,1},{1,2},{2,3},{3,0},{4,5},{5,6},{6,7},{7,4},{8,9},{9,10},{10,1... | collective-permute-start | bytes 786440 | tf_op jit(solution)/shard_map/ppermute | solution.py:21
  9.2 11.3 %collective-permute-start.6 = (bf16[512,256]{1,0:T(8,128)(2,1)S(1)}, bf16[512,256]{1,0:T(8,128)(2,1)S(1)}, u32[]{:S(2)}, u32[]{:S(2)}) collective-permute-start(bf16[512,256]{1,0:T(8,128)(2,1)S(1)} %get-tuple-element.36), channel_id=1, source_target_pairs={{0,4},{4,8},{8,12},{12,16},{16,20},{20,24},{24,28},{28,0},{1,5},{5... | collective-permute-start | bytes 786440 | tf_op jit(solution)/shard_map/ppermute | solution.py:21
  11.3 9.2 %collective-permute-start.7 = (bf16[512,256]{1,0:T(8,128)(2,1)S(1)}, bf16[512,256]{1,0:T(8,128)(2,1)S(1)}, u32[]{:S(2)}, u32[]{:S(2)}) collective-permute-start(bf16[512,256]{1,0:T(8,128)(2,1)S(1)} %part.13), channel_id=1, source_target_pairs={{0,1},{1,2},{2,3},{3,0},{4,5},{5,6},{6,7},{7,4},{8,9},{9,10},{10,1... | collective-permute-start | bytes 786440 | tf_op jit(solution)/shard_map/ppermute | solution.py:21
  15.5 11.2 %collective-permute-start.2 = (bf16[512,256]{1,0:T(8,128)(2,1)S(1)}, bf16[512,256]{1,0:T(8,128)(2,1)S(1)}, u32[]{:S(2)}, u32[]{:S(2)}) collective-permute-start(bf16[512,256]{1,0:T(8,128)(2,1)S(1)} %part.9), channel_id=1, source_target_pairs={{0,4},{4,8},{8,12},{12,16},{16,20},{20,24},{24,28},{28,0},{1,5},{5... | collective-permute-start | bytes 786440 | tf_op jit(solution)/shard_map/ppermute | solution.py:21
  16.0 10.7 %collective-permute-start.3 = (bf16[512,256]{1,0:T(8,128)(2,1)S(1)}, bf16[512,256]{1,0:T(8,128)(2,1)S(1)}, u32[]{:S(2)}, u32[]{:S(2)}) collective-permute-start(bf16[512,256]{1,0:T(8,128)(2,1)S(1)} %part.10), channel_id=1, source_target_pairs={{0,1},{1,2},{2,3},{3,0},{4,5},{5,6},{6,7},{7,4},{8,9},{9,10},{10,1... | collective-permute-start | bytes 786440 | tf_op jit(solution)/shard_map/ppermute | solution.py:21
  20.9 11.9 %collective-permute-start.8 = (bf16[512,256]{1,0:T(8,128)(2,1)S(1)}, bf16[512,256]{1,0:T(8,128)(2,1)S(1)}, u32[]{:S(2)}, u32[]{:S(2)}) collective-permute-start(bf16[512,256]{1,0:T(8,128)(2,1)S(1)} %part.14), channel_id=1, source_target_pairs={{0,4},{4,8},{8,12},{12,16},{16,20},{20,24},{24,28},{28,0},{1,5},{5... | collective-permute-start | bytes 786440 | tf_op jit(solution)/shard_map/ppermute | solution.py:21
  21.4 11.3 %collective-permute-start.9 = (bf16[512,256]{1,0:T(8,128)(2,1)S(1)}, bf16[512,256]{1,0:T(8,128)(2,1)S(1)}, u32[]{:S(2)}, u32[]{:S(2)}) collective-permute-start(bf16[512,256]{1,0:T(8,128)(2,1)S(1)} %part.15), channel_id=1, source_target_pairs={{0,1},{1,2},{2,3},{3,0},{4,5},{5,6},{6,7},{7,4},{8,9},{9,10},{10,1... | collective-permute-start | bytes 786440 | tf_op jit(solution)/shard_map/ppermute | solution.py:21
  27.2 10.8 %collective-permute-start.4 = (bf16[512,256]{1,0:T(8,128)(2,1)S(1)}, bf16[512,256]{1,0:T(8,128)(2,1)S(1)}, u32[]{:S(2)}, u32[]{:S(2)}) collective-permute-start(bf16[512,256]{1,0:T(8,128)(2,1)S(1)} %part.11), channel_id=1, source_target_pairs={{0,4},{4,8},{8,12},{12,16},{16,20},{20,24},{24,28},{28,0},{1,5},{5... | collective-permute-start | bytes 786440 | tf_op jit(solution)/shard_map/ppermute | solution.py:21
  27.7 7.3 %copy-start.1 = (s32[16,16]{1,0:T(8,128)S(1)}, s32[16,16]{1,0:T(8,128)}, u32[]{:S(2)}) copy-start(s32[16,16]{1,0:T(8,128)} %kinds.1) | copy-start | bytes 3076
  27.7 7.3 %copy-start.2 = (f32[16]{0:T(128)S(1)}, f32[16]{0:T(128)}, u32[]{:S(2)}) copy-start(f32[16]{0:T(128)} %table.1) | copy-start | bytes 196
  27.7 10.3 %copy-start = (bf16[1,1,256,1024]{3,2,1,0:T(8,128)(2,1)S(1)}, bf16[1,1,256,1024]{3,2,1,0:T(8,128)(2,1)}, u32[]{:S(2)}) copy-start(bf16[1,1,256,1024]{3,2,1,0:T(8,128)(2,1)} %param.7) | copy-start | bytes 1572868
  27.8 10.2 %collective-permute-start.5 = (bf16[512,256]{1,0:T(8,128)(2,1)S(1)}, bf16[512,256]{1,0:T(8,128)(2,1)S(1)}, u32[]{:S(2)}, u32[]{:S(2)}) collective-permute-start(bf16[512,256]{1,0:T(8,128)(2,1)S(1)} %part.12), channel_id=1, source_target_pairs={{0,1},{1,2},{2,3},{3,0},{4,5},{5,6},{6,7},{7,4},{8,9},{9,10},{10,1... | collective-permute-start | bytes 786440 | tf_op jit(solution)/shard_map/ppermute | solution.py:21
  33.2 6.7 %collective-permute-start.10 = (bf16[512,256]{1,0:T(8,128)(2,1)S(1)}, bf16[512,256]{1,0:T(8,128)(2,1)S(1)}, u32[]{:S(2)}, u32[]{:S(2)}) collective-permute-start(bf16[512,256]{1,0:T(8,128)(2,1)S(1)} %part.16), channel_id=1, source_target_pairs={{0,4},{4,8},{8,12},{12,16},{16,20},{20,24},{24,28},{1,5},{5,9},{9,... | collective-permute-start | bytes 786440 | tf_op jit(solution)/shard_map/ppermute | solution.py:26
  35.0 5.8 %collective-permute-start.11 = (bf16[512,256]{1,0:T(8,128)(2,1)S(1)}, bf16[512,256]{1,0:T(8,128)(2,1)S(1)}, u32[]{:S(2)}, u32[]{:S(2)}) collective-permute-start(bf16[512,256]{1,0:T(8,128)(2,1)S(1)} %part.17), channel_id=1, source_target_pairs={{0,1},{1,2},{2,3},{3,0},{4,5},{5,6},{6,7},{7,4},{8,9},{9,10},{10,1... | collective-permute-start | bytes 786440 | tf_op jit(solution)/shard_map/ppermute | solution.py:21
  41.2 3.8 %collective-permute-start.12 = (bf16[16,512]{1,0:T(8,128)(2,1)S(1)}, bf16[16,512]{1,0:T(8,128)(2,1)S(1)}, u32[]{:S(2)}, u32[]{:S(2)}) collective-permute-start(bf16[16,512]{1,0:T(8,128)(2,1)S(1)} %get-tuple-element.47), channel_id=1, source_target_pairs={{0,4},{1,5},{2,6},{3,7},{4,0},{5,1},{6,2},{7,3},{8,12},{9,13},{10,... | collective-permute-start | bytes 49160 | tf_op jit(solution)/shard_map/ppermute | solution.py:44
  42.9 2.2 %collective-permute-start.13 = (bf16[16,512]{1,0:T(8,128)(2,1)S(1)}, bf16[16,512]{1,0:T(8,128)(2,1)S(1)}, u32[]{:S(2)}, u32[]{:S(2)}) collective-permute-start(bf16[16,512]{1,0:T(8,128)(2,1)S(1)} %get-tuple-element.48), channel_id=1, source_target_pairs={{0,1},{1,0},{2,3},{3,2},{4,8},{5,9},{6,10},{7,11},{8,4},{9,5},{10,... | collective-permute-start | bytes 49160 | tf_op jit(solution)/shard_map/ppermute | solution.py:44
  42.9 2.2 %collective-permute-start.14 = (bf16[16,512]{1,0:T(8,128)(2,1)S(1)}, bf16[16,512]{1,0:T(8,128)(2,1)S(1)}, u32[]{:S(2)}, u32[]{:S(2)}) collective-permute-start(bf16[16,512]{1,0:T(8,128)(2,1)S(1)} %get-tuple-element.49), channel_id=1, source_target_pairs={{0,1},{1,0},{2,3},{3,2},{4,5},{5,4},{6,7},{7,6},{8,9},{9,8},{10,11... | collective-permute-start | bytes 49160 | tf_op jit(solution)/shard_map/ppermute | solution.py:44
  43.4 3.2 %collective-permute-start.15 = (bf16[16,512]{1,0:T(8,128)(2,1)S(1)}, bf16[16,512]{1,0:T(8,128)(2,1)S(1)}, u32[]{:S(2)}, u32[]{:S(2)}) collective-permute-start(bf16[16,512]{1,0:T(8,128)(2,1)S(1)} %get-tuple-element.50), channel_id=1, source_target_pairs={{0,3},{1,2},{2,1},{3,0},{4,7},{5,6},{6,5},{7,4},{8,11},{9,10},{10,... | collective-permute-start | bytes 49160 | tf_op jit(solution)/shard_map/ppermute | solution.py:44

commit v5 on v4

--- a/solution.py
+++ b/solution.py
@@ -56,10 +56,13 @@
 
 
 def product(weights, left, lower):
-    half = left.shape[0]
-    return jnp.dot(weights[:, :half], left[...], preferred_element_type=F32) + jnp.dot(
-        weights[:, half:], lower[...], preferred_element_type=F32
-    )
+    total, start = None, 0
+    for piece in (*left, lower):
+        rows = piece.shape[0]
+        share = jnp.dot(weights[:, start : start + rows], piece[...], preferred_element_type=F32)
+        total = share if total is None else total + share
+        start += rows
+    return total
 
 
 def first_right_kernel(base, width, z_hbm, left_hbm, lower_hbm, out, z_top, left, lower, sem):
@@ -81,7 +84,7 @@
     for r in range(2):
         parts[r].wait()
         here = pl.ds(r * block, block)
-        out[here] = jnp.where(at_end, 0.0, product(z_top.at[here], left, lower)).astype(BF16)
+        out[here] = jnp.where(at_end, 0.0, product(z_top.at[here], [left], lower)).astype(BF16)
 
 
 def first_right(z, left, lower, base, width):
@@ -112,7 +115,7 @@
     for r in range(2):
         parts[r].wait()
         here = pl.ds(r * block, block)
-        out[here] = jnp.where(at_end, 0.0, product(z_low.at[here], left, lower)).astype(BF16)
+        out[here] = jnp.where(at_end, 0.0, product(z_low.at[here], [left], lower)).astype(BF16)
 
 
 def first_upper(z, left, lower):
@@ -135,7 +138,7 @@
     at_end = is_last(axis)
     for r in range(2):
         here = pl.ds(r * half, half)
-        out[here] = jnp.where(at_end, 0.0, product(z.at[here], left, lower)).astype(BF16)
+        out[here] = jnp.where(at_end, 0.0, product(z.at[here], [left], lower)).astype(BF16)
 
 
 def part(axis, z, left, lower):
@@ -204,7 +207,7 @@
 
 
 def volume_kernel(weights, left, lower, volume):
-    volume[...] = product(weights, left, lower)
+    volume[...] = product(weights, [left], lower)
 
 
 def volume_of(weights, left, lower):
@@ -220,7 +223,9 @@
     )(weights, left, lower)
 
 
-def edges_kernel(cells_y, weights, left, lower, done, volume, x_pair, x_cross, y_pair, y_cross):
+def edges_kernel(cells_y, weights, lower, done, *refs):
+    left = refs[:-5]
+    volume, x_pair, x_cross, y_pair, y_cross = refs[-5:]
     cells = weights.shape[0]
     old = done.shape[1]
     volume[...] = product(weights, left, lower)
@@ -239,7 +244,7 @@
 
 def edges_of(weights, left, lower, done, cells_y):
     cells = weights.shape[0]
-    width = left.shape[1]
+    width = lower.shape[1]
     total = width + done.shape[1]
     line = lambda n: jax.ShapeDtypeStruct((n, total), BF16)
     return pl.pallas_call(
@@ -251,12 +256,12 @@
             line(cells // cells_y),
             line(cells // cells_y),
         ),
-        in_specs=[VMEM] * 4,
+        in_specs=[VMEM] * (3 + len(left)),
         out_specs=(VMEM,) * 5,
         cost_estimate=cost(2 * weights.size * width, 2 * weights.size + 4 * weights.shape[1] * width),
         compiler_params=PARAMS,
         name="edges",
-    )(weights, left, lower, done)
+    )(weights, lower, done, *left)
 
 
 def last_kernel(z_top, z_low, left, lower, right_hbm, upper_hbm, right, upper, sem):
@@ -266,7 +271,7 @@
     for z, out, out_hbm in ((z_top, right, right_hbm), (z_low, upper, upper_hbm)):
         for r in range(2):
             here = pl.ds(r * half, half)
-            out[here] = product(z.at[here], left, lower).astype(BF16)
+            out[here] = product(z.at[here], [left], lower).astype(BF16)
             copies.append(
                 pltpu.make_async_copy(out.at[here], out_hbm.at[here, pl.ds(0, width)], sem.at[len(copies)])
             )
@@ -294,26 +299,63 @@
     )(z_top, z_low, left, lower)
 
 
-def plain_kernel(z_top, z_low, left, lower, right, upper):
-    half = left.shape[0] // 2
-    for z, out in ((z_top, right), (z_low, upper)):
+def plain_kernel(z_top, z_low, lower, wavenum, first, second, *refs):
+    right_hbm, upper_hbm, inner, right, upper, sem = refs[-6:]
+    left = refs[:-8]
+    half, width = right.shape[0] // 2, right.shape[1]
+    base = right_hbm.shape[1] - width
+    copies = []
+    for z, out, out_hbm in ((z_top, right, right_hbm), (z_low, upper, upper_hbm)):
         for r in range(2):
             here = pl.ds(r * half, half)
             out[here] = product(z.at[here], left, lower).astype(BF16)
-
-
-def plain(z_top, z_low, left, lower):
-    trace, width = left.shape
-    out = jax.ShapeDtypeStruct((trace, width), BF16)
+            copies.append(
+                pltpu.make_async_copy(out.at[here], out_hbm.at[here, pl.ds(base, width)], sem.at[len(copies)])
+            )
+            copies[-1].start()
+    cells_x, cells_y = inner.shape[:2]
+    start = 0
+    for volume in (first, second):
+        where = pl.ds(start, volume.shape[1])
+        start += volume.shape[1]
+        place = lax.broadcasted_iota(jnp.int32, (cells_y, volume.shape[1]), 0)
+        for x in range(cells_x):
+            row = lambda k: volume[pl.ds(k * cells_y, cells_y)]
+            here = row(x)
+            around_it = jnp.where(place == 0, 0.0, pltpu.roll(here, 1, 0)) + jnp.where(
+                place == cells_y - 1, 0.0, pltpu.roll(here, cells_y - 1, 0)
+            )
+            if x:
+                around_it = around_it + row(x - 1)
+            if x + 1 < cells_x:
+                around_it = around_it + row(x + 1)
+            scale = wavenum[pl.ds(x * cells_y, cells_y)][:, :1]
+            inner[x, :, where] = around_it - 4.0 * here + scale * here
+    for copy in copies:
+        copy.wait()
+
+
+def plain(z_top, z_low, left, lower, wavenum, volumes, outs, cells_y):
+    trace, width = lower.shape
+    cells = volumes[0].shape[0]
+    total = outs[0].shape[1]
+    given = 6 + len(left)
     return pl.pallas_call(
         plain_kernel,
-        out_shape=(out, out),
-        in_specs=[VMEM] * 4,
-        out_specs=(VMEM, VMEM),
+        out_shape=tuple(jax.ShapeDtypeStruct(o.shape, o.dtype) for o in outs)
+        + (jax.ShapeDtypeStruct((cells // cells_y, cells_y, total), F32),),
+        in_specs=[VMEM] * given + [HBM] * 2,
+        out_specs=(HBM, HBM, VMEM),
+        scratch_shapes=[
+            pltpu.VMEM((trace, width), BF16),
+            pltpu.VMEM((trace, width), BF16),
+            pltpu.SemaphoreType.DMA((4,)),
+        ],
+        input_output_aliases={given: 0, given + 1: 1},
         cost_estimate=cost(8 * trace * trace * width, 8 * trace * trace + 8 * trace * width),
         compiler_params=PARAMS,
         name="plain",
-    )(z_top, z_low, left, lower)
+    )(z_top, z_low, lower, wavenum, *volumes, *left, *outs)
 
 
 def beside(axis, pair, cross):
@@ -325,58 +367,44 @@
     return before, after
 
 
-def finish_kernel(cells_y, *refs):
-    wavenum, right, upper, x_pair, x_cross, y_pair, y_cross = refs[:7]
-    right_hbm, upper_hbm, residual_hbm, out, sem = refs[-5:]
-    volumes = refs[7:-7]
-    base = right_hbm.shape[1] - right.shape[1]
-    copies = [
-        pltpu.make_async_copy(right, right_hbm.at[:, pl.ds(base, right.shape[1])], sem.at[0]),
-        pltpu.make_async_copy(upper, upper_hbm.at[:, pl.ds(base, upper.shape[1])], sem.at[1]),
-    ]
-    for copy in copies:
-        copy.start()
-    cells = volumes[0].shape[0]
-    start = 0
-    for volume in volumes:
-        width = volume.shape[1]
-        where = pl.ds(start, width)
-        start += width
-        before_x, after_x = beside("gx", x_pair.at[:, where], x_cross.at[:, where])
-        before_y, after_y = beside("gy", y_pair.at[:, where], y_cross.at[:, where])
-        place = lax.broadcasted_iota(jnp.int32, (cells_y, width), 0)
-        for x in range(cells // cells_y):
-            here = volume[pl.ds(x * cells_y, cells_y)]
-            left = volume[pl.ds((x - 1) * cells_y, cells_y)] if x else before_x
-            after = volume[pl.ds((x + 1) * cells_y, cells_y)] if (x + 1) * cells_y < cells else after_x
-            below = jnp.where(place == 0, before_y[x : x + 1], pltpu.roll(here, 1, 0))
-            above = jnp.where(place == cells_y - 1, after_y[x : x + 1], pltpu.roll(here, cells_y - 1, 0))
-            scale = wavenum[pl.ds(x * cells_y, cells_y)][:, :1]
-            out[x, :, where] = (after + left + above + below - 4.0 * here) + scale * here
-        copies.append(
-            pltpu.make_async_copy(out.at[:, :, where], residual_hbm.at[:, :, where], sem.at[len(copies)])
-        )
+def finish_kernel(inner, x_pair, x_cross, y_pair, y_cross, residual_hbm, out, sem):
+    cells_x, cells_y, total = inner.shape
+    groups = sem.shape[0]
+    deep = cells_x // groups
+    before_x, after_x = beside("gx", x_pair, x_cross)
+    before_y, after_y = beside("gy", y_pair, y_cross)
+    place = lax.broadcasted_iota(jnp.int32, (cells_y, total), 0)
+    copies = []
+    for group in range(groups):
+        for x in range(group * deep, (group + 1) * deep):
+            value = inner[x]
+            value = value + jnp.where(
+                place == 0, before_y[x : x + 1], jnp.where(place == cells_y - 1, after_y[x : x + 1], 0.0)
+            )
+            if x == 0:
+                value = value + before_x
+            if x == cells_x - 1:
+                value = value + after_x
+            out[x] = value
+        here = pl.ds(group * deep, deep)
+        copies.append(pltpu.make_async_copy(out.at[here], residual_hbm.at[here], sem.at[group]))
         copies[-1].start()
     for copy in copies:
         copy.wait()
 
 
-def finish(wavenum, right, upper, halos, volumes, outs, cells_y):
-    cells = volumes[0].shape[0]
-    total = outs[0].shape[1]
-    whole = (cells // cells_y, cells_y, total)
-    given = 3 + len(halos) + len(volumes)
-    return pl.pallas_call(
-        functools.partial(finish_kernel, cells_y),
-        out_shape=tuple(jax.ShapeDtypeStruct(o.shape, o.dtype) for o in outs) + (jax.ShapeDtypeStruct(whole, F32),),
-        in_specs=[VMEM] * given + [HBM] * 2,
-        out_specs=(HBM,) * 3,
-        scratch_shapes=[pltpu.VMEM(whole, F32), pltpu.SemaphoreType.DMA((2 + len(volumes),))],
-        input_output_aliases={given: 0, given + 1: 1},
-        cost_estimate=cost(10 * cells * total, 8 * cells * total),
+def finish(inner, halos):
+    groups = 2 if inner.shape[0] % 2 == 0 else 1
+    return pl.pallas_call(
+        finish_kernel,
+        out_shape=jax.ShapeDtypeStruct(inner.shape, F32),
+        in_specs=[VMEM] * (1 + len(halos)),
+        out_specs=HBM,
+        scratch_shapes=[pltpu.VMEM(inner.shape, F32), pltpu.SemaphoreType.DMA((groups,))],
+        cost_estimate=cost(4 * inner.size, 8 * inner.size),
         compiler_params=PARAMS,
         name="finish",
-    )(wavenum, right, upper, *halos, *volumes, *outs)
+    )(inner, *halos)
 
 
 def per_device(impedance, rebuild_map, left_trace, lower_trace, cell_kind, kind_wavenum):
@@ -405,22 +433,23 @@
                 upper = part("gy", z_low, left, lower)
             lower_in[c] = around(upper, "gy")
 
+    left_in[-1] = (left_in[-1],)
     wavenum = wavenum_of(kind_wavenum, cell_kind)
     volume_a = volume_of(weights, left_in[0], lower_in[0])
     outs = last(z_top, z_low, left_in[0], lower_in[0], sources)
-    volume_a, wavenum, left_in[1], lower_in[1], *outs = lax.optimization_barrier(
+    volume_a, wavenum, left, lower, *outs = lax.optimization_barrier(
         (volume_a, wavenum, left_in[1], lower_in[1], *outs)
     )
-    volume_b, x_pair, x_cross, y_pair, y_cross = edges_of(weights, left_in[1], lower_in[1], volume_a, cells_y)
+    volume_b, x_pair, x_cross, y_pair, y_cross = edges_of(weights, left, lower, volume_a, cells_y)
     x_pair = swapped(x_pair, "gx", 0)
     x_cross = swapped(x_cross, "gx", 1)
     y_cross = swapped(y_cross, "gy", 1)
     y_pair = swapped(y_pair, "gy", 0)
     halos = (x_pair, x_cross, y_pair, y_cross)
-    right, upper = plain(z_top, z_low, left_in[1], lower_in[1])
-    right_out, upper_out, residual = finish(
-        wavenum, right, upper, halos, (volume_a, volume_b), outs, cells_y
+    right_out, upper_out, inner = plain(
+        z_top, z_low, left, lower, wavenum, (volume_a, volume_b), outs, cells_y
     )
+    residual = finish(inner, halos)
     return (right_out[None, None], upper_out[None, None], residual)
 
 

time: 47.8 us -> 47.6 us (level)
  waiting for transfers between devices: 21.4 us -> 20.7 us
  Pallas kernels: 13.8 us -> 14.4 us
    ppermute x4, waiting for transfers between devices: 1.5 us -> 0.72 us  [swapped(): return lax.ppermute(block, names, pairs)]
    pallas_call x2, Pallas kernels: 1.71 us -> 2.33 us  [the longest x1 1.48 us: plain(): pl.pallas_call(plain_kernel, out_shape=tuple((jax.ShapeDtypeStruct(o.shap...]
  transfers between devices with their start and end apart: 16 -> 16, of which waited for: 8 -> 8; matrix products, arithmetic and copies ran while one was open for 0% -> 0% of each run, Pallas kernels for 22% -> 24%
where the time goes in v5:
time: 47.6 us; the launch traced here: 47.4 us
  waiting for transfers between devices  20.7 us (43%)
  Pallas kernels  14.4 us (30%)
  starting transfers between devices  11.4 us (24%)
  between operations  0.89 us (2%)
    ppermute x11, waiting for transfers between devices, around(): lax.ppermute(block, axis, [(i, (i + 1) % count) for i in range(count)])  19.7 us
    ppermute x11, starting transfers between devices, around(): lax.ppermute(block, axis, [(i, (i + 1) % count) for i in range(count)])  6.93 us
    pallas_call x9, Pallas kernels, part(): pl.pallas_call(functools.partial(part_kernel, axis), out_shape=jax.ShapeD...  3.92 us
    ppermute x4, starting transfers between devices, swapped(): return lax.ppermute(block, names, pairs)  3.13 us
    pallas_call x1, Pallas kernels, first_right(): pl.pallas_call(functools.partial(first_right_kernel, base, width), out_sh...  2.08 us
    pallas_call x1, Pallas kernels, first_upper(): pl.pallas_call(first_upper_kernel, out_shape=(vmem(trace, width), vmem(tr...  1.9 us
    pallas_call x1, Pallas kernels, part_loading(): pl.pallas_call(functools.partial(part_loading_kernel, axis, base), out_sh...  1.49 us
    pallas_call x1, Pallas kernels, plain(): pl.pallas_call(plain_kernel, out_shape=tuple((jax.ShapeDtypeStruct(o.shap...  1.48 us
  transfers between devices with their start and end apart: 16, of which 8 were waited for; matrix products, arithmetic and copies ran while one was open for 0% of the time, Pallas kernels for 24%

profile of v5, /device:TPU:0, one launch (start us, length us, event | category | flops | bytes accessed | tf_op | source)
XLA Modules:
  0.0 47.4 jit_solution(9105863796499924091)
XLA Ops:
  0.6 2.1 %first_right.1 = (bf16[512,256]{1,0:T(8,128)(2,1)S(1)}, bf16[512,1024]{1,0:T(8,128)(2,1)S(1)}, bf16[512,256]{1,0:T(8,128)(2,1)S(1)}, bf16[512,256]{1,0:T(8,128)(2,1)S(1)}) custom-call(bf16[1024,1024]{1,0:T(8,128)(2,1)} %bitcast.8, bf16[512,512]{1,0:T(8,128)(2,1)} %bitcast.10, bf16[512,512]{1,0:T(8,128)(2,1)} %bitcast.12), custom_call_target="tpu_custom_call" | custom-call | flops 268435456 | bytes 1835008 | tf_op jit(solution)/shard_map/first_right/pallas_call | solution.py:93
  2.7 3.0 %collective-permute-start = (bf16[512,256]{1,0:T(8,128)(2,1)S(1)}, bf16[512,256]{1,0:T(8,128)(2,1)S(1)}, u32[]{:S(2)}, u32[]{:S(2)}) collective-permute-start(bf16[512,256]{1,0:T(8,128)(2,1)S(1)} %get-tuple-element.32), channel_id=1, source_target_pairs={{0,4},{4,8},{8,12},{12,16},{16,20},{20,24},{24,28},{28,0},{1,5},{5... | collective-permute-start | bytes 786440 | tf_op jit(solution)/shard_map/ppermute | solution.py:21
  5.7 1.9 %first_upper.1 = (bf16[512,256]{1,0:T(8,128)(2,1)S(1)}, bf16[512,1024]{1,0:T(8,128)(2,1)S(1)}) custom-call(bf16[1024,1024]{1,0:T(8,128)(2,1)} %bitcast.9, bf16[512,256]{1,0:T(8,128)(2,1)S(1)} %get-tuple-element.29.left, bf16[512,256]{1,0:T(8,128)(2,1)S(1)} %get-tuple-element.30.lower), custom_call_target="tpu_custom_call" | custom-call | flops 268435456 | bytes 1835008 | tf_op jit(solution)/shard_map/first_upper/pallas_call | solution.py:124
  7.6 0.1 collective-permute-start.1
  7.7 1.5 %part_loading.1 = (bf16[512,256]{1,0:T(8,128)(2,1)S(1)}, bf16[512,256]{1,0:T(8,128)(2,1)S(1)}, bf16[512,256]{1,0:T(8,128)(2,1)S(1)}) custom-call(bf16[512,1024]{1,0:T(8,128)(2,1)S(1)} %get-tuple-element.28.z.z_top, bf16[512,512]{1,0:T(8,128)(2,1)} %bitcast.11, bf16[512,512]{1,0:T(8,128)(2,1)} %bitcast.13), custom_call_target="tpu_custom_call" | custom-call | flops 268435456 | bytes 1835008 | tf_op jit(solution)/shard_map/part_loading/pallas_call | solution.py:173
  9.2 1.6 %collective-permute-start.6 = (bf16[512,256]{1,0:T(8,128)(2,1)S(1)}, bf16[512,256]{1,0:T(8,128)(2,1)S(1)}, u32[]{:S(2)}, u32[]{:S(2)}) collective-permute-start(bf16[512,256]{1,0:T(8,128)(2,1)S(1)} %get-tuple-element.34), channel_id=1, source_target_pairs={{0,4},{4,8},{8,12},{12,16},{16,20},{20,24},{24,28},{28,0},{1,5},{5... | collective-permute-start | bytes 786440 | tf_op jit(solution)/shard_map/ppermute | solution.py:21
  10.8 0.4 part.13
  11.3 1.4 %collective-permute-start.7 = (bf16[512,256]{1,0:T(8,128)(2,1)S(1)}, bf16[512,256]{1,0:T(8,128)(2,1)S(1)}, u32[]{:S(2)}, u32[]{:S(2)}) collective-permute-start(bf16[512,256]{1,0:T(8,128)(2,1)S(1)} %part.13), channel_id=1, source_target_pairs={{0,1},{1,2},{2,3},{3,0},{4,5},{5,6},{6,7},{7,4},{8,9},{9,10},{10,1... | collective-permute-start | bytes 786440 | tf_op jit(solution)/shard_map/ppermute | solution.py:21
  12.6 2.4 %collective-permute-done.left = bf16[512,256]{1,0:T(8,128)(2,1)S(1)} collective-permute-done((bf16[512,256]{1,0:T(8,128)(2,1)S(1)}, bf16[512,256]{1,0:T(8,128)(2,1)S(1)}, u32[]{:S(2)}, u32[]{:S(2)}) %collective-permute-start) | collective-permute-done | bytes 262176 | tf_op jit(solution)/shard_map/ppermute | solution.py:21
  15.1 0.0 collective-permute-done.1.lower
  15.1 0.4 part.9
  15.5 0.1 collective-permute-start.2
  15.6 0.4 part.10
  16.0 0.1 collective-permute-start.3
  16.1 4.4 %collective-permute-done.6.left = bf16[512,256]{1,0:T(8,128)(2,1)S(1)} collective-permute-done((bf16[512,256]{1,0:T(8,128)(2,1)S(1)}, bf16[512,256]{1,0:T(8,128)(2,1)S(1)}, u32[]{:S(2)}, u32[]{:S(2)}) %collective-permute-start.6) | collective-permute-done | bytes 262176 | tf_op jit(solution)/shard_map/ppermute | solution.py:21
  20.5 0.0 collective-permute-done.7.lower
  20.5 0.4 part.14
  20.9 0.1 collective-permute-start.8
  21.0 0.4 part.15
  21.4 0.5 %collective-permute-start.9 = (bf16[512,256]{1,0:T(8,128)(2,1)S(1)}, bf16[512,256]{1,0:T(8,128)(2,1)S(1)}, u32[]{:S(2)}, u32[]{:S(2)}) collective-permute-start(bf16[512,256]{1,0:T(8,128)(2,1)S(1)} %part.15), channel_id=1, source_target_pairs={{0,1},{1,2},{2,3},{3,0},{4,5},{5,6},{6,7},{7,4},{8,9},{9,10},{10,1... | collective-permute-start | bytes 786440 | tf_op jit(solution)/shard_map/ppermute | solution.py:21
  22.0 4.8 %collective-permute-done.2.left = bf16[512,256]{1,0:T(8,128)(2,1)S(1)} collective-permute-done((bf16[512,256]{1,0:T(8,128)(2,1)S(1)}, bf16[512,256]{1,0:T(8,128)(2,1)S(1)}, u32[]{:S(2)}, u32[]{:S(2)}) %collective-permute-start.2) | collective-permute-done | bytes 262176 | tf_op jit(solution)/shard_map/ppermute | solution.py:21
  26.8 0.0 collective-permute-done.3.lower
  26.8 0.4 part.11
  27.2 0.1 collective-permute-start.4
  27.3 0.4 part.12
  27.7 0.0 copy-start.1
  27.7 0.0 copy-start.2
  27.7 0.0 copy-start
  27.8 0.1 collective-permute-start.5
  27.8 5.0 %collective-permute-done.8.left = bf16[512,256]{1,0:T(8,128)(2,1)S(1)} collective-permute-done((bf16[512,256]{1,0:T(8,128)(2,1)S(1)}, bf16[512,256]{1,0:T(8,128)(2,1)S(1)}, u32[]{:S(2)}, u32[]{:S(2)}) %collective-permute-start.8) | collective-permute-done | bytes 262176 | tf_op jit(solution)/shard_map/ppermute | solution.py:21
  32.8 0.0 collective-permute-done.9.lower
  32.8 0.4 part.16
  33.2 1.3 %collective-permute-start.10 = (bf16[512,256]{1,0:T(8,128)(2,1)S(1)}, bf16[512,256]{1,0:T(8,128)(2,1)S(1)}, u32[]{:S(2)}, u32[]{:S(2)}) collective-permute-start(bf16[512,256]{1,0:T(8,128)(2,1)S(1)} %part.16), channel_id=1, source_target_pairs={{0,4},{4,8},{8,12},{12,16},{16,20},{20,24},{24,28},{1,5},{5,9},{9,... | collective-permute-start | bytes 786440 | tf_op jit(solution)/shard_map/ppermute | solution.py:26
  34.6 0.4 part.17
  35.0 0.1 collective-permute-start.11
  35.1 0.0 copy-done.1
  35.1 0.0 copy-done.2
  35.1 0.7 %wavenum.1 = f32[256,128]{1,0:T(8,128)S(1)} custom-call(f32[16]{0:T(128)S(1)} %copy-done.2, s32[16,16]{1,0:T(8,128)S(1)} %copy-done.1), custom_call_target="tpu_custom_call" | custom-call | tf_op jit(solution)/shard_map/wavenum/pallas_call | solution.py:199
  35.7 2.3 %collective-permute-done.4.left = bf16[512,256]{1,0:T(8,128)(2,1)S(1)} collective-permute-done((bf16[512,256]{1,0:T(8,128)(2,1)S(1)}, bf16[512,256]{1,0:T(8,128)(2,1)S(1)}, u32[]{:S(2)}, u32[]{:S(2)}) %collective-permute-start.4) | collective-permute-done | bytes 262176 | tf_op jit(solution)/shard_map/ppermute | solution.py:21
  38.0 0.0 collective-permute-done.5.lower
  38.0 0.0 copy-done
  38.0 0.3 volume.1.done.first
  38.3 1.4 %last.1 = (bf16[512,512]{1,0:T(8,128)(2,1)}, bf16[512,512]{1,0:T(8,128)(2,1)}) custom-call(bf16[512,1024]{1,0:T(8,128)(2,1)S(1)} %get-tuple-element.28.z.z_top, bf16[512,1024]{1,0:T(8,128)(2,1)S(1)} %get-tuple-element.31.z.z_low, bf16[512,256]{1,0:T(8,128)(2,1)S(1)} %collective-permute-done.4.left, bf16[512,256]{1,0:T(8,128)(2,1)S(1)} %collective-permute-done.5.lower), custom_call_target="tpu_custom_call" | custom-call | flops 536870912 | bytes 3145728 | tf_op jit(solution)/shard_map/last/pallas_call | solution.py:286
  39.8 0.2 collective-permute-done.10.refs_0_
  40.0 0.9 %collective-permute-done.11.lower = bf16[512,256]{1,0:T(8,128)(2,1)S(1)} collective-permute-done((bf16[512,256]{1,0:T(8,128)(2,1)S(1)}, bf16[512,256]{1,0:T(8,128)(2,1)S(1)}, u32[]{:S(2)}, u32[]{:S(2)}) %collective-permute-start.11) | collective-permute-done | bytes 262176 | tf_op jit(solution)/shard_map/ppermute | solution.py:21
  40.8 0.3 edges.1
  41.2 1.7 %collective-permute-start.12 = (bf16[16,512]{1,0:T(8,128)(2,1)S(1)}, bf16[16,512]{1,0:T(8,128)(2,1)S(1)}, u32[]{:S(2)}, u32[]{:S(2)}) collective-permute-start(bf16[16,512]{1,0:T(8,128)(2,1)S(1)} %get-tuple-element.49), channel_id=1, source_target_pairs={{0,4},{1,5},{2,6},{3,7},{4,0},{5,1},{6,2},{7,3},{8,12},{9,13},{10,... | collective-permute-start | bytes 49160 | tf_op jit(solution)/shard_map/ppermute | solution.py:44
  42.9 0.0 collective-permute-start.13
  42.9 0.5 %collective-permute-start.14 = (bf16[16,512]{1,0:T(8,128)(2,1)S(1)}, bf16[16,512]{1,0:T(8,128)(2,1)S(1)}, u32[]{:S(2)}, u32[]{:S(2)}) collective-permute-start(bf16[16,512]{1,0:T(8,128)(2,1)S(1)} %get-tuple-element.51), channel_id=1, source_target_pairs={{0,1},{1,0},{2,3},{3,2},{4,5},{5,4},{6,7},{7,6},{8,9},{9,8},{10,11... | collective-permute-start | bytes 49160 | tf_op jit(solution)/shard_map/ppermute | solution.py:44
  43.4 0.9 %collective-permute-start.15 = (bf16[16,512]{1,0:T(8,128)(2,1)S(1)}, bf16[16,512]{1,0:T(8,128)(2,1)S(1)}, u32[]{:S(2)}, u32[]{:S(2)}) collective-permute-start(bf16[16,512]{1,0:T(8,128)(2,1)S(1)} %get-tuple-element.52), channel_id=1, source_target_pairs={{0,3},{1,2},{2,1},{3,0},{4,7},{5,6},{6,5},{7,4},{8,11},{9,10},{10,... | collective-permute-start | bytes 49160 | tf_op jit(solution)/shard_map/ppermute | solution.py:44
  44.3 1.5 %plain.1 = (bf16[512,512]{1,0:T(8,128)(2,1)}, bf16[512,512]{1,0:T(8,128)(2,1)}, f32[16,16,512]{2,1,0:T(8,128)S(1)}) custom-call(bf16[512,1024]{1,0:T(8,128)(2,1)S(1)} %get-tuple-element.28.z.z_top, bf16[512,1024]{1,0:T(8,128)(2,1)S(1)} %get-tuple-element.31.z.z_low, ...), custom_call_target="tpu_custom_call", output_to_operand_aliasing={{0}: (7, {}), {1}: (8, {})} | custom-call | flops 536870912 | bytes 3145728 | tf_op jit(solution)/shard_map/plain/pallas_call | solution.py:343
  45.8 0.0 collective-permute-done.12.x_pair
  45.8 0.0 collective-permute-done.13.x_cross
  45.8 0.0 collective-permute-done.14.y_pair
  45.8 0.7 %collective-permute-done.15.y_cross = bf16[16,512]{1,0:T(8,128)(2,1)S(1)} collective-permute-done((bf16[16,512]{1,0:T(8,128)(2,1)S(1)}, bf16[16,512]{1,0:T(8,128)(2,1)S(1)}, u32[]{:S(2)}, u32[]{:S(2)}) %collective-permute-start.15) | collective-permute-done | bytes 16416 | tf_op jit(solution)/shard_map/ppermute | solution.py:44
  46.5 0.8 %finish.1 = f32[16,16,512]{2,1,0:T(8,128)} custom-call(f32[16,16,512]{2,1,0:T(8,128)S(1)} %get-tuple-element.48.inner, bf16[16,512]{1,0:T(8,128)(2,1)S(1)} %collective-permute-done.12.x_pair, bf16[16,512]{1,0:T(8,128)(2,1)S(1)} %collective-permute-done.13.x_cross, bf16[16,512]{1,0:T(8,128)(2,1)S(1)} %collective-permute-done.14.y_pair, ...), custom_call_target="tpu_custom_call" | custom-call | flops 524288 | bytes 1048576 | tf_op jit(solution)/shard_map/finish/pallas_call | solution.py:398
Async XLA Ops:
  2.7 12.4 %collective-permute-start = (bf16[512,256]{1,0:T(8,128)(2,1)S(1)}, bf16[512,256]{1,0:T(8,128)(2,1)S(1)}, u32[]{:S(2)}, u32[]{:S(2)}) collective-permute-start(bf16[512,256]{1,0:T(8,128)(2,1)S(1)} %get-tuple-element.32), channel_id=1, source_target_pairs={{0,4},{4,8},{8,12},{12,16},{16,20},{20,24},{24,28},{28,0},{1,5},{5... | collective-permute-start | bytes 786440 | tf_op jit(solution)/shard_map/ppermute | solution.py:21
  7.6 7.4 %collective-permute-start.1 = (bf16[512,256]{1,0:T(8,128)(2,1)S(1)}, bf16[512,256]{1,0:T(8,128)(2,1)S(1)}, u32[]{:S(2)}, u32[]{:S(2)}) collective-permute-start(bf16[512,256]{1,0:T(8,128)(2,1)S(1)} %get-tuple-element.33), channel_id=1, source_target_pairs={{0,1},{1,2},{2,3},{3,0},{4,5},{5,6},{6,7},{7,4},{8,9},{9,10},{10,1... | collective-permute-start | bytes 786440 | tf_op jit(solution)/shard_map/ppermute | solution.py:21
  9.2 11.3 %collective-permute-start.6 = (bf16[512,256]{1,0:T(8,128)(2,1)S(1)}, bf16[512,256]{1,0:T(8,128)(2,1)S(1)}, u32[]{:S(2)}, u32[]{:S(2)}) collective-permute-start(bf16[512,256]{1,0:T(8,128)(2,1)S(1)} %get-tuple-element.34), channel_id=1, source_target_pairs={{0,4},{4,8},{8,12},{12,16},{16,20},{20,24},{24,28},{28,0},{1,5},{5... | collective-permute-start | bytes 786440 | tf_op jit(solution)/shard_map/ppermute | solution.py:21
  11.3 9.2 %collective-permute-start.7 = (bf16[512,256]{1,0:T(8,128)(2,1)S(1)}, bf16[512,256]{1,0:T(8,128)(2,1)S(1)}, u32[]{:S(2)}, u32[]{:S(2)}) collective-permute-start(bf16[512,256]{1,0:T(8,128)(2,1)S(1)} %part.13), channel_id=1, source_target_pairs={{0,1},{1,2},{2,3},{3,0},{4,5},{5,6},{6,7},{7,4},{8,9},{9,10},{10,1... | collective-permute-start | bytes 786440 | tf_op jit(solution)/shard_map/ppermute | solution.py:21
  15.5 11.2 %collective-permute-start.2 = (bf16[512,256]{1,0:T(8,128)(2,1)S(1)}, bf16[512,256]{1,0:T(8,128)(2,1)S(1)}, u32[]{:S(2)}, u32[]{:S(2)}) collective-permute-start(bf16[512,256]{1,0:T(8,128)(2,1)S(1)} %part.9), channel_id=1, source_target_pairs={{0,4},{4,8},{8,12},{12,16},{16,20},{20,24},{24,28},{28,0},{1,5},{5... | collective-permute-start | bytes 786440 | tf_op jit(solution)/shard_map/ppermute | solution.py:21
  16.0 10.7 %collective-permute-start.3 = (bf16[512,256]{1,0:T(8,128)(2,1)S(1)}, bf16[512,256]{1,0:T(8,128)(2,1)S(1)}, u32[]{:S(2)}, u32[]{:S(2)}) collective-permute-start(bf16[512,256]{1,0:T(8,128)(2,1)S(1)} %part.10), channel_id=1, source_target_pairs={{0,1},{1,2},{2,3},{3,0},{4,5},{5,6},{6,7},{7,4},{8,9},{9,10},{10,1... | collective-permute-start | bytes 786440 | tf_op jit(solution)/shard_map/ppermute | solution.py:21
  20.9 11.9 %collective-permute-start.8 = (bf16[512,256]{1,0:T(8,128)(2,1)S(1)}, bf16[512,256]{1,0:T(8,128)(2,1)S(1)}, u32[]{:S(2)}, u32[]{:S(2)}) collective-permute-start(bf16[512,256]{1,0:T(8,128)(2,1)S(1)} %part.14), channel_id=1, source_target_pairs={{0,4},{4,8},{8,12},{12,16},{16,20},{20,24},{24,28},{28,0},{1,5},{5... | collective-permute-start | bytes 786440 | tf_op jit(solution)/shard_map/ppermute | solution.py:21
  21.4 11.3 %collective-permute-start.9 = (bf16[512,256]{1,0:T(8,128)(2,1)S(1)}, bf16[512,256]{1,0:T(8,128)(2,1)S(1)}, u32[]{:S(2)}, u32[]{:S(2)}) collective-permute-start(bf16[512,256]{1,0:T(8,128)(2,1)S(1)} %part.15), channel_id=1, source_target_pairs={{0,1},{1,2},{2,3},{3,0},{4,5},{5,6},{6,7},{7,4},{8,9},{9,10},{10,1... | collective-permute-start | bytes 786440 | tf_op jit(solution)/shard_map/ppermute | solution.py:21
  27.2 10.8 %collective-permute-start.4 = (bf16[512,256]{1,0:T(8,128)(2,1)S(1)}, bf16[512,256]{1,0:T(8,128)(2,1)S(1)}, u32[]{:S(2)}, u32[]{:S(2)}) collective-permute-start(bf16[512,256]{1,0:T(8,128)(2,1)S(1)} %part.11), channel_id=1, source_target_pairs={{0,4},{4,8},{8,12},{12,16},{16,20},{20,24},{24,28},{28,0},{1,5},{5... | collective-permute-start | bytes 786440 | tf_op jit(solution)/shard_map/ppermute | solution.py:21
  27.7 7.3 %copy-start.1 = (s32[16,16]{1,0:T(8,128)S(1)}, s32[16,16]{1,0:T(8,128)}, u32[]{:S(2)}) copy-start(s32[16,16]{1,0:T(8,128)} %kinds.1) | copy-start | bytes 3076
  27.7 7.3 %copy-start.2 = (f32[16]{0:T(128)S(1)}, f32[16]{0:T(128)}, u32[]{:S(2)}) copy-start(f32[16]{0:T(128)} %table.1) | copy-start | bytes 196
  27.7 10.3 %copy-start = (bf16[1,1,256,1024]{3,2,1,0:T(8,128)(2,1)S(1)}, bf16[1,1,256,1024]{3,2,1,0:T(8,128)(2,1)}, u32[]{:S(2)}) copy-start(bf16[1,1,256,1024]{3,2,1,0:T(8,128)(2,1)} %param.7) | copy-start | bytes 1572868
  27.8 10.2 %collective-permute-start.5 = (bf16[512,256]{1,0:T(8,128)(2,1)S(1)}, bf16[512,256]{1,0:T(8,128)(2,1)S(1)}, u32[]{:S(2)}, u32[]{:S(2)}) collective-permute-start(bf16[512,256]{1,0:T(8,128)(2,1)S(1)} %part.12), channel_id=1, source_target_pairs={{0,1},{1,2},{2,3},{3,0},{4,5},{5,6},{6,7},{7,4},{8,9},{9,10},{10,1... | collective-permute-start | bytes 786440 | tf_op jit(solution)/shard_map/ppermute | solution.py:21
  33.2 6.7 %collective-permute-start.10 = (bf16[512,256]{1,0:T(8,128)(2,1)S(1)}, bf16[512,256]{1,0:T(8,128)(2,1)S(1)}, u32[]{:S(2)}, u32[]{:S(2)}) collective-permute-start(bf16[512,256]{1,0:T(8,128)(2,1)S(1)} %part.16), channel_id=1, source_target_pairs={{0,4},{4,8},{8,12},{12,16},{16,20},{20,24},{24,28},{1,5},{5,9},{9,... | collective-permute-start | bytes 786440 | tf_op jit(solution)/shard_map/ppermute | solution.py:26
  35.0 5.8 %collective-permute-start.11 = (bf16[512,256]{1,0:T(8,128)(2,1)S(1)}, bf16[512,256]{1,0:T(8,128)(2,1)S(1)}, u32[]{:S(2)}, u32[]{:S(2)}) collective-permute-start(bf16[512,256]{1,0:T(8,128)(2,1)S(1)} %part.17), channel_id=1, source_target_pairs={{0,1},{1,2},{2,3},{3,0},{4,5},{5,6},{6,7},{7,4},{8,9},{9,10},{10,1... | collective-permute-start | bytes 786440 | tf_op jit(solution)/shard_map/ppermute | solution.py:21
  41.2 4.6 %collective-permute-start.12 = (bf16[16,512]{1,0:T(8,128)(2,1)S(1)}, bf16[16,512]{1,0:T(8,128)(2,1)S(1)}, u32[]{:S(2)}, u32[]{:S(2)}) collective-permute-start(bf16[16,512]{1,0:T(8,128)(2,1)S(1)} %get-tuple-element.49), channel_id=1, source_target_pairs={{0,4},{1,5},{2,6},{3,7},{4,0},{5,1},{6,2},{7,3},{8,12},{9,13},{10,... | collective-permute-start | bytes 49160 | tf_op jit(solution)/shard_map/ppermute | solution.py:44
  42.9 2.9 %collective-permute-start.13 = (bf16[16,512]{1,0:T(8,128)(2,1)S(1)}, bf16[16,512]{1,0:T(8,128)(2,1)S(1)}, u32[]{:S(2)}, u32[]{:S(2)}) collective-permute-start(bf16[16,512]{1,0:T(8,128)(2,1)S(1)} %get-tuple-element.50), channel_id=1, source_target_pairs={{0,1},{1,0},{2,3},{3,2},{4,8},{5,9},{6,10},{7,11},{8,4},{9,5},{10,... | collective-permute-start | bytes 49160 | tf_op jit(solution)/shard_map/ppermute | solution.py:44
  42.9 3.0 %collective-permute-start.14 = (bf16[16,512]{1,0:T(8,128)(2,1)S(1)}, bf16[16,512]{1,0:T(8,128)(2,1)S(1)}, u32[]{:S(2)}, u32[]{:S(2)}) collective-permute-start(bf16[16,512]{1,0:T(8,128)(2,1)S(1)} %get-tuple-element.51), channel_id=1, source_target_pairs={{0,1},{1,0},{2,3},{3,2},{4,5},{5,4},{6,7},{7,6},{8,9},{9,8},{10,11... | collective-permute-start | bytes 49160 | tf_op jit(solution)/shard_map/ppermute | solution.py:44
  43.4 3.2 %collective-permute-start.15 = (bf16[16,512]{1,0:T(8,128)(2,1)S(1)}, bf16[16,512]{1,0:T(8,128)(2,1)S(1)}, u32[]{:S(2)}, u32[]{:S(2)}) collective-permute-start(bf16[16,512]{1,0:T(8,128)(2,1)S(1)} %get-tuple-element.52), channel_id=1, source_target_pairs={{0,3},{1,2},{2,1},{3,0},{4,7},{5,6},{6,5},{7,4},{8,11},{9,10},{10,... | collective-permute-start | bytes 49160 | tf_op jit(solution)/shard_map/ppermute | solution.py:44
